TPU v7x, 32 devices: a whole 2x2x4 slice. The times are simulated.
32 devices in a mesh: rows: 4 (over y, x), cols: 8 (over z, core).
Axes of the slice: x: 2, y: 2, z: 4, core: 2. Of those that a mesh axis runs over, the one named last changes fastest.
Arguments:
- tokens: bfloat16 [128, 256, 256], P('rows', 'cols'), may hold values from -45 to 45
- key_bias: bfloat16 [128, 256], P('rows', 'cols'), may hold values from -3 to 250
- cotangent: bfloat16 [128, 256, 256], P('rows', 'cols'), may hold values from -6 to 6
- gain_row: float32 [256], replicated, may hold values from 0.1 to 1.9
- w_qkv_row: bfloat16 [256, 768], replicated, may hold values from -0.375 to 0.375
- w_out_row: bfloat16 [256, 256], replicated, may hold values from -0.375 to 0.375
- gain_col: float32 [256], replicated, may hold values from 0.1 to 1.9
- w_qkv_col: bfloat16 [256, 768], replicated, may hold values from -0.375 to 0.375
- w_out_col: bfloat16 [256, 256], replicated, may hold values from -0.375 to 0.375
- gain_mlp: float32 [256], replicated, may hold values from 0.1 to 1.9
- w_up: bfloat16 [256, 1024], replicated, may hold values from -0.375 to 0.375
- w_down: bfloat16 [1024, 256], replicated, may hold values from -0.1875 to 0.1875
Outputs:
- d_tokens: bfloat16 [128, 256, 256], P('rows', 'cols')
- d_gain_row: float32 [256], replicated
- d_w_qkv_row: float32 [256, 768], replicated
- d_w_out_row: float32 [256, 256], replicated
- d_gain_col: float32 [256], replicated
- d_w_qkv_col: float32 [256, 768], replicated
- d_w_out_col: float32 [256, 256], replicated
- d_gain_mlp: float32 [256], replicated
- d_w_up: float32 [256, 1024], replicated
- d_w_down: float32 [1024, 256], replicated
All inputs are finite; a program needn't handle non-finite values.
Results may differ from a plain program's by a relative error of at most 0.015.
Values may be sent and summed in bfloat16 or wider, within the bound.
No kernel may reach another device: no remote copies, remote signals or barrier semaphores. Data moves between devices by JAX's collectives and lax.ppermute only.
A program may use at most 128 MiB of HBM per device.

v0:
```python
import jax
import jax.numpy as jnp
from jax import lax
from jax.sharding import PartitionSpec as P

HEADS = 4


def product(spec_text, left_op, right_op):
    return jnp.einsum(spec_text, left_op, right_op, preferred_element_type=jnp.float32)


def layer_norm(entries, gain_vec):
    floats = entries.astype(jnp.float32)
    centred = floats - jnp.mean(floats, axis=-1, keepdims=True)
    inverse = lax.rsqrt(jnp.mean(centred * centred, axis=-1, keepdims=True) + 1e-05)
    normed = centred * inverse
    return ((normed * gain_vec).astype(jnp.bfloat16), normed, inverse)


def norm_back(grad_out, normed, inverse, gain_vec):
    scaled = grad_out * gain_vec
    result = inverse * (
        scaled
        - jnp.mean(scaled, axis=-1, keepdims=True)
        - normed * jnp.mean(scaled * normed, axis=-1, keepdims=True)
    )
    gain_grad = jnp.sum((grad_out * normed).reshape(-1, gain_vec.shape[0]), axis=0)
    return (result, gain_grad)


def over_cells(left_op, right_op):
    left_flat = left_op.reshape(-1, left_op.shape[-1])
    right_flat = right_op.reshape(-1, right_op.shape[-1])
    return lax.dot_general(
        left_flat, right_flat, (((0,), (0,)), ((), ())), preferred_element_type=jnp.float32
    )


def times_transpose(entries, weight):
    return lax.dot_general(
        entries, weight, (((entries.ndim - 1,), (1,)), ((), ())), preferred_element_type=jnp.float32
    )


def letters(length_axis):
    if length_axis == 1:
        return ("sqhd,skhd->shqk", "shqk,skhd->sqhd", "shqk,sqhd->skhd")
    return ("qshd,kshd->shqk", "shqk,kshd->qshd", "shqk,qshd->kshd")


def split_heads(packed, head_count):
    features = packed.shape[-1] // 3
    head_shape = packed.shape[:-1] + (head_count, features // head_count)
    return tuple(
        (
            packed[..., member * features : (member + 1) * features].reshape(head_shape)
            for member in range(3)
        )
    )


def key_terms(bias_rows, length_axis):
    floats = bias_rows.astype(jnp.float32)
    if length_axis == 0:
        floats = floats.T
    return floats[:, None, None, :]


def attention_weights(query_block, key_rows, bias_terms, factor, length_axis):
    scores = product(letters(length_axis)[0], query_block, key_rows) * factor + bias_terms
    shifted = jnp.exp(scores - jnp.max(scores, axis=-1, keepdims=True))
    return shifted / jnp.sum(shifted, axis=-1, keepdims=True)


def join_blocks(stacked, length_axis, features):
    if length_axis == 0:
        return stacked.reshape((-1, stacked.shape[2], features))
    reordered = jnp.moveaxis(stacked, 0, 1)
    return reordered.reshape((reordered.shape[0], -1, features))


def attend(packed, bias_rows, head_count, length_axis):
    query_rows, key_rows, value_rows = split_heads(packed, head_count)
    length = packed.shape[length_axis]
    block_len = min(length, 512)
    factor = query_rows.shape[-1] ** (-0.5)
    bias_terms = key_terms(bias_rows, length_axis)
    mixing = letters(length_axis)[1]

    def one_block(offset):
        query_block = lax.dynamic_slice_in_dim(query_rows, offset, block_len, length_axis)
        weights = attention_weights(query_block, key_rows, bias_terms, factor, length_axis)
        return product(mixing, weights.astype(jnp.bfloat16), value_rows).astype(jnp.bfloat16)

    offsets = jnp.arange(length // block_len, dtype=jnp.int32) * block_len
    return join_blocks(lax.map(one_block, offsets), length_axis, packed.shape[-1] // 3)


def attend_back(grad_out, packed, bias_rows, head_count, length_axis):
    query_rows, key_rows, value_rows = split_heads(packed, head_count)
    features = packed.shape[-1] // 3
    grad_heads = grad_out.reshape(query_rows.shape)
    length = packed.shape[length_axis]
    block_len = min(length, 512)
    factor = query_rows.shape[-1] ** (-0.5)
    bias_terms = key_terms(bias_rows, length_axis)
    score_spec, mixing, gather_spec = letters(length_axis)

    def one_block(running, offset):
        key_grad, value_grad = running
        query_block = lax.dynamic_slice_in_dim(query_rows, offset, block_len, length_axis)
        grad_block = lax.dynamic_slice_in_dim(grad_heads, offset, block_len, length_axis)
        weights = attention_weights(query_block, key_rows, bias_terms, factor, length_axis)
        weights_low = weights.astype(jnp.bfloat16)
        weight_grad = product(score_spec, grad_block, value_rows)
        centre = jnp.sum(weights * weight_grad, axis=-1, keepdims=True)
        score_grad = (weights * (weight_grad - centre) * factor).astype(jnp.bfloat16)
        query_grad = product(mixing, score_grad, key_rows)
        key_grad = key_grad + product(gather_spec, score_grad, query_block)
        value_grad = value_grad + product(gather_spec, weights_low, grad_block)
        return ((key_grad, value_grad), query_grad)

    empty_grad = jnp.zeros(key_rows.shape, jnp.float32)
    offsets = jnp.arange(length // block_len, dtype=jnp.int32) * block_len
    (key_grad, value_grad), query_parts = lax.scan(one_block, (empty_grad, empty_grad), offsets)
    query_grad = join_blocks(query_parts, length_axis, features)
    flat_shape = packed.shape[:-1] + (features,)
    joined = jnp.concatenate(
        [query_grad, key_grad.reshape(flat_shape), value_grad.reshape(flat_shape)], axis=-1
    )
    return joined.astype(jnp.bfloat16)


def attention_forward(inputs, bias_rows, gain_vec, w_qkv, w_out, head_count, length_axis):
    normal_in, normed, inverse = layer_norm(inputs, gain_vec)
    packed = jnp.dot(normal_in, w_qkv, preferred_element_type=jnp.float32).astype(jnp.bfloat16)
    mixed_out = attend(packed, bias_rows, head_count, length_axis)
    output = (
        inputs.astype(jnp.float32) + jnp.dot(mixed_out, w_out, preferred_element_type=jnp.float32)
    ).astype(jnp.bfloat16)
    return (output, (normal_in, normed, inverse, packed, mixed_out))


def attention_backward(
    grad_out, saved_parts, bias_rows, gain_vec, w_qkv, w_out, head_count, length_axis
):
    normal_in, normed, inverse, packed, mixed_out = saved_parts
    out_grad = over_cells(mixed_out, grad_out)
    mixed_grad = times_transpose(grad_out, w_out).astype(jnp.bfloat16)
    packed_grad = attend_back(mixed_grad, packed, bias_rows, head_count, length_axis)
    qkv_grad = over_cells(normal_in, packed_grad)
    input_grad, gain_grad = norm_back(
        times_transpose(packed_grad, w_qkv), normed, inverse, gain_vec
    )
    return (
        (grad_out.astype(jnp.float32) + input_grad).astype(jnp.bfloat16),
        (gain_grad, qkv_grad, out_grad),
    )


def feed_backward(inputs, grad_out, gain_vec, w_up, w_down):
    normal_in, normed, inverse = layer_norm(inputs, gain_vec)
    hidden = jnp.dot(normal_in, w_up, preferred_element_type=jnp.float32)
    active, gelu_back = jax.vjp(jax.nn.gelu, hidden)
    active_low = active.astype(jnp.bfloat16)
    down_grad = over_cells(active_low, grad_out)
    hidden_grad = gelu_back(times_transpose(grad_out, w_down))[0].astype(jnp.bfloat16)
    up_grad = over_cells(normal_in, hidden_grad)
    input_grad, gain_grad = norm_back(times_transpose(hidden_grad, w_up), normed, inverse, gain_vec)
    return (
        (grad_out.astype(jnp.float32) + input_grad).astype(jnp.bfloat16),
        (gain_grad, up_grad, down_grad),
    )


def shards(
    tokens,
    key_bias,
    cotangent,
    gain_row,
    w_qkv_row,
    w_out_row,
    gain_col,
    w_qkv_col,
    w_out_col,
    gain_mlp,
    w_up,
    w_down,
):
    row_cells, row_bias = (
        lax.all_to_all(tokens, "cols", split_axis=0, concat_axis=1, tiled=True),
        lax.all_to_all(key_bias, "cols", split_axis=0, concat_axis=1, tiled=True),
    )
    after_rows, row_saved = attention_forward(
        row_cells, row_bias, gain_row, w_qkv_row, w_out_row, HEADS, 1
    )
    column_cells = lax.all_to_all(
        lax.all_to_all(after_rows, "cols", split_axis=1, concat_axis=0, tiled=True),
        "rows",
        split_axis=1,
        concat_axis=0,
        tiled=True,
    )
    column_grads, column_bias = (
        lax.all_to_all(cotangent, "rows", split_axis=1, concat_axis=0, tiled=True),
        lax.all_to_all(key_bias, "rows", split_axis=1, concat_axis=0, tiled=True),
    )
    after_cols, column_saved = attention_forward(
        column_cells, column_bias, gain_col, w_qkv_col, w_out_col, HEADS, 0
    )
    mid_grad, feed_grads = feed_backward(after_cols, column_grads, gain_mlp, w_up, w_down)
    cell_grad, attn_grads = attention_backward(
        mid_grad, column_saved, column_bias, gain_col, w_qkv_col, w_out_col, HEADS, 0
    )
    factor = float(
        tokens.shape[0] * tokens.shape[1] * lax.axis_size("rows") * lax.axis_size("cols")
    ) ** (-0.5)
    other_sums = tuple((grad_term * factor for grad_term in attn_grads + feed_grads))
    grad_rows = lax.all_to_all(
        lax.all_to_all(cell_grad, "rows", split_axis=0, concat_axis=1, tiled=True),
        "cols",
        split_axis=0,
        concat_axis=1,
        tiled=True,
    )
    token_grad_rows, row_grads = attention_backward(
        grad_rows, row_saved, row_bias, gain_row, w_qkv_row, w_out_row, HEADS, 1
    )
    d_tokens = lax.all_to_all(token_grad_rows, "cols", split_axis=1, concat_axis=0, tiled=True)
    row_sums = tuple((grad_term * factor for grad_term in row_grads))
    summed = lax.psum(
        (
            row_sums[0],
            row_sums[1],
            row_sums[2],
            other_sums[0],
            other_sums[1],
            other_sums[2],
            other_sums[3],
            other_sums[4],
            other_sums[5],
        ),
        ("rows", "cols"),
    )
    row_sums = summed[:3]
    other_sums = summed[3:]
    return (
        d_tokens,
        row_sums[0],
        row_sums[1],
        row_sums[2],
        other_sums[0],
        other_sums[1],
        other_sums[2],
        other_sums[3],
        other_sums[4],
        other_sums[5],
    )


def solution(mesh):
    in_specs = (
        P("rows", "cols", None),
        P("rows", "cols"),
        P("rows", "cols", None),
        P(),
        P(),
        P(),
        P(),
        P(),
        P(),
        P(),
        P(),
        P(),
    )
    out_specs = (P("rows", "cols", None), P(), P(), P(), P(), P(), P(), P(), P(), P())
    return jax.shard_map(shards, mesh=mesh, in_specs=in_specs, out_specs=out_specs, check_vma=False)
```

profile of v0, /device:TPU:0, one launch (start us, length us, event | category | flops | bytes accessed | tf_op | source)
XLA Modules:
  0.0 385.8 jit_solution(3843586543527307721)
XLA Ops:
  7.2 12.1 %all_to_all.134 = bf16[8,4,32]{2,1,0:T(4,128)(2,1)S(1)} all-to-all(bf16[8,4,32]{2,1,0:T(4,128)(2,1)} %bitcast.263), channel_id=1, replica_groups=mesh['rows'=4,'cols'=8] {'cols'}, dimensions={0} | all-to-all | bytes 4096 | tf_op jit(solution)/shard_map/all_to_all | solution.py:193
  19.3 3.6 all-to-all-start.1
  24.4 13.7 %all-to-all-done.1 = bf16[32,32,256]{2,1,0:T(8,128)(2,1)S(1)} async-done(((bf16[32,32,256]{2,1,0:T(8,128)(2,1)}), bf16[32,32,256]{2,1,0:T(8,128)(2,1)S(1)}, u32[]{:S(2)}, u32[]{:S(2)}) %all-to-all-start.1) | async-done | bytes 524320 | tf_op jit(solution)/shard_map/all_to_all | solution.py:192
  38.2 3.7 all-to-all-start.5
  46.3 4.7 %fusion.124 = (f32[4,4,256]{2,1,0:T(4,128)S(1)}, f32[4,4,256,256]{2,3,1,0:T(8,128)}) fusion(f32[4,256]{1,0:T(4,128)S(1)} %reshape.252, bf16[4,256,4,64]{1,3,2,0:T(8,128)(2,1)S(1)} %bitcast.249, bf16[4,256,4,64]{1,3,2,0:T(8,128)(2,1)} %bitcast.247), kind=kOutput, calls=%fused_computation.165 | convolution fusion | flops 138412288 | bytes 5263360 | tf_op jit(solution)/shard_map/while/body/eval_jaxpr/sub | solution.py:72
  51.0 2.7 convolution_convert_fusion.7
  56.1 3.5 all-to-all-start.3
  60.7 14.2 %all-to-all-done.3 = bf16[4,256,256]{2,0,1:T(4,128)(2,1)S(1)} async-done(((bf16[4,256,256]{2,0,1:T(4,128)(2,1)}), bf16[4,256,256]{2,0,1:T(4,128)(2,1)S(1)}, u32[]{:S(2)}, u32[]{:S(2)}) %all-to-all-start.3) | async-done | bytes 524320 | tf_op jit(solution)/shard_map/all_to_all | solution.py:199
  74.8 4.2 %all-to-all-start = ((bf16[32,32,256]{2,0,1:T(8,128)(2,1)}), bf16[32,32,256]{2,0,1:T(8,128)(2,1)S(1)}, u32[]{:S(2)}, u32[]{:S(2)}) async-start(bf16[32,32,256]{2,0,1:T(8,128)(2,1)} %copy.364), calls=%async_computation | async-start | bytes 1048576 | tf_op jit(solution)/shard_map/all_to_all | solution.py:206
  80.2 6.6 %all-to-all-done = bf16[32,32,256]{2,0,1:T(8,128)(2,1)S(1)} async-done(((bf16[32,32,256]{2,0,1:T(8,128)(2,1)}), bf16[32,32,256]{2,0,1:T(8,128)(2,1)S(1)}, u32[]{:S(2)}, u32[]{:S(2)}) %all-to-all-start) | async-done | bytes 524320 | tf_op jit(solution)/shard_map/all_to_all | solution.py:206
  86.9 3.7 all-to-all-start.4
  91.5 5.8 %all-to-all-done.4 = bf16[32,32,256]{2,0,1:T(8,128)(2,1)S(1)} async-done(((bf16[32,32,256]{2,0,1:T(8,128)(2,1)}), bf16[32,32,256]{2,0,1:T(8,128)(2,1)S(1)}, u32[]{:S(2)}, u32[]{:S(2)}) %all-to-all-start.4) | async-done | bytes 524320 | tf_op jit(solution)/shard_map/all_to_all | solution.py:198
  100.8 1.6 convolution_convert_fusion
  103.5 2.0 copy.387
  107.9 3.7 fusion.125
  111.6 2.0 convolution_convert_fusion.6
  115.3 2.8 multiply_convert_fusion
  118.2 3.2 fusion.10
  125.3 2.0 copy.392
  127.3 3.5 convolution_convert_fusion.5
  130.8 1.8 fusion.126
  132.6 5.2 %fusion.42 = bf16[8,4,64,128]{3,2,1,0:T(8,128)(2,1)} fusion(bf16[128,8,4,64]{0,3,2,1:T(8,128)(2,1)} %bitcast.252, f32[8,4,128,128]{2,3,1,0:T(8,128)} %fusion.126, f32[8,4,128,128]{2,3,1,0:T(8,128)} %get-tuple-element.127, f32[8,4,128]{2,1,0:T(4,128)S(1)} %get-tuple-element.126), kind=kOutput, calls=%fused_computation.49 | convolution fusion | flops 71045248 | bytes 5259264 | tf_op jit(solution)/shard_map/while/body/eval_jaxpr/shqk,kshd->qshd/dot_general | solution.py:10
  137.9 5.0 %fusion.45 = bf16[8,4,64,128]{3,2,1,0:T(8,128)(2,1)} fusion(bf16[128,8,4,64]{0,3,2,1:T(8,128)(2,1)S(1)} %bitcast.254, f32[8,4,128,128]{2,3,1,0:T(8,128)} %fusion.126, f32[8,4,128,128]{2,3,1,0:T(8,128)} %get-tuple-element.127, f32[8,4,128]{2,1,0:T(4,128)S(1)} %get-tuple-element.126), kind=kOutput, calls=%fused_computation.50 | convolution fusion | flops 71045248 | bytes 5259264 | tf_op jit(solution)/shard_map/while/body/eval_jaxpr/shqk,qshd->kshd/dot_general | solution.py:10
  144.1 2.2 copy.397
  146.4 2.0 copy.396
  148.4 3.2 multiply_reduce_fusion.2
  153.6 4.1 %all-to-all-start.6 = ((bf16[128,8,256]{2,1,0:T(8,128)(2,1)}), bf16[128,8,256]{2,1,0:T(8,128)(2,1)}, u32[]{:S(2)}, u32[]{:S(2)}) async-start(bf16[128,8,256]{2,1,0:T(8,128)(2,1)} %copy.399), calls=%async_computation.6 | async-start | bytes 1048576 | tf_op jit(solution)/shard_map/all_to_all | solution.py:221
  160.1 1.8 copy.416
  164.3 1.9 copy.454
  166.3 3.5 all-to-all-start.7
  170.1 2.3 convolution_multiply_fusion
  172.3 3.0 fusion.56
  175.3 2.0 fusion.38
  177.3 2.4 fusion.39
  179.7 5.3 %all-to-all-done.7 = bf16[32,32,256]{2,1,0:T(8,128)(2,1)S(1)} async-done(((bf16[32,32,256]{2,1,0:T(8,128)(2,1)}), bf16[32,32,256]{2,1,0:T(8,128)(2,1)S(1)}, u32[]{:S(2)}, u32[]{:S(2)}) %all-to-all-start.7) | async-done | bytes 524320 | tf_op jit(solution)/shard_map/all_to_all | solution.py:220
  185.4 3.8 convolution_convert_fusion.4
  189.3 2.7 fusion.127
  192.0 8.0 %fusion.48 = bf16[4,4,64,256]{3,2,1,0:T(8,128)(2,1)} fusion(bf16[4,256,4,64]{1,3,2,0:T(8,128)(2,1)S(1)} %bitcast.248, f32[4,4,256,256]{2,3,1,0:T(8,128)} %fusion.127, f32[4,4,256,256]{2,3,1,0:T(8,128)} %get-tuple-element.125, f32[4,4,256]{2,1,0:T(4,128)S(1)} %get-tuple-element.124), kind=kOutput, calls=%fused_computation.51 | convolution fusion | flops 141824256 | bytes 9453568 | tf_op jit(solution)/shard_map/while/body/eval_jaxpr/shqk,skhd->sqhd/dot_general | solution.py:10
  200.0 8.0 %fusion.51 = bf16[4,4,64,256]{3,2,1,0:T(8,128)(2,1)} fusion(bf16[4,256,4,64]{1,3,2,0:T(8,128)(2,1)S(1)} %bitcast.250, f32[4,4,256,256]{2,3,1,0:T(8,128)} %fusion.127, f32[4,4,256,256]{2,3,1,0:T(8,128)} %get-tuple-element.125, f32[4,4,256]{2,1,0:T(4,128)S(1)} %get-tuple-element.124), kind=kOutput, calls=%fused_computation.52 | convolution fusion | flops 141824256 | bytes 9453568 | tf_op jit(solution)/shard_map/while/body/eval_jaxpr/shqk,sqhd->skhd/dot_general | solution.py:10
  209.3 2.1 copy.406
  211.4 2.0 copy.405
  214.5 2.7 fusion.57
  221.9 3.5 all-to-all-start.8
  225.4 41.2 %all-reduce = (f32[256]{0:T(256)}, f32[256]{0:T(256)}, f32[256]{0:T(256)}) all-reduce(f32[256]{0:T(256)S(1)} %broadcast_multiply_fusion.11, f32[256]{0:T(256)S(1)} %broadcast_multiply_fusion.10, f32[256]{0:T(256)S(1)} %broadcast_multiply_fusion.9), channel_id=1, replica_groups=mesh['rows'=4,'cols'=8] {'rows','cols'}, use_global_device_ids=true, to_apply=%region_19.20 | all-reduce | flops 768 | bytes 6144 | tf_op jit(solution)/shard_map/psum | solution.py:232
  267.6 102.7 %all-reduce.4.cloned.1.call-done = (f32[256,768]{1,0:T(8,128)}, f32[256,256]{1,0:T(8,128)}, f32[256,768]{1,0:T(8,128)}, f32[256,256]{1,0:T(8,128)}, f32[256,1024]{1,0:T(8,128)}, /*index=5*/f32[1024,256]{1,0:T(8,128)}) async-done(((f32[256,768]{1,0:T(8,128)}, f32[256,256]{1,0:T(8,128)}, f32[256,768]{1,0:T(8,128)}, f32[256,256]{1,0:T(8,128)}, f32[256,1024]{1,0:T(8,128)}, /*index=5*/f32[1024,256]{1,0:T(8,128)}), ...) | async-done | bytes 4194320 | tf_op jit(solution)/shard_map/psum | solution.py:232
  370.2 2.2 copy.461
  372.5 1.7 copy.462
  374.2 2.1 copy.463
  (178 shorter events, 43.2 us)
Async XLA Ops:
  7.2 108.1 %copy-start = (bf16[256,1024]{1,0:T(8,128)(2,1)S(1)}, bf16[256,1024]{1,0:T(8,128)(2,1)}, u32[]{:S(2)}) copy-start(bf16[256,1024]{1,0:T(8,128)(2,1)} %param.22) | copy-start | bytes 1572868
  19.3 23.7 %copy-start.41 = (f32[256]{0:T(256)S(1)}, f32[256]{0:T(256)}, u32[]{:S(2)}) copy-start(f32[256]{0:T(256)} %param.15) | copy-start | bytes 3076
  19.3 18.9 %all-to-all-start.1 = ((bf16[32,32,256]{2,1,0:T(8,128)(2,1)}), bf16[32,32,256]{2,1,0:T(8,128)(2,1)S(1)}, u32[]{:S(2)}, u32[]{:S(2)}) async-start(bf16[32,32,256]{2,1,0:T(8,128)(2,1)} %param.12), calls=%async_computation.1 | async-start | bytes 1048576 | tf_op jit(solution)/shard_map/all_to_all | solution.py:192
  38.2 17.9 %all-to-all-start.5 = ((bf16[4,2,128]{2,1,0:T(2,128)(2,1)}), bf16[4,2,128]{2,1,0:T(2,128)(2,1)S(1)}, u32[]{:S(2)}, u32[]{:S(2)}) async-start(bf16[4,2,128]{2,1,0:T(2,128)(2,1)} %reshape.268), calls=%async_computation.5 | async-start | bytes 4096 | tf_op jit(solution)/shard_map/all_to_all | solution.py:207
  41.9 2.2 copy-start.36
  46.0 4.9 %copy-start.29 = (bf16[4,256,256]{1,2,0:T(8,128)(2,1)}, bf16[4,256,256]{1,2,0:T(8,128)(2,1)S(1)}, u32[]{:S(2)}) copy-start(bf16[4,256,256]{1,2,0:T(8,128)(2,1)S(1)} %copy.369) | copy-start | bytes 1572868
  46.2 4.7 %copy-start.8 = (bf16[4,256,256]{1,2,0:T(8,128)(2,1)}, bf16[4,256,256]{1,2,0:T(8,128)(2,1)S(1)}, u32[]{:S(2)}) copy-start(bf16[4,256,256]{1,2,0:T(8,128)(2,1)S(1)} %copy.368) | copy-start | bytes 1572868
  50.9 3.6 copy-start.26
  53.7 5.9 %copy-start.27 = (bf16[32,32,256]{2,1,0:T(8,128)(2,1)S(1)}, bf16[32,32,256]{2,1,0:T(8,128)(2,1)}, u32[]{:S(2)}) copy-start(bf16[32,32,256]{2,1,0:T(8,128)(2,1)} %param.14) | copy-start | bytes 1572868
  56.1 18.8 %all-to-all-start.3 = ((bf16[4,256,256]{2,0,1:T(4,128)(2,1)}), bf16[4,256,256]{2,0,1:T(4,128)(2,1)S(1)}, u32[]{:S(2)}, u32[]{:S(2)}) async-start(bf16[4,256,256]{2,0,1:T(4,128)(2,1)} %copy.374), calls=%async_computation.3 | async-start | bytes 1048576 | tf_op jit(solution)/shard_map/all_to_all | solution.py:199
  74.8 12.0 %all-to-all-start = ((bf16[32,32,256]{2,0,1:T(8,128)(2,1)}), bf16[32,32,256]{2,0,1:T(8,128)(2,1)S(1)}, u32[]{:S(2)}, u32[]{:S(2)}) async-start(bf16[32,32,256]{2,0,1:T(8,128)(2,1)} %copy.364), calls=%async_computation | async-start | bytes 1048576 | tf_op jit(solution)/shard_map/all_to_all | solution.py:206
  86.9 11.8 %copy-start.2 = (bf16[32,32,256]{2,0,1:T(8,128)(2,1)}, bf16[32,32,256]{2,0,1:T(8,128)(2,1)S(1)}, u32[]{:S(2)}) copy-start(bf16[32,32,256]{2,0,1:T(8,128)(2,1)S(1)} %all-to-all-done) | copy-start | bytes 1572868
  86.9 10.4 %all-to-all-start.4 = ((bf16[32,32,256]{2,0,1:T(8,128)(2,1)}), bf16[32,32,256]{2,0,1:T(8,128)(2,1)S(1)}, u32[]{:S(2)}, u32[]{:S(2)}) async-start(bf16[32,32,256]{2,0,1:T(8,128)(2,1)} %copy.377), calls=%async_computation.4 | async-start | bytes 1048576 | tf_op jit(solution)/shard_map/all_to_all | solution.py:198
  90.7 8.9 %copy-start.40 = (f32[256]{0:T(256)S(1)}, f32[256]{0:T(256)}, u32[]{:S(2)}) copy-start(f32[256]{0:T(256)} %param.18) | copy-start | bytes 3076
  107.9 5.8 %copy-start.20 = (bf16[128,8,256]{0,2,1:T(8,128)(2,1)}, bf16[128,8,256]{0,2,1:T(8,128)(2,1)S(1)}, u32[]{:S(2)}) copy-start(bf16[128,8,256]{0,2,1:T(8,128)(2,1)S(1)} %copy.385) | copy-start | bytes 1572868
  111.6 2.9 copy-start.25
  111.6 3.8 copy-start.39
  115.3 2.8 copy-start.12
  115.3 2.8 copy-start.44
  121.4 2.0 copy-start.13
  127.3 3.5 copy-start.21
  127.3 3.5 copy-start.22
  132.6 5.2 %copy-start.32 = (bf16[128,8,256]{0,2,1:T(8,128)(2,1)S(1)}, bf16[128,8,256]{0,2,1:T(8,128)(2,1)}, u32[]{:S(2)}) copy-start(bf16[128,8,256]{0,2,1:T(8,128)(2,1)} %copy.386) | copy-start | bytes 1572868
  144.1 4.3 %copy-start.31 = (bf16[128,8,256]{2,0,1:T(8,128)(2,1)}, bf16[128,8,256]{2,0,1:T(8,128)(2,1)S(1)}, u32[]{:S(2)}) copy-start(bf16[128,8,256]{2,0,1:T(8,128)(2,1)S(1)} %copy.398) | copy-start | bytes 1572868
  148.4 3.2 copy-start.5
  151.6 6.1 %copy-start.3 = (bf16[32,32,256]{2,0,1:T(8,128)(2,1)S(1)}, bf16[32,32,256]{2,0,1:T(8,128)(2,1)}, u32[]{:S(2)}) copy-start(bf16[32,32,256]{2,0,1:T(8,128)(2,1)} %copy-done.2) | copy-start | bytes 1572868
  152.5 6.3 %copy-start.11 = (bf16[4,4,64,256]{3,2,1,0:T(8,128)(2,1)S(1)}, bf16[4,4,64,256]{3,2,1,0:T(8,128)(2,1)}, u32[]{:S(2)}) copy-start(bf16[4,4,64,256]{3,2,1,0:T(8,128)(2,1)} %copy-done.10) | copy-start | bytes 1572868
  153.6 10.8 %all-to-all-start.6 = ((bf16[128,8,256]{2,1,0:T(8,128)(2,1)}), bf16[128,8,256]{2,1,0:T(8,128)(2,1)}, u32[]{:S(2)}, u32[]{:S(2)}) async-start(bf16[128,8,256]{2,1,0:T(8,128)(2,1)} %copy.399), calls=%async_computation.6 | async-start | bytes 1048576 | tf_op jit(solution)/shard_map/all_to_all | solution.py:221
  159.2 10.9 %copy-start.6 = (bf16[128,8,256]{2,0,1:T(8,128)(2,1)S(1)}, bf16[128,8,256]{2,0,1:T(8,128)(2,1)}, u32[]{:S(2)}) copy-start(bf16[128,8,256]{2,0,1:T(8,128)(2,1)} %copy-done.4) | copy-start | bytes 1572868
  163.5 8.9 %copy-start.18 = (bf16[128,8,256]{2,0,1:T(8,128)(2,1)S(1)}, bf16[128,8,256]{2,0,1:T(8,128)(2,1)}, u32[]{:S(2)}) copy-start(bf16[128,8,256]{2,0,1:T(8,128)(2,1)} %copy-done.17) | copy-start | bytes 1572868
  166.3 18.8 %all-to-all-start.7 = ((bf16[32,32,256]{2,1,0:T(8,128)(2,1)}), bf16[32,32,256]{2,1,0:T(8,128)(2,1)S(1)}, u32[]{:S(2)}, u32[]{:S(2)}) async-start(bf16[32,32,256]{2,1,0:T(8,128)(2,1)} %bitcast.239), calls=%async_computation.7 | async-start | bytes 1048576 | tf_op jit(solution)/shard_map/all_to_all | solution.py:220
  169.8 200.5 %all-reduce.4.cloned.1.call-start = ((), (), s32[]{:S(2)}) async-start(), calls=%async_computation.9 | async-start | bytes 8388608 | tf_op jit(solution)/shard_map/psum | solution.py:232
  172.3 3.0 copy-start.14
  175.3 2.0 copy-start.33
  175.3 2.0 copy-start.45
  185.4 3.8 copy-start.9
  189.3 2.7 copy-start.28
  192.0 8.0 %copy-start.30 = (bf16[4,256,256]{1,2,0:T(8,128)(2,1)S(1)}, bf16[4,256,256]{1,2,0:T(8,128)(2,1)}, u32[]{:S(2)}) copy-start(bf16[4,256,256]{1,2,0:T(8,128)(2,1)} %copy-done.29) | copy-start | bytes 1572868
  208.0 5.5 %copy-start.19 = (bf16[32,8,4,256]{3,1,2,0:T(8,128)(2,1)S(1)}, bf16[32,8,4,256]{3,1,2,0:T(8,128)(2,1)}, u32[]{:S(2)}) copy-start(bf16[32,8,4,256]{3,1,2,0:T(8,128)(2,1)} %copy.437) | copy-start | bytes 1572868
  208.0 6.5 %copy-start.16 = (bf16[4,256,256]{2,1,0:T(8,128)(2,1)S(1)}, bf16[4,256,256]{2,1,0:T(8,128)(2,1)}, u32[]{:S(2)}) copy-start(bf16[4,256,256]{2,1,0:T(8,128)(2,1)} %copy-done.15) | copy-start | bytes 1572868
  217.2 1.3 copy-start.37
  219.8 5.6 %copy-start.42 = (f32[256]{0:T(256)S(1)}, f32[256]{0:T(256)}, u32[]{:S(2)}) copy-start(f32[256]{0:T(256)} %get-tuple-element.73) | copy-start | bytes 3076
  219.8 5.6 %copy-start.43 = (f32[256]{0:T(256)S(1)}, f32[256]{0:T(256)}, u32[]{:S(2)}) copy-start(f32[256]{0:T(256)} %get-tuple-element.84) | copy-start | bytes 3076
  221.9 44.8 %all-to-all-start.8 = ((bf16[4,256,256]{2,0,1:T(4,128)(2,1)}), bf16[4,256,256]{2,0,1:T(4,128)(2,1)S(1)}, u32[]{:S(2)}, u32[]{:S(2)}) async-start(bf16[4,256,256]{2,0,1:T(4,128)(2,1)} %copy.409), calls=%async_computation.8 | async-start | bytes 1048576 | tf_op jit(solution)/shard_map/all_to_all | solution.py:230
  370.2 6.0 %copy-start.38 = (f32[256,256]{1,0:T(8,128)S(1)}, f32[256,256]{1,0:T(8,128)}, u32[]{:S(2)}) copy-start(f32[256,256]{1,0:T(8,128)} %get-tuple-element.143) | copy-start | bytes 786436
  370.2 6.7 %copy-start.24 = (f32[256,1024]{1,0:T(8,128)S(1)}, f32[256,1024]{1,0:T(8,128)}, u32[]{:S(2)}) copy-start(f32[256,1024]{1,0:T(8,128)} %get-tuple-element.145) | copy-start | bytes 3145732
  370.2 7.7 %copy-start.23 = (f32[1024,256]{1,0:T(8,128)S(1)}, f32[1024,256]{1,0:T(8,128)}, u32[]{:S(2)}) copy-start(f32[1024,256]{1,0:T(8,128)} %get-tuple-element.146) | copy-start | bytes 3145732
  372.5 6.4 %copy-start.1 = (bf16[256,1024]{1,0:T(8,128)(2,1)S(1)}, bf16[256,1024]{1,0:T(8,128)(2,1)}, u32[]{:S(2)}) copy-start(bf16[256,1024]{1,0:T(8,128)(2,1)} %param.22) | copy-start | bytes 1572868
  (7 other events, 6.3 us)
Sparse Core Ops, SparseCore 0:
  217.3 152.8 all-reduce.3
where the time goes:
time: 387 us; the launch traced here: 386 us
  waiting for transfers between devices  149 us (39%)
  matrix products  80.4 us (21%)
  blocking collectives  53.3 us (14%)
  local copies, waits for them, and re-layouts  52.3 us (14%)
  starting transfers between devices  30.1 us (8%)
  between operations  14.7 us (4%)
  other arithmetic  5.81 us (2%)
    psum x1, waiting for transfers between devices, shards(): lax.psum((row_sums[0], row_sums[1], row_sums[2], other_sums[0], other_sum...  103 us
    dot_general x10, matrix products, product(): jnp.einsum(spec_text, left_op, right_op, preferred_element_type=jnp.float32)  42.8 us
    psum x1, blocking collectives, shards(): lax.psum((row_sums[0], row_sums[1], row_sums[2], other_sums[0], other_sum...  41.2 us
    unnamed x104, local copies, waits for them, and re-layouts  17.6 us
    all_to_all x1, waiting for transfers between devices, shards(): lax.all_to_all(after_rows, 'cols', split_axis=1, concat_axis=0, tiled=True)  14.2 us
    all_to_all x1, waiting for transfers between devices, shards(): lax.all_to_all(tokens, 'cols', split_axis=0, concat_axis=1, tiled=True)  13.7 us
    dot_general x6, matrix products, over_cells(): lax.dot_general(left_flat, right_flat, (((0,), (0,)), ((), ())), preferre...  13.3 us
    all_to_all x1, blocking collectives, shards(): lax.all_to_all(key_bias, 'cols', split_axis=0, concat_axis=1, tiled=True)  12.1 us
  transfers between devices with their start and end apart: 9, of which 7 were waited for; matrix products, arithmetic and copies ran while one was open for 10% of the time, Pallas kernels for 0%

commit v1 on v0

v1 whole, which is shorter than its diff:
```python
import functools
import jax
import jax.numpy as jnp
from jax import lax
from jax.experimental import pallas as pl
from jax.experimental.pallas import tpu as pltpu
from jax.sharding import PartitionSpec as P

HEADS = 4
LANES = 128
ALL = ("rows", "cols")
BF = jnp.bfloat16
F32 = jnp.float32
VMEM_LIMIT = 56 * 1024 * 1024


def dot(a, b):
    return lax.dot_general(a, b, (((1,), (0,)), ((), ())), preferred_element_type=F32)


def dot_nt(a, b):
    return lax.dot_general(a, b, (((1,), (1,)), ((), ())), preferred_element_type=F32)


def dot_tn(a, b):
    return lax.dot_general(a, b, (((0,), (0,)), ((), ())), preferred_element_type=F32)


def norm(x):
    centred = x - jnp.mean(x, axis=-1, keepdims=True)
    inverse = lax.rsqrt(jnp.mean(centred * centred, axis=-1, keepdims=True) + 1e-05)
    return centred * inverse, inverse


def norm_back(grad, normed, inverse, gain):
    scaled = grad * gain
    return inverse * (
        scaled
        - jnp.mean(scaled, axis=-1, keepdims=True)
        - normed * jnp.mean(scaled * normed, axis=-1, keepdims=True)
    )


def head_masks(features):
    lane = lax.broadcasted_iota(jnp.int32, (1, features), 1) // (features // HEADS)
    return [(lane == h).astype(F32).astype(BF) for h in range(HEADS)]


def softmax_heads(q, k, bias, masks, factor):
    weights = []
    for mask in masks:
        s = dot_nt(q * (mask * factor), k) + bias
        e = jnp.exp(s - jnp.max(s, axis=-1, keepdims=True))
        weights.append(e * (1.0 / jnp.sum(e, axis=-1, keepdims=True)))
    return weights


def mix_heads(weights_low, v, masks):
    return dot(
        jnp.concatenate(weights_low, axis=1),
        jnp.concatenate([v * mask for mask in masks], axis=0),
    )


def heads_back(weights, weights_low, do, q, k, v, masks, factor):
    dos = [do * mask for mask in masks]
    low = []
    for h in range(HEADS):
        dp = dot_nt(dos[h], v)
        p = weights[h]
        centre = jnp.sum(p * dp, axis=-1, keepdims=True)
        low.append((p * (dp - centre) * factor).astype(BF))
    dq = dot(
        jnp.concatenate(low, axis=1), jnp.concatenate([k * mask for mask in masks], axis=0)
    )
    dk = dot_tn(
        jnp.concatenate(low, axis=0), jnp.concatenate([q * mask for mask in masks], axis=0)
    )
    dv = dot_tn(jnp.concatenate(weights_low, axis=0), jnp.concatenate(dos, axis=0))
    return dq.astype(BF), dk.astype(BF), dv.astype(BF)


def load_cells(ref, pieces):
    return jnp.concatenate([ref[s].astype(F32) for s in range(pieces)], axis=0)


def row_bias(b_ref, row, pieces, length):
    total = b_ref[0].astype(F32)
    for s in range(1, pieces):
        total = total + b_ref[s].astype(F32)
    features = total.shape[1]
    at = lax.broadcasted_iota(jnp.int32, total.shape, 0)
    parts = length // features
    return jnp.concatenate(
        [
            jnp.sum(jnp.where(at == row * parts + t, total, 0.0), axis=0, keepdims=True)
            for t in range(parts)
        ],
        axis=1,
    )


def row_forward_kernel(
    dims, x_ref, b_ref, gain_ref, wqkv_ref, wout_ref, y_ref, h_ref, qkv_ref, o_ref, p_ref
):
    r_size, c_size, wl, cpd, length, d = dims
    factor = float(d // HEADS) ** (-0.5)
    masks = head_masks(d)
    x = load_cells(x_ref, c_size)
    n, _ = norm(x)
    h = (n * gain_ref[...]).astype(BF)
    h_ref[0] = h
    qkv = dot(h, wqkv_ref[...]).astype(BF)
    qkv_ref[0] = qkv
    q, k, v = qkv[:, :d], qkv[:, d : 2 * d], qkv[:, 2 * d :]
    bias = row_bias(b_ref, pl.program_id(0), c_size, length)
    weights = softmax_heads(q, k, bias, masks, factor)
    low = [w.astype(BF) for w in weights]
    for i in range(HEADS):
        p_ref[0, i] = low[i]
    o = mix_heads(low, v, masks).astype(BF)
    o_ref[0] = o
    y = (x + dot(o, wout_ref[...])).astype(BF)
    for c in range(c_size):
        for r in range(r_size):
            at = c * wl + r * cpd
            y_ref[r * c_size + c, 0] = y[at : at + cpd]


def row_backward_kernel(
    dims, x_ref, dy_ref, qkv_ref, p_ref, gain_ref, wqkv_ref, wout_ref,
    dt_ref, dyr_ref, dqkv_ref, dg_ref,
):
    r_size, c_size, wl, cpd, length, d = dims
    factor = float(d // HEADS) ** (-0.5)
    masks = head_masks(d)
    dy = jnp.concatenate(
        [dy_ref[r * c_size + c, 0].astype(F32) for c in range(c_size) for r in range(r_size)],
        axis=0,
    )
    dy_low = dy.astype(BF)
    dyr_ref[0] = dy_low
    do = dot_nt(dy_low, wout_ref[...]).astype(BF)
    qkv = qkv_ref[0]
    q, k, v = qkv[:, :d], qkv[:, d : 2 * d], qkv[:, 2 * d :]
    low = [p_ref[0, i] for i in range(HEADS)]
    weights = [w.astype(F32) for w in low]
    dq, dk, dv = heads_back(weights, low, do, q, k, v, masks, factor)
    dqkv = jnp.concatenate([dq, dk, dv], axis=1)
    dqkv_ref[0] = dqkv
    g = dot_nt(dqkv, wqkv_ref[...])
    n, inverse = norm(load_cells(x_ref, c_size))
    dt = (dy + norm_back(g, n, inverse, gain_ref[...])).astype(BF)
    for s in range(c_size):
        dt_ref[s] = dt[s * wl : (s + 1) * wl]
    dg = jnp.sum(g * n, axis=0, keepdims=True)

    @pl.when(pl.program_id(0) == 0)
    def _():
        dg_ref[...] = dg

    @pl.when(pl.program_id(0) != 0)
    def _():
        dg_ref[...] += dg


def column_kernel(
    dims, y_ref, ct_ref, gain_ref, wqkv_ref, wout_ref, gmlp_ref, wup_ref, wdown_ref,
    dy_ref, h2_ref, dqkv_ref, o2_ref, dy2_ref, h3_ref, du_ref, act_ref, ctc_ref, dg_ref, dgm_ref,
    wire_s, x_s, ct_s, bias_s, p_s,
):
    r_size, hl, cpd, length, d, chunk = dims
    step, steps = pl.program_id(0), pl.num_programs(0)
    factor = float(d // HEADS) ** (-0.5)
    masks = head_masks(d)
    tokens = chunk * length

    @pl.when(step == 0)
    def _():
        for lanes in range(d // LANES):
            cut = slice(lanes * LANES, (lanes + 1) * LANES)
            wire_s[lanes] = y_ref[:, cut].astype(F32)
            for j in range(cpd):
                x_s[j, :, cut] = wire_s[lanes, pl.ds(j, length, stride=cpd), :]
        block = hl * cpd
        for lanes in range(d // LANES):
            cut = slice(lanes * LANES, (lanes + 1) * LANES)
            for r in range(r_size):
                wire_s[lanes, r * block : (r + 1) * block, :] = ct_ref[r, :block, cut].astype(F32)
            for j in range(cpd):
                ct_s[j, :, cut] = wire_s[lanes, pl.ds(j, length, stride=cpd), :]
        total = ct_ref[0, block:].astype(F32)
        for r in range(1, r_size):
            total = total + ct_ref[r, block:].astype(F32)
        for j in range(cpd):
            bias_s[j] = total[j : j + 1, :length]
        dg_ref[...] = jnp.zeros_like(dg_ref)
        dgm_ref[...] = jnp.zeros_like(dgm_ref)

    at = pl.ds(step * chunk, chunk)
    x = x_s[at].reshape(tokens, d)
    ct = ct_s[at].reshape(tokens, d)
    n2, r2 = norm(x)
    h2 = (n2 * gain_ref[...]).astype(BF)
    h2_ref[...] = h2
    qkv = dot(h2, wqkv_ref[...]).astype(BF)
    outs = []
    for j in range(chunk):
        part = slice(j * length, (j + 1) * length)
        q, k, v = qkv[part, :d], qkv[part, d : 2 * d], qkv[part, 2 * d :]
        weights = softmax_heads(q, k, bias_s[step * chunk + j], masks, factor)
        for i in range(HEADS):
            p_s[j, i] = weights[i]
        outs.append(mix_heads([w.astype(BF) for w in weights], v, masks))
    o2 = jnp.concatenate(outs, axis=0).astype(BF)
    o2_ref[...] = o2
    y2 = (x + dot(o2, wout_ref[...])).astype(BF).astype(F32)
    n3, r3 = norm(y2)
    h3 = (n3 * gmlp_ref[...]).astype(BF)
    h3_ref[...] = h3
    ct_low = ct.astype(BF)
    ctc_ref[...] = ct_low
    u = dot(h3, wup_ref[...])
    root = 0.7978845608028654
    square = u * u
    t = jnp.tanh(root * (u + 0.044715 * (u * square)))
    act_ref[...] = (0.5 * u * (1.0 + t)).astype(BF)
    slope = 0.5 * (1.0 + t) + 0.5 * u * (1.0 - t * t) * (root * (1.0 + 3.0 * 0.044715 * square))
    du = (dot_nt(ct_low, wdown_ref[...]) * slope).astype(BF)
    du_ref[...] = du
    g3 = dot_nt(du, wup_ref[...])
    dgm_ref[...] += jnp.sum(g3 * n3, axis=0, keepdims=True)
    dy2 = (ct + norm_back(g3, n3, r3, gmlp_ref[...])).astype(BF)
    dy2_ref[...] = dy2
    do = dot_nt(dy2, wout_ref[...]).astype(BF)
    grads = []
    for j in range(chunk):
        part = slice(j * length, (j + 1) * length)
        q, k, v = qkv[part, :d], qkv[part, d : 2 * d], qkv[part, 2 * d :]
        weights = [p_s[j, i] for i in range(HEADS)]
        low = [w.astype(BF) for w in weights]
        grads.append(
            jnp.concatenate(heads_back(weights, low, do[part], q, k, v, masks, factor), axis=1)
        )
    dqkv = jnp.concatenate(grads, axis=0)
    dqkv_ref[...] = dqkv
    g2 = dot_nt(dqkv, wqkv_ref[...])
    dg_ref[...] += jnp.sum(g2 * n2, axis=0, keepdims=True)
    dy1 = dy2.astype(F32) + norm_back(g2, n2, r2, gain_ref[...])
    x_s[at] = dy1.reshape(chunk, length, d)

    @pl.when(step == steps - 1)
    def _():
        for lanes in range(d // LANES):
            cut = slice(lanes * LANES, (lanes + 1) * LANES)
            for j in range(cpd):
                wire_s[lanes, pl.ds(j, length, stride=cpd), :] = x_s[j, :, cut]
            dy_ref[:, cut] = wire_s[lanes].astype(BF)


def whole(shape):
    return pl.BlockSpec(shape, lambda i: (0,) * len(shape))


def params():
    return pltpu.CompilerParams(
        dimension_semantics=("arbitrary",), vmem_limit_bytes=VMEM_LIMIT
    )


def row_forward(dims, rpd, recv, gain, w_qkv, w_out):
    r_size, c_size, wl, cpd, length, d = dims
    n_dev = r_size * c_size
    extra = recv.shape[1] - rpd * wl
    return pl.pallas_call(
        functools.partial(row_forward_kernel, dims),
        grid=(rpd,),
        in_specs=[
            pl.BlockSpec((c_size, wl, d), lambda i: (0, i, 0)),
            pl.BlockSpec((c_size, extra, d), lambda i: (0, rpd * wl // extra, 0)),
            whole((1, d)),
            whole((d, 3 * d)),
            whole((d, d)),
        ],
        out_specs=[
            pl.BlockSpec((n_dev, 1, cpd, d), lambda i: (0, i, 0, 0)),
            pl.BlockSpec((1, length, d), lambda i: (i, 0, 0)),
            pl.BlockSpec((1, length, 3 * d), lambda i: (i, 0, 0)),
            pl.BlockSpec((1, length, d), lambda i: (i, 0, 0)),
            pl.BlockSpec((1, HEADS, length, length), lambda i: (i, 0, 0, 0)),
        ],
        out_shape=[
            jax.ShapeDtypeStruct((n_dev, rpd, cpd, d), BF),
            jax.ShapeDtypeStruct((rpd, length, d), BF),
            jax.ShapeDtypeStruct((rpd, length, 3 * d), BF),
            jax.ShapeDtypeStruct((rpd, length, d), BF),
            jax.ShapeDtypeStruct((rpd, HEADS, length, length), BF),
        ],
        compiler_params=params(),
        name="row_forward",
    )(recv, recv, gain, w_qkv, w_out)


def row_backward(dims, rpd, recv, dy, qkv, p, gain, w_qkv, w_out):
    r_size, c_size, wl, cpd, length, d = dims
    n_dev = r_size * c_size
    return pl.pallas_call(
        functools.partial(row_backward_kernel, dims),
        grid=(rpd,),
        in_specs=[
            pl.BlockSpec((c_size, wl, d), lambda i: (0, i, 0)),
            pl.BlockSpec((n_dev, 1, cpd, d), lambda i: (0, i, 0, 0)),
            pl.BlockSpec((1, length, 3 * d), lambda i: (i, 0, 0)),
            pl.BlockSpec((1, HEADS, length, length), lambda i: (i, 0, 0, 0)),
            whole((1, d)),
            whole((d, 3 * d)),
            whole((d, d)),
        ],
        out_specs=[
            pl.BlockSpec((c_size, wl, d), lambda i: (0, i, 0)),
            pl.BlockSpec((1, length, d), lambda i: (i, 0, 0)),
            pl.BlockSpec((1, length, 3 * d), lambda i: (i, 0, 0)),
            whole((1, d)),
        ],
        out_shape=[
            jax.ShapeDtypeStruct((c_size, rpd * wl, d), BF),
            jax.ShapeDtypeStruct((rpd, length, d), BF),
            jax.ShapeDtypeStruct((rpd, length, 3 * d), BF),
            jax.ShapeDtypeStruct((1, d), F32),
        ],
        compiler_params=params(),
        name="row_backward",
    )(recv, dy, qkv, p, gain, w_qkv, w_out)


def column_stage(dims, y_wire, ct_wire, gain, w_qkv, w_out, gain_mlp, w_up, w_down):
    r_size, hl, cpd, length, d, chunk = dims
    tokens = cpd * length
    ff = w_up.shape[1]
    part = chunk * length

    def rows_of(width):
        return pl.BlockSpec((part, width), lambda i: (i, 0))

    def shape_of(width):
        return jax.ShapeDtypeStruct((tokens, width), BF)

    widths = (d, 3 * d, d, d, d, ff, ff, d)
    return pl.pallas_call(
        functools.partial(column_kernel, dims),
        grid=(cpd // chunk,),
        in_specs=[
            whole((tokens, d)),
            whole(ct_wire.shape),
            whole((1, d)),
            whole((d, 3 * d)),
            whole((d, d)),
            whole((1, d)),
            whole((d, ff)),
            whole((ff, d)),
        ],
        out_specs=[whole((tokens, d))] + [rows_of(w) for w in widths] + [whole((1, d))] * 2,
        out_shape=[shape_of(d)]
        + [shape_of(w) for w in widths]
        + [jax.ShapeDtypeStruct((1, d), F32)] * 2,
        scratch_shapes=[
            pltpu.VMEM((d // LANES, tokens, LANES), F32),
            pltpu.VMEM((cpd, length, d), F32),
            pltpu.VMEM((cpd, length, d), F32),
            pltpu.VMEM((cpd, 1, length), F32),
            pltpu.VMEM((chunk, HEADS, length, length), F32),
        ],
        compiler_params=params(),
        name="column_stage",
    )(y_wire, ct_wire, gain, w_qkv, w_out, gain_mlp, w_up, w_down)


def exchange(x, axes):
    return lax.all_to_all(x, axes, split_axis=0, concat_axis=0, tiled=True)


def wgrad(left, right, factor):
    left = left.reshape(-1, left.shape[-1])
    right = right.reshape(-1, right.shape[-1])
    return (dot_tn(left, right) * factor).astype(BF)


def total_of(rows, r_size, c_size):
    m, d = rows.shape
    part = exchange(rows, "rows").reshape(r_size, m // r_size, d)
    part = jnp.sum(part.astype(F32), axis=0).astype(BF)
    part = exchange(part, "cols").reshape(c_size, m // r_size // c_size, d)
    part = jnp.sum(part.astype(F32), axis=0).astype(BF)
    part = lax.all_gather(part, "cols", axis=0, tiled=True)
    return lax.all_gather(part, "rows", axis=0, tiled=True)


def wide(grad, d):
    return [grad[:, i * d : (i + 1) * d] for i in range(grad.shape[1] // d)]


def narrow(rows, count, d):
    return jnp.concatenate([rows[i * d : (i + 1) * d] for i in range(count)], axis=1).astype(F32)


def shards(
    tokens, key_bias, cotangent, gain_row, w_qkv_row, w_out_row,
    gain_col, w_qkv_col, w_out_col, gain_mlp, w_up, w_down,
):
    r_size, c_size = lax.axis_size("rows"), lax.axis_size("cols")
    hl, wl, d = tokens.shape
    ff = w_up.shape[1]
    rpd, cpd = hl // c_size, wl // r_size
    row_len, col_len = wl * c_size, hl * r_size
    factor = float(row_len * col_len) ** (-0.5)
    r_at, c_at = lax.axis_index("rows"), lax.axis_index("cols")
    row_dims = (r_size, c_size, wl, cpd, row_len, d)
    chunk = min(cpd, max(1, 512 // col_len))
    col_dims = (r_size, hl, cpd, col_len, d, chunk)

    place = jnp.arange(c_size)[None, :, None] == c_at
    row_extra = jnp.where(place, key_bias[:, None, :], jnp.zeros((), BF))
    row_extra = row_extra.reshape(c_size, rpd * row_len // d, d)
    pad = -row_extra.shape[1] % 8
    row_extra = jnp.pad(row_extra, ((0, 0), (0, pad), (0, 0)))
    send = jnp.concatenate([tokens.reshape(c_size, rpd * wl, d), row_extra], axis=1)
    recv = exchange(send, "cols")

    col_bias = key_bias.T.reshape(r_size, cpd, 1, hl)
    place = jnp.arange(r_size)[None, None, :, None] == r_at
    col_extra = jnp.where(place, col_bias, jnp.zeros((), BF)).reshape(r_size, cpd, col_len)
    col_extra = jnp.pad(col_extra, ((0, 0), (0, -cpd % 8), (0, d - col_len)))
    ct_send = jnp.moveaxis(cotangent.reshape(hl, r_size, cpd, d), 1, 0)
    ct_send = jnp.concatenate([ct_send.reshape(r_size, hl * cpd, d), col_extra], axis=1)
    ct_wire = exchange(ct_send, "rows")

    y_send, h1, qkv1, o1, p1 = row_forward(
        row_dims, rpd, recv, gain_row[None], w_qkv_row, w_out_row
    )
    y_wire = exchange(y_send, ALL).reshape(hl * r_size * cpd, d)
    (dy_send, h2, dqkv2, o2, dy2, h3, du, act, ct_cols, dg_col, dg_mlp) = column_stage(
        col_dims, y_wire, ct_wire, gain_col[None], w_qkv_col, w_out_col,
        gain_mlp[None], w_up, w_down,
    )
    dy_wire = exchange(dy_send.reshape(y_send.shape), ALL)

    col_parts = wide(wgrad(h2, dqkv2, factor), d)
    col_parts += [wgrad(o2, dy2, factor)]
    col_parts += wide(wgrad(h3, du, factor), d)
    col_parts += [wgrad(act, ct_cols, factor)]
    col_sums = total_of(jnp.concatenate(col_parts, axis=0), r_size, c_size)

    dt_send, dy_rows, dqkv1, dg_row = row_backward(
        row_dims, rpd, recv, dy_wire, qkv1, p1, gain_row[None], w_qkv_row, w_out_row
    )
    gains = (jnp.concatenate([dg_row, dg_col, dg_mlp], axis=0) * factor).astype(BF)
    row_parts = wide(wgrad(h1, dqkv1, factor), d)
    row_parts += [wgrad(o1, dy_rows, factor)]
    unit = 8 * r_size * c_size
    rows = 4 * d + 3
    row_parts += [jnp.pad(gains, ((0, -rows % unit), (0, 0)))]
    row_sums = total_of(jnp.concatenate(row_parts, axis=0), r_size, c_size)
    d_tokens = exchange(dt_send, "cols").reshape(hl, wl, d)

    gain_sums = row_sums[4 * d : 4 * d + 3].astype(F32)
    nff = ff // d
    return (
        d_tokens,
        gain_sums[0],
        narrow(row_sums, 3, d),
        row_sums[3 * d : 4 * d].astype(F32),
        gain_sums[1],
        narrow(col_sums, 3, d),
        col_sums[3 * d : 4 * d].astype(F32),
        gain_sums[2],
        narrow(col_sums[4 * d :], nff, d),
        col_sums[(4 + nff) * d :].astype(F32),
    )


def solution(mesh):
    cells = P("rows", "cols", None)
    in_specs = (cells, P("rows", "cols"), cells) + (P(),) * 9
    out_specs = (cells,) + (P(),) * 9
    return jax.shard_map(shards, mesh=mesh, in_specs=in_specs, out_specs=out_specs, check_vma=False)
```

time: 387 us -> 244 us (0.63)
  waiting for transfers between devices: 149 us -> 45.3 us
  matrix products: 80.4 us -> 9.12 us
  local copies, waits for them, and re-layouts: 52.3 us -> 8.38 us
  blocking collectives: 53.3 us -> 95.2 us
  Pallas kernels: 0 us -> 34.3 us
  other arithmetic: 5.81 us -> 12.6 us
  starting transfers between devices: 30.1 us -> 23.4 us
    psum x1 -> x0, waiting for transfers between devices: 103 us -> none  [shards(): lax.psum((row_sums[0], row_sums[1], row_sums[2], other_sums[0], other_sum...]
    dot_general x27 -> x6, matrix products: 72 us -> 9.12 us  [dot_tn(): lax.dot_general(a, b, (((0,), (0,)), ((), ())), preferred_element_type=F32)]
    all_gather x0 -> x3, blocking collectives: none -> 48 us  [the longest x2 37.2 us: total_of(): part = lax.all_gather(part, 'cols', axis=0, tiled=True)]
    psum x1 -> x0, blocking collectives: 41.2 us -> none  [shards(): lax.psum((row_sums[0], row_sums[1], row_sums[2], other_sums[0], other_sum...]
    all_to_all x1 -> x3, blocking collectives: 12.1 us -> 47.2 us  [exchange(): return lax.all_to_all(x, axes, split_axis=0, concat_axis=0, tiled=True)]
    pallas_call x0 -> x3, Pallas kernels: none -> 34.3 us  [the longest x1 18.6 us: column_stage(): pl.pallas_call(functools.partial(column_kernel, dims), grid=(cpd // chunk...]
    unnamed x104 -> x42, local copies, waits for them, and re-layouts: 17.6 us -> 6.52 us
    reshape x5 -> x1, local copies, waits for them, and re-layouts: 8.94 us -> 0.04 us  [shards(): ct_send.reshape(r_size, hl * cpd, d)]
  transfers between devices with their start and end apart: 9 -> 7, of which waited for: 7 -> 5; matrix products, arithmetic and copies ran while one was open for 10% -> 6% of each run, Pallas kernels for 0% -> 6%
where the time goes in v1:
time: 244 us; the launch traced here: 243 us
  blocking collectives  95.2 us (39%)
  waiting for transfers between devices  45.3 us (19%)
  Pallas kernels  34.3 us (14%)
  starting transfers between devices  23.4 us (10%)
  between operations  14.4 us (6%)
  other arithmetic  12.6 us (5%)
  matrix products  9.12 us (4%)
  local copies, waits for them, and re-layouts  8.38 us (3%)
    all_to_all x3, blocking collectives, exchange(): return lax.all_to_all(x, axes, split_axis=0, concat_axis=0, tiled=True)  47.2 us
    all_to_all x6, waiting for transfers between devices, exchange(): return lax.all_to_all(x, axes, split_axis=0, concat_axis=0, tiled=True)  45.3 us
    all_gather x2, blocking collectives, total_of(): part = lax.all_gather(part, 'cols', axis=0, tiled=True)  37.2 us
    all_to_all x6, starting transfers between devices, exchange(): return lax.all_to_all(x, axes, split_axis=0, concat_axis=0, tiled=True)  23.3 us
    pallas_call x1, Pallas kernels, column_stage(): pl.pallas_call(functools.partial(column_kernel, dims), grid=(cpd // chunk...  18.6 us
    all_gather x1, blocking collectives, total_of(): return lax.all_gather(part, 'rows', axis=0, tiled=True)  10.8 us
    dot_general x6, matrix products, dot_tn(): lax.dot_general(a, b, (((0,), (0,)), ((), ())), preferred_element_type=F32)  9.12 us
    pallas_call x1, Pallas kernels, row_backward(): pl.pallas_call(functools.partial(row_backward_kernel, dims), grid=(rpd,),...  7.89 us
  transfers between devices with their start and end apart: 7, of which 5 were waited for; matrix products, arithmetic and copies ran while one was open for 6% of the time, Pallas kernels for 6%

profile of v1, /device:TPU:0, one launch (start us, length us, event | category | flops | bytes accessed | tf_op | source)
XLA Modules:
  0.0 242.6 jit_solution(18004804276502317910)
XLA Ops:
  7.4 0.7 broadcast_in_dim.70
  8.2 1.9 fusion.13
  10.1 6.3 %all-to-all-start = ((bf16[8,136,256]{2,1,0:T(8,128)(2,1)}), bf16[8,136,256]{2,1,0:T(8,128)(2,1)S(1)}, u32[]{:S(2)}, u32[]{:S(2)}) async-start(bf16[8,136,256]{2,1,0:T(8,128)(2,1)} %fusion.13), calls=%async_computation | async-start | bytes 1114112 | tf_op jit(solution)/shard_map/all_to_all | solution.py:379
  16.9 0.8 fusion.14
  17.7 14.8 %all-to-all-done.x_ref.b_ref = bf16[8,136,256]{2,1,0:T(8,128)(2,1)S(1)} async-done(((bf16[8,136,256]{2,1,0:T(8,128)(2,1)}), bf16[8,136,256]{2,1,0:T(8,128)(2,1)S(1)}, u32[]{:S(2)}, u32[]{:S(2)}) %all-to-all-start) | async-done | bytes 557088 | tf_op jit(solution)/shard_map/all_to_all | solution.py:379
  32.5 3.7 %all-to-all-start.2 = ((bf16[4,264,256]{2,1,0:T(8,128)(2,1)}), bf16[4,264,256]{2,1,0:T(8,128)(2,1)S(1)}, u32[]{:S(2)}, u32[]{:S(2)}) async-start(bf16[4,264,256]{2,1,0:T(8,128)(2,1)} %fusion.14), calls=%async_computation.2 | async-start | bytes 1081344 | tf_op jit(solution)/shard_map/all_to_all | solution.py:379
  36.2 7.8 %row_forward.1 = (bf16[32,4,8,256]{3,2,1,0:T(8,128)(2,1)}, bf16[4,256,256]{2,1,0:T(8,128)(2,1)}, bf16[4,256,768]{2,1,0:T(8,128)(2,1)}, bf16[4,256,256]{2,1,0:T(8,128)(2,1)}, bf16[4,4,256,256]{3,2,1,0:T(8,128)(2,1)}) custom-call(bf16[8,136,256]{2,1,0:T(8,128)(2,1)} %copy-done.1, bf16[8,136,256]{2,1,0:T(8,128)(2,1)} %copy-done.1, f32[1,256]{1,0:T(1,128)} %bitcast.57, ...), custom_call_target="tpu_custom_call" | custom-call | tf_op jit(solution)/shard_map/row_forward/pallas_call | solution.py:275
  44.0 0.2 all-to-all-done.2.ct_ref
  44.2 20.2 %all_to_all.61 = bf16[32,4,8,256]{3,2,1,0:T(8,128)(2,1)} all-to-all(bf16[32,4,8,256]{3,2,1,0:T(8,128)(2,1)} %get-tuple-element.30), channel_id=1, replica_groups=mesh['rows'=4,'cols'=8] {'rows','cols'}, dimensions={0} | all-to-all | bytes 1048576 | tf_op jit(solution)/shard_map/all_to_all | solution.py:379
  64.5 18.6 %column_stage.1 = (bf16[1024,256]{1,0:T(8,128)(2,1)}, bf16[1024,256]{1,0:T(8,128)(2,1)}, bf16[1024,768]{1,0:T(8,128)(2,1)}, bf16[1024,256]{1,0:T(8,128)(2,1)}, b...) custom-call(bf16[1024,256]{1,0:T(8,128)(2,1)} %bitcast.51, ...), custom_call_target="tpu_custom_call" | custom-call | tf_op jit(solution)/shard_map/column_stage/pallas_call | solution.py:349
  83.1 2.3 fusion.5
  85.4 0.7 slice_dynamic-update-slice_fusion.6
  86.1 0.7 slice_dynamic-update-slice_fusion.5
  86.8 0.7 slice_dynamic-update-slice_fusion.4
  87.5 2.6 %all-to-all-start.3 = ((bf16[32,4,8,256]{3,2,1,0:T(8,128)(2,1)}), bf16[32,4,8,256]{3,2,1,0:T(8,128)(2,1)S(1)}, u32[]{:S(2)}, u32[]{:S(2)}) async-start(bf16[32,4,8,256]{3,2,1,0:T(8,128)(2,1)} %bitcast.55), calls=%async_computation.3 | async-start | bytes 1048576 | tf_op jit(solution)/shard_map/all_to_all | solution.py:379
  90.1 1.9 fusion
  92.0 1.0 fusion.8
  93.0 0.7 slice_dynamic-update-slice_fusion.3
  93.7 0.7 slice_dynamic-update-slice_fusion.2
  94.4 0.7 slice_dynamic-update-slice_fusion.1
  95.0 0.7 slice_dynamic-update-slice_fusion
  95.7 1.6 fusion.2
  97.3 9.1 %all-to-all-done.3.dy_ref = bf16[32,4,8,256]{3,2,1,0:T(8,128)(2,1)S(1)} async-done(((bf16[32,4,8,256]{3,2,1,0:T(8,128)(2,1)}), bf16[32,4,8,256]{3,2,1,0:T(8,128)(2,1)S(1)}, u32[]{:S(2)}, u32[]{:S(2)}) %all-to-all-start.3) | async-done | bytes 524320 | tf_op jit(solution)/shard_map/all_to_all | solution.py:379
  106.4 0.8 copy-done.3
  107.2 3.7 %all-to-all-start.7 = ((bf16[4,768,256]{2,1,0:T(8,128)(2,1)}), bf16[4,768,256]{2,1,0:T(8,128)(2,1)S(1)}, u32[]{:S(2)}, u32[]{:S(2)}) async-start(bf16[4,768,256]{2,1,0:T(8,128)(2,1)} %bitcast.18), calls=%async_computation.7 | async-start | bytes 3145728 | tf_op jit(solution)/shard_map/all_to_all | solution.py:379
  111.0 7.9 %row_backward.1 = (bf16[8,128,256]{2,1,0:T(8,128)(2,1)}, bf16[4,256,256]{2,1,0:T(8,128)(2,1)}, bf16[4,256,768]{2,1,0:T(8,128)(2,1)}, f32[1,256]{1,0:T(1,128)}) custom-call(bf16[8,136,256]{2,1,0:T(8,128)(2,1)} %copy-done.1, bf16[32,4,8,256]{3,2,1,0:T(8,128)(2,1)} %copy-done.3, bf16[4,256,768]{2,1,0:T(8,128)(2,1)} %get-tuple-element.32.qkv_ref, ...), custom_call_target="tpu_custom_call" | custom-call | tf_op jit(solution)/shard_map/row_backward/pallas_call | solution.py:307
  118.9 0.7 fusion.15
  119.7 10.8 %all-to-all-done.7 = bf16[4,768,256]{2,1,0:T(8,128)(2,1)S(1)} async-done(((bf16[4,768,256]{2,1,0:T(8,128)(2,1)}), bf16[4,768,256]{2,1,0:T(8,128)(2,1)S(1)}, u32[]{:S(2)}, u32[]{:S(2)}) %all-to-all-start.7) | async-done | bytes 1572896 | tf_op jit(solution)/shard_map/all_to_all | solution.py:379
  130.5 1.1 reduce_sum.50
  131.5 3.5 %all-to-all-start.8 = ((bf16[8,96,256]{2,1,0:T(8,128)(2,1)}), bf16[8,96,256]{2,1,0:T(8,128)(2,1)S(1)}, u32[]{:S(2)}, u32[]{:S(2)}) async-start(bf16[8,96,256]{2,1,0:T(8,128)(2,1)} %bitcast.19), calls=%async_computation.8 | async-start | bytes 786432 | tf_op jit(solution)/shard_map/all_to_all | solution.py:379
  135.1 2.0 fusion.4
  137.1 10.3 %all-to-all-done.8 = bf16[8,96,256]{2,1,0:T(8,128)(2,1)S(1)} async-done(((bf16[8,96,256]{2,1,0:T(8,128)(2,1)}), bf16[8,96,256]{2,1,0:T(8,128)(2,1)S(1)}, u32[]{:S(2)}, u32[]{:S(2)}) %all-to-all-start.8) | async-done | bytes 393248 | tf_op jit(solution)/shard_map/all_to_all | solution.py:379
  147.5 15.5 %all_gather.14 = bf16[768,256]{1,0:T(8,128)(2,1)} all-gather(bf16[96,256]{1,0:T(8,128)(2,1)S(1)} %reduce_sum.51), channel_id=1, replica_groups=mesh['rows'=4,'cols'=8] {'cols'}, dimensions={0}, use_global_device_ids=true | all-gather | bytes 442368 | tf_op jit(solution)/shard_map/all_gather | solution.py:394
  163.1 0.3 fusion.10
  163.5 17.3 %all_to_all.62 = bf16[4,320,256]{2,1,0:T(8,128)(2,1)S(1)} all-to-all(bf16[4,320,256]{2,1,0:T(8,128)(2,1)S(1)} %bitcast.52), channel_id=1, replica_groups=mesh['rows'=4,'cols'=8] {'rows'}, dimensions={0} | all-to-all | bytes 1310720 | tf_op jit(solution)/shard_map/all_to_all | solution.py:379
  180.8 0.1 reduce_sum.48
  180.9 9.6 %all_to_all.63 = bf16[8,40,256]{2,1,0:T(8,128)(2,1)S(1)} all-to-all(bf16[8,40,256]{2,1,0:T(8,128)(2,1)S(1)} %bitcast.53), channel_id=1, replica_groups=mesh['rows'=4,'cols'=8] {'cols'}, dimensions={0} | all-to-all | bytes 327680 | tf_op jit(solution)/shard_map/all_to_all | solution.py:379
  190.6 3.5 %all-to-all-start.4 = ((bf16[8,128,256]{2,1,0:T(8,128)(2,1)}), bf16[8,128,256]{2,1,0:T(8,128)(2,1)S(1)}, u32[]{:S(2)}, u32[]{:S(2)}) async-start(bf16[8,128,256]{2,1,0:T(8,128)(2,1)} %get-tuple-element.34), calls=%async_computation.4 | async-start | bytes 1048576 | tf_op jit(solution)/shard_map/all_to_all | solution.py:379
  194.1 21.6 %all_gather.12 = bf16[320,256]{1,0:T(8,128)(2,1)S(1)} all-gather(bf16[40,256]{1,0:T(8,128)(2,1)S(1)} %reduce_sum.49), channel_id=1, replica_groups=mesh['rows'=4,'cols'=8] {'cols'}, dimensions={0}, use_global_device_ids=true | all-gather | bytes 184320 | tf_op jit(solution)/shard_map/all_gather | solution.py:394
  215.7 10.8 %all_gather.13 = bf16[1280,256]{1,0:T(8,128)(2,1)S(1)} all-gather(bf16[320,256]{1,0:T(8,128)(2,1)S(1)} %all_gather.12), channel_id=1, replica_groups=mesh['rows'=4,'cols'=8] {'rows'}, dimensions={0}, use_global_device_ids=true | all-gather | bytes 819200 | tf_op jit(solution)/shard_map/all_gather | solution.py:395
  226.6 0.8 slice_convert_fusion.2
  227.3 0.9 maximum_convert_fusion.1
  228.2 0.6 fusion.17
  228.8 2.1 fusion.16
  230.9 0.9 maximum_convert_fusion.2
  231.8 1.1 maximum_convert_fusion
  232.9 2.1 slice_convert_fusion
  235.0 0.8 copy.50
  (53 shorter events, 1.0 us)
Async XLA Ops:
  7.2 9.6 %copy-start = (bf16[32,32,256]{2,1,0:T(8,128)(2,1)S(1)}, bf16[32,32,256]{2,1,0:T(8,128)(2,1)}, u32[]{:S(2)}) copy-start(bf16[32,32,256]{2,1,0:T(8,128)(2,1)} %param.14) | copy-start | bytes 1572868
  7.2 9.2 %copy-start.6 = (bf16[32,32]{1,0:T(8,128)(2,1)S(1)}, bf16[32,32]{1,0:T(8,128)(2,1)}, u32[]{:S(2)}) copy-start(bf16[32,32]{1,0:T(8,128)(2,1)} %param.13) | copy-start | bytes 6148
  10.1 22.4 %all-to-all-start = ((bf16[8,136,256]{2,1,0:T(8,128)(2,1)}), bf16[8,136,256]{2,1,0:T(8,128)(2,1)S(1)}, u32[]{:S(2)}, u32[]{:S(2)}) async-start(bf16[8,136,256]{2,1,0:T(8,128)(2,1)} %fusion.13), calls=%async_computation | async-start | bytes 1114112 | tf_op jit(solution)/shard_map/all_to_all | solution.py:379
  32.5 3.7 %copy-start.1 = (bf16[8,136,256]{2,1,0:T(8,128)(2,1)}, bf16[8,136,256]{2,1,0:T(8,128)(2,1)S(1)}, u32[]{:S(2)}) copy-start(bf16[8,136,256]{2,1,0:T(8,128)(2,1)S(1)} %all-to-all-done.x_ref.b_ref) | copy-start | bytes 1671172
  32.5 11.7 %all-to-all-start.2 = ((bf16[4,264,256]{2,1,0:T(8,128)(2,1)}), bf16[4,264,256]{2,1,0:T(8,128)(2,1)S(1)}, u32[]{:S(2)}, u32[]{:S(2)}) async-start(bf16[4,264,256]{2,1,0:T(8,128)(2,1)} %fusion.14), calls=%async_computation.2 | async-start | bytes 1081344 | tf_op jit(solution)/shard_map/all_to_all | solution.py:379
  44.2 20.3 %copy-start.2 = (bf16[4,264,256]{2,1,0:T(8,128)(2,1)}, bf16[4,264,256]{2,1,0:T(8,128)(2,1)S(1)}, u32[]{:S(2)}) copy-start(bf16[4,264,256]{2,1,0:T(8,128)(2,1)S(1)} %all-to-all-done.2.ct_ref) | copy-start | bytes 1622020
  83.1 7.0 %copy-start.4 = (bf16[1024,1024]{1,0:T(8,128)(2,1)S(1)}, bf16[1024,1024]{1,0:T(8,128)(2,1)}, u32[]{:S(2)}) copy-start(bf16[1024,1024]{1,0:T(8,128)(2,1)} %get-tuple-element.47) | copy-start | bytes 6291460
  87.5 19.0 %all-to-all-start.3 = ((bf16[32,4,8,256]{3,2,1,0:T(8,128)(2,1)}), bf16[32,4,8,256]{3,2,1,0:T(8,128)(2,1)S(1)}, u32[]{:S(2)}, u32[]{:S(2)}) async-start(bf16[32,4,8,256]{3,2,1,0:T(8,128)(2,1)} %bitcast.55), calls=%async_computation.3 | async-start | bytes 1048576 | tf_op jit(solution)/shard_map/all_to_all | solution.py:379
  90.1 1.9 copy-start.13
  90.1 1.9 copy-start.14
  90.1 5.6 %copy-start.12 = (bf16[1024,256]{1,0:T(8,128)(2,1)S(1)}, bf16[1024,256]{1,0:T(8,128)(2,1)}, u32[]{:S(2)}) copy-start(bf16[1024,256]{1,0:T(8,128)(2,1)} %get-tuple-element.49) | copy-start | bytes 1572868
  92.0 3.7 %copy-start.9 = (bf16[1024,1024]{1,0:T(8,128)(2,1)S(1)}, bf16[1024,1024]{1,0:T(8,128)(2,1)}, u32[]{:S(2)}) copy-start(bf16[1024,1024]{1,0:T(8,128)(2,1)} %get-tuple-element.48) | copy-start | bytes 6291460
  106.4 0.8 copy-start.3
  107.2 23.2 %all-to-all-start.7 = ((bf16[4,768,256]{2,1,0:T(8,128)(2,1)}), bf16[4,768,256]{2,1,0:T(8,128)(2,1)S(1)}, u32[]{:S(2)}, u32[]{:S(2)}) async-start(bf16[4,768,256]{2,1,0:T(8,128)(2,1)} %bitcast.18), calls=%async_computation.7 | async-start | bytes 3145728 | tf_op jit(solution)/shard_map/all_to_all | solution.py:379
  111.0 7.9 %copy-start.7 = (f32[1,256]{1,0:T(1,128)S(1)}, f32[1,256]{1,0:T(1,128)}, u32[]{:S(2)}) copy-start(f32[1,256]{1,0:T(1,128)} %get-tuple-element.40) | copy-start | bytes 3076
  111.0 7.9 %copy-start.8 = (f32[1,256]{1,0:T(1,128)S(1)}, f32[1,256]{1,0:T(1,128)}, u32[]{:S(2)}) copy-start(f32[1,256]{1,0:T(1,128)} %get-tuple-element.41) | copy-start | bytes 3076
  118.9 16.2 %copy-start.5 = (bf16[4,256,256]{2,1,0:T(8,128)(2,1)S(1)}, bf16[4,256,256]{2,1,0:T(8,128)(2,1)}, u32[]{:S(2)}) copy-start(bf16[4,256,256]{2,1,0:T(8,128)(2,1)} %get-tuple-element.35) | copy-start | bytes 1572868
  131.5 15.9 %all-to-all-start.8 = ((bf16[8,96,256]{2,1,0:T(8,128)(2,1)}), bf16[8,96,256]{2,1,0:T(8,128)(2,1)S(1)}, u32[]{:S(2)}, u32[]{:S(2)}) async-start(bf16[8,96,256]{2,1,0:T(8,128)(2,1)} %bitcast.19), calls=%async_computation.8 | async-start | bytes 786432 | tf_op jit(solution)/shard_map/all_to_all | solution.py:379
  135.0 93.8 %all-gather.2.cloned.1.call-start = ((), (), s32[]{:S(2)}) async-start(), calls=%async_computation.9 | async-start | bytes 1966080 | tf_op jit(solution)/shard_map/all_gather | solution.py:395
  137.1 26.0 %copy-start.10 = (bf16[4,256,256]{2,1,0:T(8,128)(2,1)S(1)}, bf16[4,256,256]{2,1,0:T(8,128)(2,1)}, u32[]{:S(2)}) copy-start(bf16[4,256,256]{2,1,0:T(8,128)(2,1)} %get-tuple-element.37) | copy-start | bytes 1572868
  137.1 26.0 %copy-start.11 = (bf16[4,256,256]{2,1,0:T(8,128)(2,1)S(1)}, bf16[4,256,256]{2,1,0:T(8,128)(2,1)}, u32[]{:S(2)}) copy-start(bf16[4,256,256]{2,1,0:T(8,128)(2,1)} %get-tuple-element.38) | copy-start | bytes 1572868
  190.6 38.3 %all-to-all-start.4 = ((bf16[8,128,256]{2,1,0:T(8,128)(2,1)}), bf16[8,128,256]{2,1,0:T(8,128)(2,1)S(1)}, u32[]{:S(2)}, u32[]{:S(2)}) async-start(bf16[8,128,256]{2,1,0:T(8,128)(2,1)} %get-tuple-element.34), calls=%async_computation.4 | async-start | bytes 1048576 | tf_op jit(solution)/shard_map/all_to_all | solution.py:379
Sparse Core Ops, SparseCore 0:
  163.2 31.4 all-gather.1

commit v2 on v1

--- a/solution.py
+++ b/solution.py
@@ -101,7 +101,7 @@
 
 
 def row_forward_kernel(
-    dims, x_ref, b_ref, gain_ref, wqkv_ref, wout_ref, y_ref, h_ref, qkv_ref, o_ref, p_ref
+    dims, x_ref, b_ref, gain_ref, wqkv_ref, wout_ref, y_ref, qkv_ref, o_ref, p_ref
 ):
     r_size, c_size, wl, cpd, length, d = dims
     factor = float(d // HEADS) ** (-0.5)
@@ -109,7 +109,6 @@
     x = load_cells(x_ref, c_size)
     n, _ = norm(x)
     h = (n * gain_ref[...]).astype(BF)
-    h_ref[0] = h
     qkv = dot(h, wqkv_ref[...]).astype(BF)
     qkv_ref[0] = qkv
     q, k, v = qkv[:, :d], qkv[:, d : 2 * d], qkv[:, 2 * d :]
@@ -127,19 +126,45 @@
             y_ref[r * c_size + c, 0] = y[at : at + cpd]
 
 
+def store_rows(keep_ref, send_ref, parity, row, value):
+    half = keep_ref.shape[0]
+    for side in range(2):
+        start, stop = max(row, side * half), min(row + value.shape[0], (side + 1) * half)
+        if start < stop:
+            piece = value[start - row : stop - row]
+            to = slice(start - side * half, stop - side * half)
+
+            @pl.when(parity == side)
+            def _():
+                keep_ref[to] = piece
+
+            @pl.when(parity != side)
+            def _():
+                send_ref[to] = piece
+
+
 def row_backward_kernel(
-    dims, x_ref, dy_ref, qkv_ref, p_ref, gain_ref, wqkv_ref, wout_ref,
-    dt_ref, dyr_ref, dqkv_ref, dg_ref,
+    dims, x_ref, dy_ref, qkv_ref, o_ref, p_ref, gain_ref, wqkv_ref, wout_ref, dgc_ref, dgm_ref,
+    dt_ref, keep_ref, send_ref, dg_s, dwqkv_s, dwout_s,
 ):
     r_size, c_size, wl, cpd, length, d = dims
+    step, steps = pl.program_id(0), pl.num_programs(0)
     factor = float(d // HEADS) ** (-0.5)
     masks = head_masks(d)
+
+    @pl.when(step == 0)
+    def _():
+        dg_s[...] = jnp.zeros_like(dg_s)
+        dwqkv_s[...] = jnp.zeros_like(dwqkv_s)
+        dwout_s[...] = jnp.zeros_like(dwout_s)
+        keep_ref[...] = jnp.zeros_like(keep_ref)
+        send_ref[...] = jnp.zeros_like(send_ref)
+
     dy = jnp.concatenate(
         [dy_ref[r * c_size + c, 0].astype(F32) for c in range(c_size) for r in range(r_size)],
         axis=0,
     )
     dy_low = dy.astype(BF)
-    dyr_ref[0] = dy_low
     do = dot_nt(dy_low, wout_ref[...]).astype(BF)
     qkv = qkv_ref[0]
     q, k, v = qkv[:, :d], qkv[:, d : 2 * d], qkv[:, 2 * d :]
@@ -147,33 +172,160 @@
     weights = [w.astype(F32) for w in low]
     dq, dk, dv = heads_back(weights, low, do, q, k, v, masks, factor)
     dqkv = jnp.concatenate([dq, dk, dv], axis=1)
-    dqkv_ref[0] = dqkv
     g = dot_nt(dqkv, wqkv_ref[...])
     n, inverse = norm(load_cells(x_ref, c_size))
+    h = (n * gain_ref[...]).astype(BF)
     dt = (dy + norm_back(g, n, inverse, gain_ref[...])).astype(BF)
     for s in range(c_size):
         dt_ref[s] = dt[s * wl : (s + 1) * wl]
-    dg = jnp.sum(g * n, axis=0, keepdims=True)
-
-    @pl.when(pl.program_id(0) == 0)
+    dg_s[...] += jnp.sum(g * n, axis=0, keepdims=True)
+    dwqkv_s[...] += dot_tn(h, dqkv)
+    dwout_s[...] += dot_tn(o_ref[0], dy_low)
+
+    @pl.when(step == steps - 1)
     def _():
-        dg_ref[...] = dg
-
-    @pl.when(pl.program_id(0) != 0)
+        scale = float(length * steps * r_size * c_size) ** (-0.5)
+        parity = lax.rem(lax.axis_index("cols"), 2)
+        for i in range(3):
+            grad = (dwqkv_s[:, i * d : (i + 1) * d] * scale).astype(BF)
+            store_rows(keep_ref, send_ref, parity, i * d, grad)
+        store_rows(keep_ref, send_ref, parity, 3 * d, (dwout_s[...] * scale).astype(BF))
+        gains = jnp.concatenate(
+            [dg_s[...], dgc_ref[...], dgm_ref[...], jnp.zeros((5, d), F32)], axis=0
+        )
+        store_rows(keep_ref, send_ref, parity, 4 * d, (gains * scale).astype(BF))
+
+
+def pack_tokens_kernel(dims, x_ref, b_ref, out_ref):
+    r_size, c_size, wl, cpd, length, d = dims
+    cells = x_ref.shape[1]
+    rpd = cells // wl
+    extra = out_ref.shape[1] - cells
+    lane = lax.broadcasted_iota(jnp.int32, (wl, length), 1)
+    cell = lax.broadcasted_iota(jnp.int32, (wl, length), 0)
+    place = (lane == cell + lax.axis_index("cols") * wl).astype(F32).astype(BF)
+    spread = dot(b_ref[...], place)
+    parts = length // d
+    for s in range(c_size):
+        out_ref[s, :cells] = x_ref[s]
+        rows = [
+            spread[s * rpd + i : s * rpd + i + 1, t * d : (t + 1) * d]
+            for i in range(rpd)
+            for t in range(parts)
+        ]
+        if extra > rpd * parts:
+            rows.append(jnp.zeros((extra - rpd * parts, d), F32))
+        out_ref[s, cells:] = jnp.concatenate(rows, axis=0).astype(BF)
+
+
+def pack_cotangent_kernel(dims, ct_ref, b_ref, *out_refs):
+    r_size, hl, cpd, length, d = dims
+    r_at = lax.axis_index("rows")
+    lane = lax.broadcasted_iota(jnp.int32, (hl, d), 1)
+    cell = lax.broadcasted_iota(jnp.int32, (hl, d), 0)
+    place = (lane == cell + r_at * hl).astype(F32).astype(BF)
+    spread = dot_tn(b_ref[...], place)
+    for s in range(r_size):
+        for r in range(r_size):
+
+            @pl.when(jnp.bitwise_xor(r_at, s) == r)
+            def _():
+                out_refs[s][: hl * cpd] = (
+                    ct_ref[:, r * cpd : (r + 1) * cpd, :].astype(F32).reshape(hl * cpd, d).astype(BF)
+                )
+                rows = spread[r * cpd : (r + 1) * cpd]
+                if cpd % 8:
+                    rows = jnp.concatenate([rows, jnp.zeros((-cpd % 8, d), F32)], axis=0)
+                out_refs[s][hl * cpd :] = rows.astype(BF)
+
+
+def weight_grad_kernel(
+    scale, h2_ref, dqkv_ref, o2_ref, dy2_ref, h3_ref, du_ref, act_ref, ct_ref,
+    keep_ref, send_ref, dwqkv_s, dwout_s, dwup_s, dwdown_s,
+):
+    step, steps = pl.program_id(0), pl.num_programs(0)
+    sums = (
+        (dwqkv_s, h2_ref, dqkv_ref),
+        (dwout_s, o2_ref, dy2_ref),
+        (dwup_s, h3_ref, du_ref),
+        (dwdown_s, act_ref, ct_ref),
+    )
+
+    @pl.when(step == 0)
     def _():
-        dg_ref[...] += dg
+        for total, left, right in sums:
+            total[...] = dot_tn(left[...], right[...])
+
+    @pl.when(step != 0)
+    def _():
+        for total, left, right in sums:
+            total[...] += dot_tn(left[...], right[...])
+
+    @pl.when(step == steps - 1)
+    def _():
+        parity = lax.rem(lax.axis_index("cols"), 2)
+        d = dwout_s.shape[0]
+        row = 0
+        for total, _, _ in sums[:3]:
+            for i in range(total.shape[1] // d):
+                grad = (total[:, i * d : (i + 1) * d] * scale).astype(BF)
+                store_rows(keep_ref, send_ref, parity, row, grad)
+                row += d
+        store_rows(keep_ref, send_ref, parity, row, (dwdown_s[...] * scale).astype(BF))
+        row += dwdown_s.shape[0]
+        if row < 2 * keep_ref.shape[0]:
+            rest = jnp.zeros((2 * keep_ref.shape[0] - row, d), BF)
+            store_rows(keep_ref, send_ref, parity, row, rest)
+
+
+def unpack_kernel(dims, own_ref, got_ref, *out_refs):
+    r_size, z_size, col_rows, row_rows, d, layout = dims
+    r_at, c_at = lax.axis_index("rows"), lax.axis_index("cols")
+    z_at, parity = lax.div(c_at, 2), lax.rem(c_at, 2)
+    for core in range(2):
+        for r in range(r_size):
+            for z in range(z_size):
+                at = (core * r_size + r) * z_size + z
+                s, t = jnp.bitwise_xor(r_at, r), jnp.bitwise_xor(z_at, z)
+                for base, size, sections in (
+                    (0, col_rows, layout[0]),
+                    (col_rows, row_rows, layout[1]),
+                ):
+                    first = at * size
+                    for start, stop, which, row0, lane0 in sections:
+                        low, high = max(first, start), min(first + size, stop)
+                        if low >= high:
+                            continue
+                        cut = slice(base + low - first, base + high - first)
+                        to = slice(row0 + low - start, row0 + high - start)
+                        lanes = slice(lane0, lane0 + d)
+                        out_ref = out_refs[which]
+
+                        @pl.when(parity == core)
+                        def _():
+                            out_ref[to, lanes] = own_ref[s, t, cut, :].astype(F32)
+
+                        @pl.when(parity != core)
+                        def _():
+                            out_ref[to, lanes] = got_ref[s, t, cut, :].astype(F32)
 
 
 def column_kernel(
-    dims, y_ref, ct_ref, gain_ref, wqkv_ref, wout_ref, gmlp_ref, wup_ref, wdown_ref,
-    dy_ref, h2_ref, dqkv_ref, o2_ref, dy2_ref, h3_ref, du_ref, act_ref, ctc_ref, dg_ref, dgm_ref,
-    wire_s, x_s, ct_s, bias_s, p_s,
+    dims, *refs
 ):
     r_size, hl, cpd, length, d, chunk = dims
+    y_ref, *ct_refs = refs[: 1 + r_size]
+    (
+        gain_ref, wqkv_ref, wout_ref, gmlp_ref, wup_ref, wdown_ref,
+        dy_ref, h2_ref, dqkv_ref, o2_ref, dy2_ref, h3_ref, du_ref, act_ref, ctc_ref,
+        dg_ref, dgm_ref, wire_s, x_s, ct_s, bias_s, p_s,
+    ) = refs[1 + r_size :]
     step, steps = pl.program_id(0), pl.num_programs(0)
     factor = float(d // HEADS) ** (-0.5)
     masks = head_masks(d)
     tokens = chunk * length
+
+    r_at = lax.axis_index("rows")
 
     @pl.when(step == 0)
     def _():
@@ -185,13 +337,15 @@
         block = hl * cpd
         for lanes in range(d // LANES):
             cut = slice(lanes * LANES, (lanes + 1) * LANES)
-            for r in range(r_size):
-                wire_s[lanes, r * block : (r + 1) * block, :] = ct_ref[r, :block, cut].astype(F32)
+            for s in range(r_size):
+                source = jnp.bitwise_xor(r_at, s)
+                to = pl.ds(pl.multiple_of(source * block, block), block)
+                wire_s[lanes, to, :] = ct_refs[s][:block, cut].astype(F32)
             for j in range(cpd):
                 ct_s[j, :, cut] = wire_s[lanes, pl.ds(j, length, stride=cpd), :]
-        total = ct_ref[0, block:].astype(F32)
-        for r in range(1, r_size):
-            total = total + ct_ref[r, block:].astype(F32)
+        total = ct_refs[0][block:].astype(F32)
+        for s in range(1, r_size):
+            total = total + ct_refs[s][block:].astype(F32)
         for j in range(cpd):
             bias_s[j] = total[j : j + 1, :length]
         dg_ref[...] = jnp.zeros_like(dg_ref)
@@ -268,6 +422,16 @@
     )
 
 
+def whole(shape):
+    return pl.BlockSpec(shape, lambda i: (0,) * len(shape))
+
+
+def params():
+    return pltpu.CompilerParams(
+        dimension_semantics=("arbitrary",), vmem_limit_bytes=VMEM_LIMIT
+    )
+
+
 def row_forward(dims, rpd, recv, gain, w_qkv, w_out):
     r_size, c_size, wl, cpd, length, d = dims
     n_dev = r_size * c_size
@@ -284,14 +448,12 @@
         ],
         out_specs=[
             pl.BlockSpec((n_dev, 1, cpd, d), lambda i: (0, i, 0, 0)),
-            pl.BlockSpec((1, length, d), lambda i: (i, 0, 0)),
             pl.BlockSpec((1, length, 3 * d), lambda i: (i, 0, 0)),
             pl.BlockSpec((1, length, d), lambda i: (i, 0, 0)),
             pl.BlockSpec((1, HEADS, length, length), lambda i: (i, 0, 0, 0)),
         ],
         out_shape=[
             jax.ShapeDtypeStruct((n_dev, rpd, cpd, d), BF),
-            jax.ShapeDtypeStruct((rpd, length, d), BF),
             jax.ShapeDtypeStruct((rpd, length, 3 * d), BF),
             jax.ShapeDtypeStruct((rpd, length, d), BF),
             jax.ShapeDtypeStruct((rpd, HEADS, length, length), BF),
@@ -301,7 +463,7 @@
     )(recv, recv, gain, w_qkv, w_out)
 
 
-def row_backward(dims, rpd, recv, dy, qkv, p, gain, w_qkv, w_out):
+def row_backward(dims, rpd, half, recv, dy, qkv, o, p, gain, w_qkv, w_out, dg_col, dg_mlp):
     r_size, c_size, wl, cpd, length, d = dims
     n_dev = r_size * c_size
     return pl.pallas_call(
@@ -311,29 +473,35 @@
             pl.BlockSpec((c_size, wl, d), lambda i: (0, i, 0)),
             pl.BlockSpec((n_dev, 1, cpd, d), lambda i: (0, i, 0, 0)),
             pl.BlockSpec((1, length, 3 * d), lambda i: (i, 0, 0)),
+            pl.BlockSpec((1, length, d), lambda i: (i, 0, 0)),
             pl.BlockSpec((1, HEADS, length, length), lambda i: (i, 0, 0, 0)),
             whole((1, d)),
             whole((d, 3 * d)),
             whole((d, d)),
+            whole((1, d)),
+            whole((1, d)),
         ],
         out_specs=[
             pl.BlockSpec((c_size, wl, d), lambda i: (0, i, 0)),
-            pl.BlockSpec((1, length, d), lambda i: (i, 0, 0)),
-            pl.BlockSpec((1, length, 3 * d), lambda i: (i, 0, 0)),
-            whole((1, d)),
+            whole((half, d)),
+            whole((half, d)),
         ],
         out_shape=[
             jax.ShapeDtypeStruct((c_size, rpd * wl, d), BF),
-            jax.ShapeDtypeStruct((rpd, length, d), BF),
-            jax.ShapeDtypeStruct((rpd, length, 3 * d), BF),
-            jax.ShapeDtypeStruct((1, d), F32),
+            jax.ShapeDtypeStruct((half, d), BF),
+            jax.ShapeDtypeStruct((half, d), BF),
+        ],
+        scratch_shapes=[
+            pltpu.VMEM((1, d), F32),
+            pltpu.VMEM((d, 3 * d), F32),
+            pltpu.VMEM((d, d), F32),
         ],
         compiler_params=params(),
         name="row_backward",
-    )(recv, dy, qkv, p, gain, w_qkv, w_out)
-
-
-def column_stage(dims, y_wire, ct_wire, gain, w_qkv, w_out, gain_mlp, w_up, w_down):
+    )(recv, dy, qkv, o, p, gain, w_qkv, w_out, dg_col, dg_mlp)
+
+
+def column_stage(dims, y_wire, ct_blocks, gain, w_qkv, w_out, gain_mlp, w_up, w_down):
     r_size, hl, cpd, length, d, chunk = dims
     tokens = cpd * length
     ff = w_up.shape[1]
@@ -351,7 +519,7 @@
         grid=(cpd // chunk,),
         in_specs=[
             whole((tokens, d)),
-            whole(ct_wire.shape),
+            *[whole(block.shape) for block in ct_blocks],
             whole((1, d)),
             whole((d, 3 * d)),
             whole((d, d)),
@@ -372,35 +540,86 @@
         ],
         compiler_params=params(),
         name="column_stage",
-    )(y_wire, ct_wire, gain, w_qkv, w_out, gain_mlp, w_up, w_down)
+    )(y_wire, *ct_blocks, gain, w_qkv, w_out, gain_mlp, w_up, w_down)
+
+
+def pack_tokens(dims, extra, tokens, key_bias):
+    c_size, cells, d = tokens.shape
+    return pl.pallas_call(
+        functools.partial(pack_tokens_kernel, dims),
+        out_shape=jax.ShapeDtypeStruct((c_size, cells + extra, d), BF),
+        compiler_params=pltpu.CompilerParams(vmem_limit_bytes=VMEM_LIMIT),
+        name="pack_tokens",
+    )(tokens, key_bias)
+
+
+def pack_cotangent(dims, cotangent, key_bias):
+    r_size, hl, cpd, length, d = dims
+    rows = hl * cpd + cpd + -cpd % 8
+    return pl.pallas_call(
+        functools.partial(pack_cotangent_kernel, dims),
+        out_shape=[jax.ShapeDtypeStruct((rows, d), BF)] * r_size,
+        compiler_params=pltpu.CompilerParams(vmem_limit_bytes=VMEM_LIMIT),
+        name="pack_cotangent",
+    )(cotangent, key_bias)
+
+
+def weight_grads(scale, half, steps, pairs):
+    d = pairs[1][0].shape[1]
+    flat = [x for pair in pairs for x in pair]
+    part = flat[0].shape[0] // steps
+    return pl.pallas_call(
+        functools.partial(weight_grad_kernel, scale),
+        grid=(steps,),
+        in_specs=[pl.BlockSpec((part, x.shape[1]), lambda i: (i, 0)) for x in flat],
+        out_specs=[whole((half, d))] * 2,
+        out_shape=[jax.ShapeDtypeStruct((half, d), BF)] * 2,
+        scratch_shapes=[pltpu.VMEM((left.shape[1], right.shape[1]), F32) for left, right in pairs],
+        compiler_params=params(),
+        name="weight_grads",
+    )(*flat)
+
+
+def unpack(dims, own, got, shapes):
+    return pl.pallas_call(
+        functools.partial(unpack_kernel, dims),
+        out_shape=[jax.ShapeDtypeStruct(shape, F32) for shape in shapes],
+        compiler_params=pltpu.CompilerParams(vmem_limit_bytes=VMEM_LIMIT),
+        name="unpack",
+    )(own, got)
 
 
 def exchange(x, axes):
     return lax.all_to_all(x, axes, split_axis=0, concat_axis=0, tiled=True)
 
 
-def wgrad(left, right, factor):
-    left = left.reshape(-1, left.shape[-1])
-    right = right.reshape(-1, right.shape[-1])
-    return (dot_tn(left, right) * factor).astype(BF)
-
-
-def total_of(rows, r_size, c_size):
-    m, d = rows.shape
-    part = exchange(rows, "rows").reshape(r_size, m // r_size, d)
-    part = jnp.sum(part.astype(F32), axis=0).astype(BF)
-    part = exchange(part, "cols").reshape(c_size, m // r_size // c_size, d)
-    part = jnp.sum(part.astype(F32), axis=0).astype(BF)
-    part = lax.all_gather(part, "cols", axis=0, tiled=True)
-    return lax.all_gather(part, "rows", axis=0, tiled=True)
-
-
-def wide(grad, d):
-    return [grad[:, i * d : (i + 1) * d] for i in range(grad.shape[1] // d)]
-
-
-def narrow(rows, count, d):
-    return jnp.concatenate([rows[i * d : (i + 1) * d] for i in range(count)], axis=1).astype(F32)
+def swap(x, axis, step):
+    size = lax.axis_size(axis)
+    return lax.ppermute(x, axis, [(i, i ^ step) for i in range(size)])
+
+
+def add(parts):
+    total = parts[0].astype(F32)
+    for part in parts[1:]:
+        total = total + part.astype(F32)
+    return total.astype(BF)
+
+
+def scatter_sum(blocks, axis, at, unit):
+    n = blocks.shape[0]
+    parts = [lax.dynamic_index_in_dim(blocks, at, 0, keepdims=False)]
+    for s in range(1, n):
+        block = lax.dynamic_index_in_dim(blocks, jnp.bitwise_xor(at, s), 0, keepdims=False)
+        parts.append(swap(block, axis, s * unit))
+    return add(parts)
+
+
+def gather(block, axis, n, unit):
+    return jnp.stack([block] + [swap(block, axis, s * unit) for s in range(1, n)])
+
+
+def padded(rows, unit):
+    return rows + -rows % unit
 
 
 def shards(
@@ -412,69 +631,73 @@
     ff = w_up.shape[1]
     rpd, cpd = hl // c_size, wl // r_size
     row_len, col_len = wl * c_size, hl * r_size
-    factor = float(row_len * col_len) ** (-0.5)
+    scale = float(row_len * col_len) ** (-0.5)
     r_at, c_at = lax.axis_index("rows"), lax.axis_index("cols")
+    z_size, z_at = c_size // 2, lax.axis_index("cols") // 2
     row_dims = (r_size, c_size, wl, cpd, row_len, d)
     chunk = min(cpd, max(1, 512 // col_len))
     col_dims = (r_size, hl, cpd, col_len, d, chunk)
-
-    place = jnp.arange(c_size)[None, :, None] == c_at
-    row_extra = jnp.where(place, key_bias[:, None, :], jnp.zeros((), BF))
-    row_extra = row_extra.reshape(c_size, rpd * row_len // d, d)
-    pad = -row_extra.shape[1] % 8
-    row_extra = jnp.pad(row_extra, ((0, 0), (0, pad), (0, 0)))
-    send = jnp.concatenate([tokens.reshape(c_size, rpd * wl, d), row_extra], axis=1)
-    recv = exchange(send, "cols")
-
-    col_bias = key_bias.T.reshape(r_size, cpd, 1, hl)
-    place = jnp.arange(r_size)[None, None, :, None] == r_at
-    col_extra = jnp.where(place, col_bias, jnp.zeros((), BF)).reshape(r_size, cpd, col_len)
-    col_extra = jnp.pad(col_extra, ((0, 0), (0, -cpd % 8), (0, d - col_len)))
-    ct_send = jnp.moveaxis(cotangent.reshape(hl, r_size, cpd, d), 1, 0)
-    ct_send = jnp.concatenate([ct_send.reshape(r_size, hl * cpd, d), col_extra], axis=1)
-    ct_wire = exchange(ct_send, "rows")
-
-    y_send, h1, qkv1, o1, p1 = row_forward(
-        row_dims, rpd, recv, gain_row[None], w_qkv_row, w_out_row
-    )
+    unit = 8 * 2 * r_size * z_size
+    col_half = padded(3 * d + d + 2 * ff, unit) // 2
+    row_half = padded(4 * d + 8, unit) // 2
+
+    extra = padded(rpd * row_len // d, 8)
+    recv = exchange(
+        pack_tokens(row_dims, extra, tokens.reshape(c_size, rpd * wl, d), key_bias), "cols"
+    )
+    ct_blocks = pack_cotangent(col_dims[:5], cotangent, key_bias)
+    ct_blocks = [ct_blocks[0]] + [swap(ct_blocks[s], "rows", s) for s in range(1, r_size)]
+
+    y_send, qkv1, o1, p1 = row_forward(row_dims, rpd, recv, gain_row[None], w_qkv_row, w_out_row)
     y_wire = exchange(y_send, ALL).reshape(hl * r_size * cpd, d)
     (dy_send, h2, dqkv2, o2, dy2, h3, du, act, ct_cols, dg_col, dg_mlp) = column_stage(
-        col_dims, y_wire, ct_wire, gain_col[None], w_qkv_col, w_out_col,
+        col_dims, y_wire, ct_blocks, gain_col[None], w_qkv_col, w_out_col,
         gain_mlp[None], w_up, w_down,
     )
     dy_wire = exchange(dy_send.reshape(y_send.shape), ALL)
 
-    col_parts = wide(wgrad(h2, dqkv2, factor), d)
-    col_parts += [wgrad(o2, dy2, factor)]
-    col_parts += wide(wgrad(h3, du, factor), d)
-    col_parts += [wgrad(act, ct_cols, factor)]
-    col_sums = total_of(jnp.concatenate(col_parts, axis=0), r_size, c_size)
-
-    dt_send, dy_rows, dqkv1, dg_row = row_backward(
-        row_dims, rpd, recv, dy_wire, qkv1, p1, gain_row[None], w_qkv_row, w_out_row
-    )
-    gains = (jnp.concatenate([dg_row, dg_col, dg_mlp], axis=0) * factor).astype(BF)
-    row_parts = wide(wgrad(h1, dqkv1, factor), d)
-    row_parts += [wgrad(o1, dy_rows, factor)]
-    unit = 8 * r_size * c_size
-    rows = 4 * d + 3
-    row_parts += [jnp.pad(gains, ((0, -rows % unit), (0, 0)))]
-    row_sums = total_of(jnp.concatenate(row_parts, axis=0), r_size, c_size)
+    keep, send = weight_grads(
+        scale, col_half, 4, ((h2, dqkv2), (o2, dy2), (h3, du), (act, ct_cols))
+    )
+    col_sum = add([keep, swap(send, "cols", 1)])
+    col_sum = scatter_sum(col_sum.reshape(r_size, -1, d), "rows", r_at, 1)
+
+    dt_send, keep, send = row_backward(
+        row_dims, rpd, row_half, recv, dy_wire, qkv1, o1, p1, gain_row[None], w_qkv_row,
+        w_out_row, dg_col, dg_mlp,
+    )
     d_tokens = exchange(dt_send, "cols").reshape(hl, wl, d)
-
-    gain_sums = row_sums[4 * d : 4 * d + 3].astype(F32)
+    row_sum = add([keep, swap(send, "cols", 1)])
+    row_sum = scatter_sum(row_sum.reshape(r_size, -1, d), "rows", r_at, 1)
+    both = jnp.concatenate(
+        [col_sum.reshape(z_size, -1, d), row_sum.reshape(z_size, -1, d)], axis=1
+    )
+    both = scatter_sum(both, "cols", z_at, 2)
+    both = gather(both, "cols", z_size, 2)
+    both = gather(both, "rows", r_size, 1)
+    other = swap(both, "cols", 1)
+
     nff = ff // d
+    col_layout = [(i * d, (i + 1) * d, 4, 0, i * d) for i in range(3)]
+    col_layout += [(3 * d, 4 * d, 5, 0, 0)]
+    col_layout += [((4 + i) * d, (5 + i) * d, 7, 0, i * d) for i in range(nff)]
+    col_layout += [((4 + nff) * d, (4 + nff) * d + ff, 8, 0, 0)]
+    row_layout = [(i * d, (i + 1) * d, 1, 0, i * d) for i in range(3)]
+    row_layout += [(3 * d, 4 * d, 2, 0, 0), (4 * d, 4 * d + 8, 0, 0, 0)]
+    shapes = [
+        (8, d), (d, 3 * d), (d, d), (8, d), (d, 3 * d), (d, d), (8, d), (d, ff), (ff, d),
+    ]
+    shapes = [s for i, s in enumerate(shapes) if i not in (3, 6)]
+    index = {0: 0, 1: 1, 2: 2, 4: 3, 5: 4, 7: 5, 8: 6}
+    layout = tuple(
+        tuple((a, b, index[w], r, l) for a, b, w, r, l in part)
+        for part in (col_layout, row_layout)
+    )
+    dims = (r_size, z_size, 2 * col_half // (2 * r_size * z_size),
+            2 * row_half // (2 * r_size * z_size), d, layout)
+    gains, qkv_row, out_row, qkv_col, out_col, up, down = unpack(dims, both, other, shapes)
     return (
-        d_tokens,
-        gain_sums[0],
-        narrow(row_sums, 3, d),
-        row_sums[3 * d : 4 * d].astype(F32),
-        gain_sums[1],
-        narrow(col_sums, 3, d),
-        col_sums[3 * d : 4 * d].astype(F32),
-        gain_sums[2],
-        narrow(col_sums[4 * d :], nff, d),
-        col_sums[(4 + nff) * d :].astype(F32),
+        d_tokens, gains[0], qkv_row, out_row, gains[1], qkv_col, out_col, gains[2], up, down,
     )
 
 

time: 244 us -> 175 us (0.72)
  blocking collectives: 95.2 us -> 41.2 us
  Pallas kernels: 34.3 us -> 49.9 us
  between operations: 14.4 us -> 0.8 us
  other arithmetic: 12.6 us -> 0.71 us
  matrix products: 9.12 us -> 0 us
  starting transfers between devices: 23.4 us -> 29.7 us
  local copies, waits for them, and re-layouts: 8.38 us -> 5.65 us
    all_gather x3 -> x0, blocking collectives: 48 us -> none  [the longest x2 37.2 us: total_of(): part = lax.all_gather(part, 'cols', axis=0, tiled=True)]
    ppermute x0 -> x21, waiting for transfers between devices: none -> 35.6 us  [swap(): return lax.ppermute(x, axis, [(i, i ^ step) for i in range(size)])]
    all_to_all x6 -> x2, waiting for transfers between devices: 45.3 us -> 10.5 us  [exchange(): return lax.all_to_all(x, axes, split_axis=0, concat_axis=0, tiled=True)]
    ppermute x0 -> x21, starting transfers between devices: none -> 23 us  [swap(): return lax.ppermute(x, axis, [(i, i ^ step) for i in range(size)])]
    all_to_all x6 -> x2, starting transfers between devices: 23.3 us -> 6.73 us  [exchange(): return lax.all_to_all(x, axes, split_axis=0, concat_axis=0, tiled=True)]
    pallas_call x0 -> x4, Pallas kernels: none -> 15.2 us  [the longest x1 6.64 us: weight_grads(): pl.pallas_call(functools.partial(weight_grad_kernel, scale), grid=(steps,...]
    dot_general x6 -> x0, matrix products: 9.12 us -> none  [dot_tn(): lax.dot_general(a, b, (((0,), (0,)), ((), ())), preferred_element_type=F32)]
    convert_element_type x7 -> x5, other arithmetic: 6.54 us -> 0.49 us  [add(): return total.astype(BF)]
  transfers between devices with their start and end apart: 7 -> 23, of which waited for: 5 -> 16; matrix products, arithmetic and copies ran while one was open for 6% -> 0% of each run, Pallas kernels for 6% -> 10%
where the time goes in v2:
time: 175 us; the launch traced here: 174 us
  Pallas kernels  49.9 us (29%)
  waiting for transfers between devices  46.2 us (26%)
  blocking collectives  41.2 us (24%)
  starting transfers between devices  29.7 us (17%)
  local copies, waits for them, and re-layouts  5.65 us (3%)
    all_to_all x2, blocking collectives, exchange(): return lax.all_to_all(x, axes, split_axis=0, concat_axis=0, tiled=True)  41.2 us
    ppermute x21, waiting for transfers between devices, swap(): return lax.ppermute(x, axis, [(i, i ^ step) for i in range(size)])  35.6 us
    ppermute x21, starting transfers between devices, swap(): return lax.ppermute(x, axis, [(i, i ^ step) for i in range(size)])  23 us
    pallas_call x1, Pallas kernels, column_stage(): pl.pallas_call(functools.partial(column_kernel, dims), grid=(cpd // chunk...  18.7 us
    all_to_all x2, waiting for transfers between devices, exchange(): return lax.all_to_all(x, axes, split_axis=0, concat_axis=0, tiled=True)  10.5 us
    pallas_call x1, Pallas kernels, row_backward(): pl.pallas_call(functools.partial(row_backward_kernel, dims), grid=(rpd,),...  8.5 us
    pallas_call x1, Pallas kernels, row_forward(): pl.pallas_call(functools.partial(row_forward_kernel, dims), grid=(rpd,),...  7.52 us
    all_to_all x2, starting transfers between devices, exchange(): return lax.all_to_all(x, axes, split_axis=0, concat_axis=0, tiled=True)  6.73 us
  transfers between devices with their start and end apart: 23, of which 16 were waited for; matrix products, arithmetic and copies ran while one was open for 0% of the time, Pallas kernels for 10%

profile of v2, /device:TPU:0, one launch (start us, length us, event | category | flops | bytes accessed | tf_op | source)
XLA Modules:
  0.0 174.1 jit_solution(16866843486051377403)
XLA Ops:
  0.6 2.0 %pack_tokens.1 = bf16[8,136,256]{2,1,0:T(8,128)(2,1)} custom-call(bf16[8,128,256]{2,1,0:T(8,128)(2,1)} %bitcast.62, bf16[32,32]{1,0:T(8,128)(2,1)} %b_ref.3), custom_call_target="tpu_custom_call" | custom-call | tf_op jit(solution)/shard_map/pack_tokens/pallas_call | solution.py:548
  2.6 22.5 %all_to_all.20.x_ref.b_ref = bf16[8,136,256]{2,1,0:T(8,128)(2,1)} all-to-all(bf16[8,136,256]{2,1,0:T(8,128)(2,1)} %pack_tokens.1), channel_id=1, replica_groups=mesh['rows'=4,'cols'=8] {'cols'}, dimensions={0} | all-to-all | bytes 1114112 | tf_op jit(solution)/shard_map/all_to_all | solution.py:593
  25.1 7.5 %row_forward.1 = (bf16[32,4,8,256]{3,2,1,0:T(8,128)(2,1)}, bf16[4,256,768]{2,1,0:T(8,128)(2,1)}, bf16[4,256,256]{2,1,0:T(8,128)(2,1)}, bf16[4,4,256,256]{3,2,1,0:T(8,128)(2,1)}) custom-call(bf16[8,136,256]{2,1,0:T(8,128)(2,1)} %all_to_all.20.x_ref.b_ref, bf16[8,136,256]{2,1,0:T(8,128)(2,1)} %all_to_all.20.x_ref.b_ref, f32[1,256]{1,0:T(1,128)} %bitcast.71, ...), custom_call_target="tpu_custom_call" | custom-call | tf_op jit(solution)/shard_map/row_forward/pallas_call | solution.py:439
  32.6 3.5 %all-to-all-start.1 = ((bf16[32,4,8,256]{3,2,1,0:T(8,128)(2,1)}), bf16[32,4,8,256]{3,2,1,0:T(8,128)(2,1)S(1)}, u32[]{:S(2)}, u32[]{:S(2)}) async-start(bf16[32,4,8,256]{3,2,1,0:T(8,128)(2,1)} %get-tuple-element.41), calls=%async_computation.1 | async-start | bytes 1048576 | tf_op jit(solution)/shard_map/all_to_all | solution.py:593
  36.1 2.1 %pack_cotangent.1 = (bf16[264,256]{1,0:T(8,128)(2,1)}, bf16[264,256]{1,0:T(8,128)(2,1)}, bf16[264,256]{1,0:T(8,128)(2,1)}, bf16[264,256]{1,0:T(8,128)(2,1)}) custom-call(bf16[32,32,256]{2,1,0:T(8,128)(2,1)} %ct_ref.1, bf16[32,32]{1,0:T(8,128)(2,1)} %b_ref.3), custom_call_target="tpu_custom_call" | custom-call | tf_op jit(solution)/shard_map/pack_cotangent/pallas_call | solution.py:559
  38.2 1.8 %collective-permute-start = (bf16[264,256]{1,0:T(8,128)(2,1)}, bf16[264,256]{1,0:T(8,128)(2,1)S(1)}, u32[]{:S(2)}, u32[]{:S(2)}) collective-permute-start(bf16[264,256]{1,0:T(8,128)(2,1)} %get-tuple-element.43), channel_id=1, source_target_pairs={{0,8},{8,0},{16,24},{24,16},{1,9},{9,1},{17,25},{25,17},{2,10},{10... | collective-permute-start | bytes 405512 | tf_op jit(solution)/shard_map/ppermute | solution.py:598
  40.0 1.5 collective-permute-start.1
  41.7 4.6 %collective-permute-done.refs_2_ = bf16[264,256]{1,0:T(8,128)(2,1)S(1)} collective-permute-done((bf16[264,256]{1,0:T(8,128)(2,1)}, bf16[264,256]{1,0:T(8,128)(2,1)S(1)}, u32[]{:S(2)}, u32[]{:S(2)}) %collective-permute-start) | collective-permute-done | bytes 135200 | tf_op jit(solution)/shard_map/ppermute | solution.py:598
  46.3 3.1 %collective-permute-done.1.refs_3_ = bf16[264,256]{1,0:T(8,128)(2,1)S(1)} collective-permute-done((bf16[264,256]{1,0:T(8,128)(2,1)}, bf16[264,256]{1,0:T(8,128)(2,1)S(1)}, u32[]{:S(2)}, u32[]{:S(2)}) %collective-permute-start.1) | collective-permute-done | bytes 135200 | tf_op jit(solution)/shard_map/ppermute | solution.py:598
  49.4 2.0 %collective-permute-done.2.refs_4_ = bf16[264,256]{1,0:T(8,128)(2,1)S(1)} collective-permute-done((bf16[264,256]{1,0:T(8,128)(2,1)}, bf16[264,256]{1,0:T(8,128)(2,1)S(1)}, u32[]{:S(2)}, u32[]{:S(2)}) %collective-permute-start.2) | collective-permute-done | bytes 135200 | tf_op jit(solution)/shard_map/ppermute | solution.py:598
  51.4 1.1 all-to-all-done.1
  52.5 0.8 copy-done.2
  53.3 18.7 %column_stage.1 = (bf16[1024,256]{1,0:T(8,128)(2,1)}, bf16[1024,256]{1,0:T(8,128)(2,1)}, bf16[1024,768]{1,0:T(8,128)(2,1)}, bf16[1024,256]{1,0:T(8,128)(2,1)}, b...) custom-call(bf16[1024,256]{1,0:T(8,128)(2,1)} %bitcast.55, ...), custom_call_target="tpu_custom_call" | custom-call | tf_op jit(solution)/shard_map/column_stage/pallas_call | solution.py:517
  72.0 3.2 %all-to-all-start.2 = ((bf16[32,4,8,256]{3,2,1,0:T(8,128)(2,1)}), bf16[32,4,8,256]{3,2,1,0:T(8,128)(2,1)S(1)}, u32[]{:S(2)}, u32[]{:S(2)}) async-start(bf16[32,4,8,256]{3,2,1,0:T(8,128)(2,1)} %bitcast.63), calls=%async_computation.2 | async-start | bytes 1048576 | tf_op jit(solution)/shard_map/all_to_all | solution.py:593
  75.2 6.6 %weight_grads.1 = (bf16[1536,256]{1,0:T(8,128)(2,1)}, bf16[1536,256]{1,0:T(8,128)(2,1)}) custom-call(bf16[1024,256]{1,0:T(8,128)(2,1)} %get-tuple-element.53.h2_ref, bf16[1024,768]{1,0:T(8,128)(2,1)} %get-tuple-element.54.dqkv_ref, bf16[1024,256]{1,0:T(8,128)(2,1)} %get-tuple-element.55.o2_ref, bf16[1024,256]{1,0:T(8,128)(2,1)} %get-tuple-element.56.dy2_ref, ...), custom_call_target="tpu_custom_call" | custom-call | tf_op jit(solution)/shard_map/weight_grads/pallas_call | solution.py:571
  81.9 9.5 %all-to-all-done.2.dy_ref = bf16[32,4,8,256]{3,2,1,0:T(8,128)(2,1)S(1)} async-done(((bf16[32,4,8,256]{3,2,1,0:T(8,128)(2,1)}), bf16[32,4,8,256]{3,2,1,0:T(8,128)(2,1)S(1)}, u32[]{:S(2)}, u32[]{:S(2)}) %all-to-all-start.2) | async-done | bytes 524320 | tf_op jit(solution)/shard_map/all_to_all | solution.py:593
  91.4 0.8 copy-done.1
  92.2 8.5 %row_backward.1 = (bf16[8,128,256]{2,1,0:T(8,128)(2,1)}, bf16[640,256]{1,0:T(8,128)(2,1)}, bf16[640,256]{1,0:T(8,128)(2,1)}) custom-call(bf16[8,136,256]{2,1,0:T(8,128)(2,1)} %all_to_all.20.x_ref.b_ref, bf16[32,4,8,256]{3,2,1,0:T(8,128)(2,1)} %copy-done.1, bf16[4,256,768]{2,1,0:T(8,128)(2,1)} %get-tuple-element.47.qkv_ref, ...), custom_call_target="tpu_custom_call" | custom-call | tf_op jit(solution)/shard_map/row_backward/pallas_call | solution.py:469
  101.1 0.9 collective-permute-start.4
  102.5 2.2 %collective-permute-start.6 = (bf16[384,256]{1,0:T(8,128)(2,1)S(1)}, bf16[384,256]{1,0:T(8,128)(2,1)S(1)}, u32[]{:S(2)}, u32[]{:S(2)}) collective-permute-start(bf16[384,256]{1,0:T(8,128)(2,1)S(1)} %get-tuple-element.73), channel_id=1, source_target_pairs={{0,24},{8,16},{16,8},{24,0},{1,25},{9,17},{17,9},{25,1},{2,26},{10... | collective-permute-start | bytes 589832 | tf_op jit(solution)/shard_map/ppermute | solution.py:598
  104.8 0.8 collective-permute-start.10
  105.6 1.5 collective-permute-start.8
  107.1 1.7 collective-permute-done.4
  108.8 0.9 collective-permute-start.9
  109.7 4.1 %collective-permute-done.5 = bf16[384,256]{1,0:T(8,128)(2,1)S(1)} collective-permute-done((bf16[384,256]{1,0:T(8,128)(2,1)S(1)}, bf16[384,256]{1,0:T(8,128)(2,1)S(1)}, u32[]{:S(2)}, u32[]{:S(2)}) %collective-permute-start.5) | collective-permute-done | bytes 196640 | tf_op jit(solution)/shard_map/ppermute | solution.py:598
  113.9 1.2 collective-permute-done.10
  115.2 1.0 collective-permute-done.8
  116.8 1.3 collective-permute-start.12
  118.1 2.7 %collective-permute-start.13 = (bf16[136,256]{1,0:T(8,128)(2,1)S(1)}, bf16[136,256]{1,0:T(8,128)(2,1)S(1)}, u32[]{:S(2)}, u32[]{:S(2)}) collective-permute-start(bf16[136,256]{1,0:T(8,128)(2,1)S(1)} %get-tuple-element.82), channel_id=1, source_target_pairs={{0,6},{1,7},{2,4},{3,5},{4,2},{5,3},{6,0},{7,1},{8,14},{9,15},{10,... | collective-permute-start | bytes 208904 | tf_op jit(solution)/shard_map/ppermute | solution.py:598
  120.8 0.7 collective-permute-done.11
  121.4 3.8 %collective-permute-done.12 = bf16[136,256]{1,0:T(8,128)(2,1)S(1)} collective-permute-done((bf16[136,256]{1,0:T(8,128)(2,1)S(1)}, bf16[136,256]{1,0:T(8,128)(2,1)S(1)}, u32[]{:S(2)}, u32[]{:S(2)}) %collective-permute-start.12) | collective-permute-done | bytes 69664 | tf_op jit(solution)/shard_map/ppermute | solution.py:598
  125.3 1.4 collective-permute-start.14
  126.7 0.9 collective-permute-start.15
  127.7 2.1 %collective-permute-start.16 = (bf16[136,256]{1,0:T(8,128)(2,1)S(1)}, bf16[136,256]{1,0:T(8,128)(2,1)S(1)}, u32[]{:S(2)}, u32[]{:S(2)}) collective-permute-start(bf16[136,256]{1,0:T(8,128)(2,1)S(1)} %fusion.8), channel_id=1, source_target_pairs={{0,6},{1,7},{2,4},{3,5},{4,2},{5,3},{6,0},{7,1},{8,14},{9,15},{10,... | collective-permute-start | bytes 208904 | tf_op jit(solution)/shard_map/ppermute | solution.py:598
  129.8 1.4 collective-permute-done.14
  131.1 1.7 collective-permute-done.15
  132.8 1.1 collective-permute-done.16
  133.9 1.6 collective-permute-start.17
  135.6 0.6 collective-permute-start.18
  136.2 1.3 collective-permute-start.19
  137.5 5.2 %collective-permute-done.17 = bf16[4,136,256]{2,1,0:T(8,128)(2,1)S(1)} collective-permute-done((bf16[4,136,256]{2,1,0:T(8,128)(2,1)S(1)}, bf16[4,136,256]{2,1,0:T(8,128)(2,1)S(1)}, u32[]{:S(2)}, u32[]{:S(2)}) %collective-permute-start.17) | collective-permute-done | bytes 278560 | tf_op jit(solution)/shard_map/ppermute | solution.py:598
  142.7 4.0 %collective-permute-done.18 = bf16[4,136,256]{2,1,0:T(8,128)(2,1)S(1)} collective-permute-done((bf16[4,136,256]{2,1,0:T(8,128)(2,1)S(1)}, bf16[4,136,256]{2,1,0:T(8,128)(2,1)S(1)}, u32[]{:S(2)}, u32[]{:S(2)}) %collective-permute-start.18) | collective-permute-done | bytes 278560 | tf_op jit(solution)/shard_map/ppermute | solution.py:598
  146.9 0.8 copy-done.5
  147.7 18.7 %all_to_all.21 = bf16[8,128,256]{2,1,0:T(8,128)(2,1)S(1)} all-to-all(bf16[8,128,256]{2,1,0:T(8,128)(2,1)S(1)} %copy-done.5), channel_id=1, replica_groups=mesh['rows'=4,'cols'=8] {'cols'}, dimensions={0} | all-to-all | bytes 1048576 | tf_op jit(solution)/shard_map/all_to_all | solution.py:593
  166.5 1.0 copy-done.3
  167.5 4.5 %unpack.1 = (f32[8,256]{1,0:T(8,128)}, f32[256,768]{1,0:T(8,128)}, f32[256,256]{1,0:T(8,128)}, f32[256,768]{1,0:T(8,128)}, f32[256,256]{1,0:T(8,128)}, /*index=5*/f32[256,1024]{1,0:T(8,128)}, f32[1024,256]{1,0:T(8,128)}) custom-call(bf16[4,4,136,256]{3,2,1,0:T(8,128)(2,1)} %copy-done, bf16[4,4,136,256]{3,2,1,0:T(8,128)(2,1)} %copy-done.3), custom_call_target="tpu_custom_call" | custom-call | tf_op jit(solution)/shard_map/unpack/pallas_call | solution.py:584
  171.9 1.4 fusion.18
  173.3 0.8 copy.23
  (39 shorter events, 2.3 us)
Async XLA Ops:
  32.6 19.9 %all-to-all-start.1 = ((bf16[32,4,8,256]{3,2,1,0:T(8,128)(2,1)}), bf16[32,4,8,256]{3,2,1,0:T(8,128)(2,1)S(1)}, u32[]{:S(2)}, u32[]{:S(2)}) async-start(bf16[32,4,8,256]{3,2,1,0:T(8,128)(2,1)} %get-tuple-element.41), calls=%async_computation.1 | async-start | bytes 1048576 | tf_op jit(solution)/shard_map/all_to_all | solution.py:593
  38.2 8.1 %collective-permute-start = (bf16[264,256]{1,0:T(8,128)(2,1)}, bf16[264,256]{1,0:T(8,128)(2,1)S(1)}, u32[]{:S(2)}, u32[]{:S(2)}) collective-permute-start(bf16[264,256]{1,0:T(8,128)(2,1)} %get-tuple-element.43), channel_id=1, source_target_pairs={{0,8},{8,0},{16,24},{24,16},{1,9},{9,1},{17,25},{25,17},{2,10},{10... | collective-permute-start | bytes 405512 | tf_op jit(solution)/shard_map/ppermute | solution.py:598
  40.0 9.4 %collective-permute-start.1 = (bf16[264,256]{1,0:T(8,128)(2,1)}, bf16[264,256]{1,0:T(8,128)(2,1)S(1)}, u32[]{:S(2)}, u32[]{:S(2)}) collective-permute-start(bf16[264,256]{1,0:T(8,128)(2,1)} %get-tuple-element.44), channel_id=1, source_target_pairs={{0,16},{8,24},{16,0},{24,8},{1,17},{9,25},{17,1},{25,9},{2,18},{10... | collective-permute-start | bytes 405512 | tf_op jit(solution)/shard_map/ppermute | solution.py:598
  41.5 9.9 %collective-permute-start.2 = (bf16[264,256]{1,0:T(8,128)(2,1)}, bf16[264,256]{1,0:T(8,128)(2,1)S(1)}, u32[]{:S(2)}, u32[]{:S(2)}) collective-permute-start(bf16[264,256]{1,0:T(8,128)(2,1)} %get-tuple-element.45), channel_id=1, source_target_pairs={{0,24},{8,16},{16,8},{24,0},{1,25},{9,17},{17,9},{25,1},{2,26},{10... | collective-permute-start | bytes 405512 | tf_op jit(solution)/shard_map/ppermute | solution.py:598
  46.3 6.2 %copy-start.7 = (bf16[264,256]{1,0:T(8,128)(2,1)}, bf16[264,256]{1,0:T(8,128)(2,1)S(1)}, u32[]{:S(2)}) copy-start(bf16[264,256]{1,0:T(8,128)(2,1)S(1)} %collective-permute-done.refs_2_) | copy-start | bytes 405508
  49.4 3.1 %copy-start.8 = (bf16[264,256]{1,0:T(8,128)(2,1)}, bf16[264,256]{1,0:T(8,128)(2,1)S(1)}, u32[]{:S(2)}) copy-start(bf16[264,256]{1,0:T(8,128)(2,1)S(1)} %collective-permute-done.1.refs_3_) | copy-start | bytes 405508
  51.4 1.1 copy-start.9
  52.5 0.8 copy-start.2
  72.0 19.4 %all-to-all-start.2 = ((bf16[32,4,8,256]{3,2,1,0:T(8,128)(2,1)}), bf16[32,4,8,256]{3,2,1,0:T(8,128)(2,1)S(1)}, u32[]{:S(2)}, u32[]{:S(2)}) async-start(bf16[32,4,8,256]{3,2,1,0:T(8,128)(2,1)} %bitcast.63), calls=%async_computation.2 | async-start | bytes 1048576 | tf_op jit(solution)/shard_map/all_to_all | solution.py:593
  81.9 18.9 %collective-permute-start.3 = (bf16[1536,256]{1,0:T(8,128)(2,1)}, bf16[1536,256]{1,0:T(8,128)(2,1)S(1)}, u32[]{:S(2)}, u32[]{:S(2)}) collective-permute-start(bf16[1536,256]{1,0:T(8,128)(2,1)} %get-tuple-element.62), channel_id=1, source_target_pairs={{0,1},{1,0},{2,3},{3,2},{4,5},{5,4},{6,7},{7,6},{8,9},{9,8},{10,11... | collective-permute-start | bytes 2359304 | tf_op jit(solution)/shard_map/ppermute | solution.py:598
  91.4 0.8 copy-start.1
  92.2 8.6 %copy-start.4 = (bf16[1536,256]{1,0:T(8,128)(2,1)S(1)}, bf16[1536,256]{1,0:T(8,128)(2,1)}, u32[]{:S(2)}) copy-start(bf16[1536,256]{1,0:T(8,128)(2,1)} %get-tuple-element.61) | copy-start | bytes 2359300
  100.7 4.0 %collective-permute-start.7 = (bf16[640,256]{1,0:T(8,128)(2,1)}, bf16[640,256]{1,0:T(8,128)(2,1)S(1)}, u32[]{:S(2)}, u32[]{:S(2)}) collective-permute-start(bf16[640,256]{1,0:T(8,128)(2,1)} %get-tuple-element.64), channel_id=1, source_target_pairs={{0,1},{1,0},{2,3},{3,2},{4,5},{5,4},{6,7},{7,6},{8,9},{9,8},{10,11... | collective-permute-start | bytes 983048 | tf_op jit(solution)/shard_map/ppermute | solution.py:598
  101.0 3.7 %copy-start.6 = (bf16[640,256]{1,0:T(8,128)(2,1)S(1)}, bf16[640,256]{1,0:T(8,128)(2,1)}, u32[]{:S(2)}) copy-start(bf16[640,256]{1,0:T(8,128)(2,1)} %get-tuple-element.63) | copy-start | bytes 983044
  101.1 7.8 %collective-permute-start.4 = (bf16[384,256]{1,0:T(8,128)(2,1)S(1)}, bf16[384,256]{1,0:T(8,128)(2,1)S(1)}, u32[]{:S(2)}, u32[]{:S(2)}) collective-permute-start(bf16[384,256]{1,0:T(8,128)(2,1)S(1)} %get-tuple-element.72), channel_id=1, source_target_pairs={{0,8},{8,0},{16,24},{24,16},{1,9},{9,1},{17,25},{25,17},{2,10},{10... | collective-permute-start | bytes 589832 | tf_op jit(solution)/shard_map/ppermute | solution.py:598
  102.0 11.9 %collective-permute-start.5 = (bf16[384,256]{1,0:T(8,128)(2,1)S(1)}, bf16[384,256]{1,0:T(8,128)(2,1)S(1)}, u32[]{:S(2)}, u32[]{:S(2)}) collective-permute-start(bf16[384,256]{1,0:T(8,128)(2,1)S(1)} %get-tuple-element.74), channel_id=1, source_target_pairs={{0,16},{8,24},{16,0},{24,8},{1,17},{9,25},{17,1},{25,9},{2,18},{10... | collective-permute-start | bytes 589832 | tf_op jit(solution)/shard_map/ppermute | solution.py:598
  102.5 11.3 %collective-permute-start.6 = (bf16[384,256]{1,0:T(8,128)(2,1)S(1)}, bf16[384,256]{1,0:T(8,128)(2,1)S(1)}, u32[]{:S(2)}, u32[]{:S(2)}) collective-permute-start(bf16[384,256]{1,0:T(8,128)(2,1)S(1)} %get-tuple-element.73), channel_id=1, source_target_pairs={{0,24},{8,16},{16,8},{24,0},{1,25},{9,17},{17,9},{25,1},{2,26},{10... | collective-permute-start | bytes 589832 | tf_op jit(solution)/shard_map/ppermute | solution.py:598
  104.8 10.4 %collective-permute-start.10 = (bf16[160,256]{1,0:T(8,128)(2,1)S(1)}, bf16[160,256]{1,0:T(8,128)(2,1)S(1)}, u32[]{:S(2)}, u32[]{:S(2)}) collective-permute-start(bf16[160,256]{1,0:T(8,128)(2,1)S(1)} %get-tuple-element.76), channel_id=1, source_target_pairs={{0,24},{8,16},{16,8},{24,0},{1,25},{9,17},{17,9},{25,1},{2,26},{10... | collective-permute-start | bytes 245768 | tf_op jit(solution)/shard_map/ppermute | solution.py:598
  105.6 10.6 %collective-permute-start.8 = (bf16[160,256]{1,0:T(8,128)(2,1)S(1)}, bf16[160,256]{1,0:T(8,128)(2,1)S(1)}, u32[]{:S(2)}, u32[]{:S(2)}) collective-permute-start(bf16[160,256]{1,0:T(8,128)(2,1)S(1)} %get-tuple-element.75), channel_id=1, source_target_pairs={{0,8},{8,0},{16,24},{24,16},{1,9},{9,1},{17,25},{25,17},{2,10},{10... | collective-permute-start | bytes 245768 | tf_op jit(solution)/shard_map/ppermute | solution.py:598
  108.8 7.4 %collective-permute-start.9 = (bf16[160,256]{1,0:T(8,128)(2,1)S(1)}, bf16[160,256]{1,0:T(8,128)(2,1)S(1)}, u32[]{:S(2)}, u32[]{:S(2)}) collective-permute-start(bf16[160,256]{1,0:T(8,128)(2,1)S(1)} %get-tuple-element.77), channel_id=1, source_target_pairs={{0,16},{8,24},{16,0},{24,8},{1,17},{9,25},{17,1},{25,9},{2,18},{10... | collective-permute-start | bytes 245768 | tf_op jit(solution)/shard_map/ppermute | solution.py:598
  116.3 5.1 %collective-permute-start.11 = (bf16[136,256]{1,0:T(8,128)(2,1)S(1)}, bf16[136,256]{1,0:T(8,128)(2,1)S(1)}, u32[]{:S(2)}, u32[]{:S(2)}) collective-permute-start(bf16[136,256]{1,0:T(8,128)(2,1)S(1)} %get-tuple-element.80), channel_id=1, source_target_pairs={{0,2},{1,3},{2,0},{3,1},{4,6},{5,7},{6,4},{7,5},{8,10},{9,11},{10,... | collective-permute-start | bytes 208904 | tf_op jit(solution)/shard_map/ppermute | solution.py:598
  116.8 8.5 %collective-permute-start.12 = (bf16[136,256]{1,0:T(8,128)(2,1)S(1)}, bf16[136,256]{1,0:T(8,128)(2,1)S(1)}, u32[]{:S(2)}, u32[]{:S(2)}) collective-permute-start(bf16[136,256]{1,0:T(8,128)(2,1)S(1)} %get-tuple-element.81), channel_id=1, source_target_pairs={{0,4},{1,5},{2,6},{3,7},{4,0},{5,1},{6,2},{7,3},{8,12},{9,13},{10,... | collective-permute-start | bytes 208904 | tf_op jit(solution)/shard_map/ppermute | solution.py:598
  118.1 7.2 %collective-permute-start.13 = (bf16[136,256]{1,0:T(8,128)(2,1)S(1)}, bf16[136,256]{1,0:T(8,128)(2,1)S(1)}, u32[]{:S(2)}, u32[]{:S(2)}) collective-permute-start(bf16[136,256]{1,0:T(8,128)(2,1)S(1)} %get-tuple-element.82), channel_id=1, source_target_pairs={{0,6},{1,7},{2,4},{3,5},{4,2},{5,3},{6,0},{7,1},{8,14},{9,15},{10,... | collective-permute-start | bytes 208904 | tf_op jit(solution)/shard_map/ppermute | solution.py:598
  125.3 5.8 %collective-permute-start.14 = (bf16[136,256]{1,0:T(8,128)(2,1)S(1)}, bf16[136,256]{1,0:T(8,128)(2,1)S(1)}, u32[]{:S(2)}, u32[]{:S(2)}) collective-permute-start(bf16[136,256]{1,0:T(8,128)(2,1)S(1)} %fusion.8), channel_id=1, source_target_pairs={{0,2},{1,3},{2,0},{3,1},{4,6},{5,7},{6,4},{7,5},{8,10},{9,11},{10,... | collective-permute-start | bytes 208904 | tf_op jit(solution)/shard_map/ppermute | solution.py:598
  126.7 6.1 %collective-permute-start.15 = (bf16[136,256]{1,0:T(8,128)(2,1)S(1)}, bf16[136,256]{1,0:T(8,128)(2,1)S(1)}, u32[]{:S(2)}, u32[]{:S(2)}) collective-permute-start(bf16[136,256]{1,0:T(8,128)(2,1)S(1)} %fusion.8), channel_id=1, source_target_pairs={{0,4},{1,5},{2,6},{3,7},{4,0},{5,1},{6,2},{7,3},{8,12},{9,13},{10,... | collective-permute-start | bytes 208904 | tf_op jit(solution)/shard_map/ppermute | solution.py:598
  127.7 6.2 %collective-permute-start.16 = (bf16[136,256]{1,0:T(8,128)(2,1)S(1)}, bf16[136,256]{1,0:T(8,128)(2,1)S(1)}, u32[]{:S(2)}, u32[]{:S(2)}) collective-permute-start(bf16[136,256]{1,0:T(8,128)(2,1)S(1)} %fusion.8), channel_id=1, source_target_pairs={{0,6},{1,7},{2,4},{3,5},{4,2},{5,3},{6,0},{7,1},{8,14},{9,15},{10,... | collective-permute-start | bytes 208904 | tf_op jit(solution)/shard_map/ppermute | solution.py:598
  133.9 8.7 %collective-permute-start.17 = (bf16[4,136,256]{2,1,0:T(8,128)(2,1)S(1)}, bf16[4,136,256]{2,1,0:T(8,128)(2,1)S(1)}, u32[]{:S(2)}, u32[]{:S(2)}) collective-permute-start(bf16[4,136,256]{2,1,0:T(8,128)(2,1)S(1)} %get-tuple-element.79), channel_id=1, source_target_pairs={{0,8},{8,0},{16,24},{24,16},{1,9},{9,1},{17,25},{25,17},{2,10},{10... | collective-permute-start | bytes 835592 | tf_op jit(solution)/shard_map/ppermute | solution.py:598
  135.6 11.1 %collective-permute-start.18 = (bf16[4,136,256]{2,1,0:T(8,128)(2,1)S(1)}, bf16[4,136,256]{2,1,0:T(8,128)(2,1)S(1)}, u32[]{:S(2)}, u32[]{:S(2)}) collective-permute-start(bf16[4,136,256]{2,1,0:T(8,128)(2,1)S(1)} %get-tuple-element.79), channel_id=1, source_target_pairs={{0,16},{8,24},{16,0},{24,8},{1,17},{9,25},{17,1},{25,9},{2,18},{10... | collective-permute-start | bytes 835592 | tf_op jit(solution)/shard_map/ppermute | solution.py:598
  136.2 10.5 %collective-permute-start.19 = (bf16[4,136,256]{2,1,0:T(8,128)(2,1)S(1)}, bf16[4,136,256]{2,1,0:T(8,128)(2,1)S(1)}, u32[]{:S(2)}, u32[]{:S(2)}) collective-permute-start(bf16[4,136,256]{2,1,0:T(8,128)(2,1)S(1)} %get-tuple-element.79), channel_id=1, source_target_pairs={{0,24},{8,16},{16,8},{24,0},{1,25},{9,17},{17,9},{25,1},{2,26},{10... | collective-permute-start | bytes 835592 | tf_op jit(solution)/shard_map/ppermute | solution.py:598
  146.7 1.0 copy-start.5
  146.8 19.6 %copy-start = (bf16[4,4,136,256]{3,2,1,0:T(8,128)(2,1)}, bf16[4,4,136,256]{3,2,1,0:T(8,128)(2,1)S(1)}, u32[]{:S(2)}) copy-start(bf16[4,4,136,256]{3,2,1,0:T(8,128)(2,1)S(1)} %pad_maximum_fusion.own_ref) | copy-start | bytes 3342340
  146.9 19.6 %collective-permute-start.20 = (bf16[4,4,136,256]{3,2,1,0:T(8,128)(2,1)S(1)}, bf16[4,4,136,256]{3,2,1,0:T(8,128)(2,1)S(1)}, u32[]{:S(2)}, u32[]{:S(2)}) collective-permute-start(bf16[4,4,136,256]{3,2,1,0:T(8,128)(2,1)S(1)} %pad_maximum_fusion.own_ref), channel_id=1, source_target_pairs={{0,1},{1,0},{2,3},{3,2},{4,5},{5,4},{6,7},{7,6},{8,9},{9,8},{10,11... | collective-permute-start | bytes 3342344 | tf_op jit(solution)/shard_map/ppermute | solution.py:598
  166.5 1.0 copy-start.3

commit v3 on v2

--- a/solution.py
+++ b/solution.py
@@ -239,43 +239,53 @@
                 out_refs[s][hl * cpd :] = rows.astype(BF)
 
 
-def weight_grad_kernel(
-    scale, h2_ref, dqkv_ref, o2_ref, dy2_ref, h3_ref, du_ref, act_ref, ct_ref,
-    keep_ref, send_ref, dwqkv_s, dwout_s, dwup_s, dwdown_s,
-):
+def weight_grad_kernel(scale, n_out, *refs):
+    ins, out_refs = refs[:8], refs[8 : 8 + n_out]
+    sums = refs[8 + n_out :]
     step, steps = pl.program_id(0), pl.num_programs(0)
-    sums = (
-        (dwqkv_s, h2_ref, dqkv_ref),
-        (dwout_s, o2_ref, dy2_ref),
-        (dwup_s, h3_ref, du_ref),
-        (dwdown_s, act_ref, ct_ref),
-    )
+    pairs = tuple(zip(sums, ins[::2], ins[1::2]))
 
     @pl.when(step == 0)
     def _():
-        for total, left, right in sums:
+        for total, left, right in pairs:
             total[...] = dot_tn(left[...], right[...])
 
     @pl.when(step != 0)
     def _():
-        for total, left, right in sums:
+        for total, left, right in pairs:
             total[...] += dot_tn(left[...], right[...])
 
     @pl.when(step == steps - 1)
     def _():
-        parity = lax.rem(lax.axis_index("cols"), 2)
-        d = dwout_s.shape[0]
-        row = 0
-        for total, _, _ in sums[:3]:
-            for i in range(total.shape[1] // d):
-                grad = (total[:, i * d : (i + 1) * d] * scale).astype(BF)
-                store_rows(keep_ref, send_ref, parity, row, grad)
-                row += d
-        store_rows(keep_ref, send_ref, parity, row, (dwdown_s[...] * scale).astype(BF))
-        row += dwdown_s.shape[0]
-        if row < 2 * keep_ref.shape[0]:
-            rest = jnp.zeros((2 * keep_ref.shape[0] - row, d), BF)
-            store_rows(keep_ref, send_ref, parity, row, rest)
+        r_at = lax.axis_index("rows")
+        d = sums[1].shape[0]
+        block = out_refs[0].shape[0]
+        sections = []
+        for total in sums[:3]:
+            sections += [(total, slice(0, d), slice(i, i + d)) for i in range(0, total.shape[1], d)]
+        sections += [(sums[3], slice(i, i + d), slice(0, d)) for i in range(0, sums[3].shape[0], d)]
+        for r in range(n_out):
+            for s in range(n_out):
+
+                @pl.when(jnp.bitwise_xor(r_at, s) == r)
+                def _():
+                    end = len(sections) * d
+                    for at in range(0, block, d):
+                        size = min(d, block - at)
+                        row = r * block + at
+                        while size > 0:
+                            if row < end:
+                                total, rows, lanes = sections[row // d]
+                                skip = row % d
+                                part = min(size, d - skip)
+                                rows = slice(rows.start + skip, rows.start + skip + part)
+                                piece = (total[rows, lanes] * scale).astype(BF)
+                            else:
+                                part = size
+                                piece = jnp.zeros((part, d), BF)
+                            to = row - r * block
+                            out_refs[s][to : to + part] = piece
+                            row, size = row + part, size - part
 
 
 def unpack_kernel(dims, own_ref, got_ref, *out_refs):
@@ -283,31 +293,38 @@
     r_at, c_at = lax.axis_index("rows"), lax.axis_index("cols")
     z_at, parity = lax.div(c_at, 2), lax.rem(c_at, 2)
     for core in range(2):
+        copies = []
         for r in range(r_size):
             for z in range(z_size):
-                at = (core * r_size + r) * z_size + z
-                s, t = jnp.bitwise_xor(r_at, r), jnp.bitwise_xor(z_at, z)
-                for base, size, sections in (
-                    (0, col_rows, layout[0]),
-                    (col_rows, row_rows, layout[1]),
+                for base, size, sections, at in (
+                    (0, col_rows, layout[0], (r * 2 + core) * z_size + z),
+                    (col_rows, row_rows, layout[1], (core * r_size + r) * z_size + z),
                 ):
                     first = at * size
                     for start, stop, which, row0, lane0 in sections:
                         low, high = max(first, start), min(first + size, stop)
-                        if low >= high:
-                            continue
-                        cut = slice(base + low - first, base + high - first)
-                        to = slice(row0 + low - start, row0 + high - start)
-                        lanes = slice(lane0, lane0 + d)
-                        out_ref = out_refs[which]
-
-                        @pl.when(parity == core)
-                        def _():
-                            out_ref[to, lanes] = own_ref[s, t, cut, :].astype(F32)
-
-                        @pl.when(parity != core)
-                        def _():
-                            out_ref[to, lanes] = got_ref[s, t, cut, :].astype(F32)
+                        if low < high:
+                            cut = slice(base + low - first, base + high - first)
+                            to = slice(row0 + low - start, row0 + high - start)
+                            copies.append((r, z, cut, which, to, slice(lane0, lane0 + d)))
+
+        def place(source):
+            for r, z, cut, which, to, lanes in copies:
+                s, t = jnp.bitwise_xor(r_at, r), jnp.bitwise_xor(z_at, z)
+                piece = source[s, t, cut, :].astype(F32)
+                if which < 0:
+                    for i in range(3):
+                        out_refs[i][...] = piece[i : i + 1]
+                else:
+                    out_refs[which][to, lanes] = piece
+
+        @pl.when(parity == core)
+        def _():
+            place(own_ref)
+
+        @pl.when(parity != core)
+        def _():
+            place(got_ref)
 
 
 def column_kernel(
@@ -564,16 +581,16 @@
     )(cotangent, key_bias)
 
 
-def weight_grads(scale, half, steps, pairs):
+def weight_grads(scale, n_out, rows, steps, pairs):
     d = pairs[1][0].shape[1]
     flat = [x for pair in pairs for x in pair]
     part = flat[0].shape[0] // steps
     return pl.pallas_call(
-        functools.partial(weight_grad_kernel, scale),
+        functools.partial(weight_grad_kernel, scale, n_out),
         grid=(steps,),
         in_specs=[pl.BlockSpec((part, x.shape[1]), lambda i: (i, 0)) for x in flat],
-        out_specs=[whole((half, d))] * 2,
-        out_shape=[jax.ShapeDtypeStruct((half, d), BF)] * 2,
+        out_specs=[whole((rows // n_out, d))] * n_out,
+        out_shape=[jax.ShapeDtypeStruct((rows // n_out, d), BF)] * n_out,
         scratch_shapes=[pltpu.VMEM((left.shape[1], right.shape[1]), F32) for left, right in pairs],
         compiler_params=params(),
         name="weight_grads",
@@ -656,11 +673,13 @@
     )
     dy_wire = exchange(dy_send.reshape(y_send.shape), ALL)
 
-    keep, send = weight_grads(
-        scale, col_half, 4, ((h2, dqkv2), (o2, dy2), (h3, du), (act, ct_cols))
-    )
-    col_sum = add([keep, swap(send, "cols", 1)])
-    col_sum = scatter_sum(col_sum.reshape(r_size, -1, d), "rows", r_at, 1)
+    col_blocks = weight_grads(
+        scale, r_size, 2 * col_half, 4, ((h2, dqkv2), (o2, dy2), (h3, du), (act, ct_cols))
+    )
+    col_sum = add(
+        [col_blocks[0]] + [swap(col_blocks[s], "rows", s) for s in range(1, r_size)]
+    )
+    col_sum = scatter_sum(col_sum.reshape(2, -1, d), "cols", c_at % 2, 1)
 
     dt_send, keep, send = row_backward(
         row_dims, rpd, row_half, recv, dy_wire, qkv1, o1, p1, gain_row[None], w_qkv_row,
@@ -674,30 +693,25 @@
     )
     both = scatter_sum(both, "cols", z_at, 2)
     both = gather(both, "cols", z_size, 2)
+    both, d_tokens = lax.optimization_barrier((both, d_tokens))
     both = gather(both, "rows", r_size, 1)
     other = swap(both, "cols", 1)
 
     nff = ff // d
-    col_layout = [(i * d, (i + 1) * d, 4, 0, i * d) for i in range(3)]
-    col_layout += [(3 * d, 4 * d, 5, 0, 0)]
+    col_layout = [(i * d, (i + 1) * d, 5, 0, i * d) for i in range(3)]
+    col_layout += [(3 * d, 4 * d, 6, 0, 0)]
     col_layout += [((4 + i) * d, (5 + i) * d, 7, 0, i * d) for i in range(nff)]
     col_layout += [((4 + nff) * d, (4 + nff) * d + ff, 8, 0, 0)]
-    row_layout = [(i * d, (i + 1) * d, 1, 0, i * d) for i in range(3)]
-    row_layout += [(3 * d, 4 * d, 2, 0, 0), (4 * d, 4 * d + 8, 0, 0, 0)]
-    shapes = [
-        (8, d), (d, 3 * d), (d, d), (8, d), (d, 3 * d), (d, d), (8, d), (d, ff), (ff, d),
-    ]
-    shapes = [s for i, s in enumerate(shapes) if i not in (3, 6)]
-    index = {0: 0, 1: 1, 2: 2, 4: 3, 5: 4, 7: 5, 8: 6}
-    layout = tuple(
-        tuple((a, b, index[w], r, l) for a, b, w, r, l in part)
-        for part in (col_layout, row_layout)
-    )
+    row_layout = [(i * d, (i + 1) * d, 3, 0, i * d) for i in range(3)]
+    row_layout += [(3 * d, 4 * d, 4, 0, 0), (4 * d, 4 * d + 8, -1, 0, 0)]
+    layout = (tuple(col_layout), tuple(row_layout))
+    shapes = [(1, d)] * 3 + [(d, 3 * d), (d, d), (d, 3 * d), (d, d), (d, ff), (ff, d)]
     dims = (r_size, z_size, 2 * col_half // (2 * r_size * z_size),
             2 * row_half // (2 * r_size * z_size), d, layout)
-    gains, qkv_row, out_row, qkv_col, out_col, up, down = unpack(dims, both, other, shapes)
+    outs = unpack(dims, both, other, shapes)
+    g_row, g_col, g_mlp, qkv_row, out_row, qkv_col, out_col, up, down = outs
     return (
-        d_tokens, gains[0], qkv_row, out_row, gains[1], qkv_col, out_col, gains[2], up, down,
+        d_tokens, g_row[0], qkv_row, out_row, g_col[0], qkv_col, out_col, g_mlp[0], up, down,
     )
 
 

time: 175 us -> 161 us (0.920)
  blocking collectives: 41.2 us -> 22.5 us
  starting transfers between devices: 29.7 us -> 33.8 us
  waiting for transfers between devices: 46.2 us -> 49.7 us
  local copies, waits for them, and re-layouts: 5.65 us -> 3.45 us
    all_to_all x2 -> x1, blocking collectives: 41.2 us -> 22.5 us  [exchange(): return lax.all_to_all(x, axes, split_axis=0, concat_axis=0, tiled=True)]
    ppermute x21, waiting for transfers between devices: 35.6 us -> 42.5 us  [swap(): return lax.ppermute(x, axis, [(i, i ^ step) for i in range(size)])]
    all_to_all x2 -> x3, starting transfers between devices: 6.73 us -> 10.6 us  [exchange(): return lax.all_to_all(x, axes, split_axis=0, concat_axis=0, tiled=True)]
    all_to_all x2 -> x3, waiting for transfers between devices: 10.5 us -> 7.18 us  [exchange(): return lax.all_to_all(x, axes, split_axis=0, concat_axis=0, tiled=True)]
    unnamed x21 -> x19, local copies, waits for them, and re-layouts: 4.19 us -> 3.4 us
  transfers between devices with their start and end apart: 23 -> 24, of which waited for: 16 -> 16; matrix products, arithmetic and copies ran while one was open for 0% -> 0% of each run, Pallas kernels for 10% -> 11%
where the time goes in v3:
time: 161 us; the launch traced here: 160 us
  waiting for transfers between devices  49.7 us (31%)
  Pallas kernels  49.3 us (31%)
  starting transfers between devices  33.8 us (21%)
  blocking collectives  22.5 us (14%)
  local copies, waits for them, and re-layouts  3.45 us (2%)
    ppermute x21, waiting for transfers between devices, swap(): return lax.ppermute(x, axis, [(i, i ^ step) for i in range(size)])  42.5 us
    ppermute x21, starting transfers between devices, swap(): return lax.ppermute(x, axis, [(i, i ^ step) for i in range(size)])  23.2 us
    all_to_all x1, blocking collectives, exchange(): return lax.all_to_all(x, axes, split_axis=0, concat_axis=0, tiled=True)  22.5 us
    pallas_call x1, Pallas kernels, column_stage(): pl.pallas_call(functools.partial(column_kernel, dims), grid=(cpd // chunk...  18.7 us
    all_to_all x3, starting transfers between devices, exchange(): return lax.all_to_all(x, axes, split_axis=0, concat_axis=0, tiled=True)  10.6 us
    pallas_call x1, Pallas kernels, row_backward(): pl.pallas_call(functools.partial(row_backward_kernel, dims), grid=(rpd,),...  8.45 us
    pallas_call x1, Pallas kernels, row_forward(): pl.pallas_call(functools.partial(row_forward_kernel, dims), grid=(rpd,),...  7.52 us
    all_to_all x3, waiting for transfers between devices, exchange(): return lax.all_to_all(x, axes, split_axis=0, concat_axis=0, tiled=True)  7.18 us
  transfers between devices with their start and end apart: 24, of which 16 were waited for; matrix products, arithmetic and copies ran while one was open for 0% of the time, Pallas kernels for 11%

profile of v3, /device:TPU:0, one launch (start us, length us, event | category | flops | bytes accessed | tf_op | source)
XLA Modules:
  0.0 160.2 jit_solution(3661841592332905528)
XLA Ops:
  0.6 2.0 %pack_tokens.1 = bf16[8,136,256]{2,1,0:T(8,128)(2,1)} custom-call(bf16[8,128,256]{2,1,0:T(8,128)(2,1)} %bitcast.58, bf16[32,32]{1,0:T(8,128)(2,1)} %b_ref.3), custom_call_target="tpu_custom_call" | custom-call | tf_op jit(solution)/shard_map/pack_tokens/pallas_call | solution.py:565
  2.6 22.5 %all_to_all.20.x_ref.b_ref = bf16[8,136,256]{2,1,0:T(8,128)(2,1)} all-to-all(bf16[8,136,256]{2,1,0:T(8,128)(2,1)} %pack_tokens.1), channel_id=1, replica_groups=mesh['rows'=4,'cols'=8] {'cols'}, dimensions={0} | all-to-all | bytes 1114112 | tf_op jit(solution)/shard_map/all_to_all | solution.py:610
  25.1 7.5 %row_forward.1 = (bf16[32,4,8,256]{3,2,1,0:T(8,128)(2,1)}, bf16[4,256,768]{2,1,0:T(8,128)(2,1)}, bf16[4,256,256]{2,1,0:T(8,128)(2,1)}, bf16[4,4,256,256]{3,2,1,0:T(8,128)(2,1)}) custom-call(bf16[8,136,256]{2,1,0:T(8,128)(2,1)} %all_to_all.20.x_ref.b_ref, bf16[8,136,256]{2,1,0:T(8,128)(2,1)} %all_to_all.20.x_ref.b_ref, f32[1,256]{1,0:T(1,128)} %bitcast.67, ...), custom_call_target="tpu_custom_call" | custom-call | tf_op jit(solution)/shard_map/row_forward/pallas_call | solution.py:456
  32.6 3.5 %all-to-all-start.1 = ((bf16[32,4,8,256]{3,2,1,0:T(8,128)(2,1)}), bf16[32,4,8,256]{3,2,1,0:T(8,128)(2,1)S(1)}, u32[]{:S(2)}, u32[]{:S(2)}) async-start(bf16[32,4,8,256]{3,2,1,0:T(8,128)(2,1)} %get-tuple-element.47), calls=%async_computation.1 | async-start | bytes 1048576 | tf_op jit(solution)/shard_map/all_to_all | solution.py:610
  36.1 2.1 %pack_cotangent.1 = (bf16[264,256]{1,0:T(8,128)(2,1)}, bf16[264,256]{1,0:T(8,128)(2,1)}, bf16[264,256]{1,0:T(8,128)(2,1)}, bf16[264,256]{1,0:T(8,128)(2,1)}) custom-call(bf16[32,32,256]{2,1,0:T(8,128)(2,1)} %ct_ref.1, bf16[32,32]{1,0:T(8,128)(2,1)} %b_ref.3), custom_call_target="tpu_custom_call" | custom-call | tf_op jit(solution)/shard_map/pack_cotangent/pallas_call | solution.py:576
  38.2 1.8 %collective-permute-start = (bf16[264,256]{1,0:T(8,128)(2,1)}, bf16[264,256]{1,0:T(8,128)(2,1)S(1)}, u32[]{:S(2)}, u32[]{:S(2)}) collective-permute-start(bf16[264,256]{1,0:T(8,128)(2,1)} %get-tuple-element.49), channel_id=1, source_target_pairs={{0,8},{8,0},{16,24},{24,16},{1,9},{9,1},{17,25},{25,17},{2,10},{10... | collective-permute-start | bytes 405512 | tf_op jit(solution)/shard_map/ppermute | solution.py:615
  40.0 1.5 collective-permute-start.1
  41.5 0.2 collective-permute-start.2
  41.7 4.6 %collective-permute-done.refs_2_ = bf16[264,256]{1,0:T(8,128)(2,1)S(1)} collective-permute-done((bf16[264,256]{1,0:T(8,128)(2,1)}, bf16[264,256]{1,0:T(8,128)(2,1)S(1)}, u32[]{:S(2)}, u32[]{:S(2)}) %collective-permute-start) | collective-permute-done | bytes 135200 | tf_op jit(solution)/shard_map/ppermute | solution.py:615
  46.3 3.1 %collective-permute-done.1.refs_3_ = bf16[264,256]{1,0:T(8,128)(2,1)S(1)} collective-permute-done((bf16[264,256]{1,0:T(8,128)(2,1)}, bf16[264,256]{1,0:T(8,128)(2,1)S(1)}, u32[]{:S(2)}, u32[]{:S(2)}) %collective-permute-start.1) | collective-permute-done | bytes 135200 | tf_op jit(solution)/shard_map/ppermute | solution.py:615
  49.4 2.0 %collective-permute-done.2.refs_4_ = bf16[264,256]{1,0:T(8,128)(2,1)S(1)} collective-permute-done((bf16[264,256]{1,0:T(8,128)(2,1)}, bf16[264,256]{1,0:T(8,128)(2,1)S(1)}, u32[]{:S(2)}, u32[]{:S(2)}) %collective-permute-start.2) | collective-permute-done | bytes 135200 | tf_op jit(solution)/shard_map/ppermute | solution.py:615
  51.4 1.1 all-to-all-done.1
  52.5 0.8 copy-done.2
  53.3 18.7 %column_stage.1 = (bf16[1024,256]{1,0:T(8,128)(2,1)}, bf16[1024,256]{1,0:T(8,128)(2,1)}, bf16[1024,768]{1,0:T(8,128)(2,1)}, bf16[1024,256]{1,0:T(8,128)(2,1)}, b...) custom-call(bf16[1024,256]{1,0:T(8,128)(2,1)} %bitcast.48, ...), custom_call_target="tpu_custom_call" | custom-call | tf_op jit(solution)/shard_map/column_stage/pallas_call | solution.py:534
  72.0 3.2 %all-to-all-start.2 = ((bf16[32,4,8,256]{3,2,1,0:T(8,128)(2,1)}), bf16[32,4,8,256]{3,2,1,0:T(8,128)(2,1)S(1)}, u32[]{:S(2)}, u32[]{:S(2)}) async-start(bf16[32,4,8,256]{3,2,1,0:T(8,128)(2,1)} %bitcast.59), calls=%async_computation.2 | async-start | bytes 1048576 | tf_op jit(solution)/shard_map/all_to_all | solution.py:610
  75.2 6.7 %weight_grads.1 = (bf16[768,256]{1,0:T(8,128)(2,1)}, bf16[768,256]{1,0:T(8,128)(2,1)}, bf16[768,256]{1,0:T(8,128)(2,1)}, bf16[768,256]{1,0:T(8,128)(2,1)}) custom-call(bf16[1024,256]{1,0:T(8,128)(2,1)} %get-tuple-element.52.refs_0_, bf16[1024,768]{1,0:T(8,128)(2,1)} %get-tuple-element.53.refs_1_, bf16[1024,256]{1,0:T(8,128)(2,1)} %get-tuple-element.54.refs_2_, ...), custom_call_target="tpu_custom_call" | custom-call | tf_op jit(solution)/shard_map/weight_grads/pallas_call | solution.py:588
  81.9 1.6 collective-permute-start.3
  83.5 1.5 collective-permute-start.4
  84.9 0.4 collective-permute-start.5
  85.4 6.1 %all-to-all-done.2.dy_ref = bf16[32,4,8,256]{3,2,1,0:T(8,128)(2,1)S(1)} async-done(((bf16[32,4,8,256]{3,2,1,0:T(8,128)(2,1)}), bf16[32,4,8,256]{3,2,1,0:T(8,128)(2,1)S(1)}, u32[]{:S(2)}, u32[]{:S(2)}) %all-to-all-start.2) | async-done | bytes 524320 | tf_op jit(solution)/shard_map/all_to_all | solution.py:610
  91.5 0.8 copy-done.1
  92.3 8.4 %row_backward.1 = (bf16[8,128,256]{2,1,0:T(8,128)(2,1)}, bf16[640,256]{1,0:T(8,128)(2,1)}, bf16[640,256]{1,0:T(8,128)(2,1)}) custom-call(bf16[8,136,256]{2,1,0:T(8,128)(2,1)} %all_to_all.20.x_ref.b_ref, bf16[32,4,8,256]{3,2,1,0:T(8,128)(2,1)} %copy-done.1, bf16[4,256,768]{2,1,0:T(8,128)(2,1)} %get-tuple-element.65.qkv_ref, ...), custom_call_target="tpu_custom_call" | custom-call | tf_op jit(solution)/shard_map/row_backward/pallas_call | solution.py:486
  100.8 2.0 %collective-permute-done.4 = bf16[768,256]{1,0:T(8,128)(2,1)S(1)} collective-permute-done((bf16[768,256]{1,0:T(8,128)(2,1)}, bf16[768,256]{1,0:T(8,128)(2,1)S(1)}, u32[]{:S(2)}, u32[]{:S(2)}) %collective-permute-start.4) | collective-permute-done | bytes 393248 | tf_op jit(solution)/shard_map/ppermute | solution.py:615
  102.8 1.7 %collective-permute-done.5 = bf16[768,256]{1,0:T(8,128)(2,1)S(1)} collective-permute-done((bf16[768,256]{1,0:T(8,128)(2,1)}, bf16[768,256]{1,0:T(8,128)(2,1)S(1)}, u32[]{:S(2)}, u32[]{:S(2)}) %collective-permute-start.5) | collective-permute-done | bytes 393248 | tf_op jit(solution)/shard_map/ppermute | solution.py:615
  104.8 3.9 %all-to-all-start.3 = ((bf16[8,128,256]{2,1,0:T(8,128)(2,1)}), bf16[8,128,256]{2,1,0:T(8,128)(2,1)S(1)}, u32[]{:S(2)}, u32[]{:S(2)}) async-start(bf16[8,128,256]{2,1,0:T(8,128)(2,1)} %get-tuple-element.72), calls=%async_computation.3 | async-start | bytes 1048576 | tf_op jit(solution)/shard_map/all_to_all | solution.py:610
  108.9 1.5 collective-permute-start.10
  110.4 1.2 collective-permute-start.8
  111.6 0.8 collective-permute-start.9
  112.5 2.6 %collective-permute-done.10 = bf16[160,256]{1,0:T(8,128)(2,1)S(1)} collective-permute-done((bf16[160,256]{1,0:T(8,128)(2,1)S(1)}, bf16[160,256]{1,0:T(8,128)(2,1)S(1)}, u32[]{:S(2)}, u32[]{:S(2)}) %collective-permute-start.10) | collective-permute-done | bytes 81952 | tf_op jit(solution)/shard_map/ppermute | solution.py:615
  115.1 1.1 collective-permute-done.8
  116.1 0.3 collective-permute-done.9
  116.5 1.8 %collective-permute-start.11 = (bf16[136,256]{1,0:T(8,128)(2,1)S(1)}, bf16[136,256]{1,0:T(8,128)(2,1)S(1)}, u32[]{:S(2)}, u32[]{:S(2)}) collective-permute-start(bf16[136,256]{1,0:T(8,128)(2,1)S(1)} %get-tuple-element.87), channel_id=1, source_target_pairs={{0,2},{1,3},{2,0},{3,1},{4,6},{5,7},{6,4},{7,5},{8,10},{9,11},{10,... | collective-permute-start | bytes 208904 | tf_op jit(solution)/shard_map/ppermute | solution.py:615
  118.4 2.4 %collective-permute-start.12 = (bf16[136,256]{1,0:T(8,128)(2,1)S(1)}, bf16[136,256]{1,0:T(8,128)(2,1)S(1)}, u32[]{:S(2)}, u32[]{:S(2)}) collective-permute-start(bf16[136,256]{1,0:T(8,128)(2,1)S(1)} %get-tuple-element.88), channel_id=1, source_target_pairs={{0,4},{1,5},{2,6},{3,7},{4,0},{5,1},{6,2},{7,3},{8,12},{9,13},{10,... | collective-permute-start | bytes 208904 | tf_op jit(solution)/shard_map/ppermute | solution.py:615
  120.7 0.2 collective-permute-start.13
  121.0 0.7 collective-permute-done.11
  121.7 7.4 %collective-permute-done.12 = bf16[136,256]{1,0:T(8,128)(2,1)S(1)} collective-permute-done((bf16[136,256]{1,0:T(8,128)(2,1)S(1)}, bf16[136,256]{1,0:T(8,128)(2,1)S(1)}, u32[]{:S(2)}, u32[]{:S(2)}) %collective-permute-start.12) | collective-permute-done | bytes 69664 | tf_op jit(solution)/shard_map/ppermute | solution.py:615
  129.1 1.6 %collective-permute-start.14 = (bf16[136,256]{1,0:T(8,128)(2,1)S(1)}, bf16[136,256]{1,0:T(8,128)(2,1)S(1)}, u32[]{:S(2)}, u32[]{:S(2)}) collective-permute-start(bf16[136,256]{1,0:T(8,128)(2,1)S(1)} %fusion.6), channel_id=1, source_target_pairs={{0,2},{1,3},{2,0},{3,1},{4,6},{5,7},{6,4},{7,5},{8,10},{9,11},{10,... | collective-permute-start | bytes 208904 | tf_op jit(solution)/shard_map/ppermute | solution.py:615
  130.8 2.8 %collective-permute-start.16 = (bf16[136,256]{1,0:T(8,128)(2,1)S(1)}, bf16[136,256]{1,0:T(8,128)(2,1)S(1)}, u32[]{:S(2)}, u32[]{:S(2)}) collective-permute-start(bf16[136,256]{1,0:T(8,128)(2,1)S(1)} %fusion.6), channel_id=1, source_target_pairs={{0,6},{1,7},{2,4},{3,5},{4,2},{5,3},{6,0},{7,1},{8,14},{9,15},{10,... | collective-permute-start | bytes 208904 | tf_op jit(solution)/shard_map/ppermute | solution.py:615
  133.6 5.1 %collective-permute-done.15 = bf16[136,256]{1,0:T(8,128)(2,1)S(1)} collective-permute-done((bf16[136,256]{1,0:T(8,128)(2,1)S(1)}, bf16[136,256]{1,0:T(8,128)(2,1)S(1)}, u32[]{:S(2)}, u32[]{:S(2)}) %collective-permute-start.15) | collective-permute-done | bytes 69664 | tf_op jit(solution)/shard_map/ppermute | solution.py:615
  138.7 1.1 collective-permute-start.17
  139.9 0.9 collective-permute-start.18
  140.8 1.5 collective-permute-start.19
  142.3 5.5 %collective-permute-done.17 = bf16[4,136,256]{2,1,0:T(8,128)(2,1)S(1)} collective-permute-done((bf16[4,136,256]{2,1,0:T(8,128)(2,1)S(1)}, bf16[4,136,256]{2,1,0:T(8,128)(2,1)S(1)}, u32[]{:S(2)}, u32[]{:S(2)}) %collective-permute-start.17) | collective-permute-done | bytes 278560 | tf_op jit(solution)/shard_map/ppermute | solution.py:615
  147.8 3.8 %collective-permute-done.18 = bf16[4,136,256]{2,1,0:T(8,128)(2,1)S(1)} collective-permute-done((bf16[4,136,256]{2,1,0:T(8,128)(2,1)S(1)}, bf16[4,136,256]{2,1,0:T(8,128)(2,1)S(1)}, u32[]{:S(2)}, u32[]{:S(2)}) %collective-permute-start.18) | collective-permute-done | bytes 278560 | tf_op jit(solution)/shard_map/ppermute | solution.py:615
  151.8 2.7 %collective-permute-done.20.got_ref = bf16[4,4,136,256]{3,2,1,0:T(8,128)(2,1)S(1)} collective-permute-done((bf16[4,4,136,256]{3,2,1,0:T(8,128)(2,1)S(1)}, bf16[4,4,136,256]{3,2,1,0:T(8,128)(2,1)S(1)}, u32[]{:S(2)}, u32[]{:S(2)}) %collective-permute-start.20) | collective-permute-done | bytes 1114144 | tf_op jit(solution)/shard_map/ppermute | solution.py:615
  154.5 1.0 copy-done.3
  155.5 3.9 %unpack.1 = (f32[1,256]{1,0:T(1,128)}, f32[1,256]{1,0:T(1,128)}, f32[1,256]{1,0:T(1,128)}, f32[256,768]{1,0:T(8,128)}, f32[256,256]{1,0:T(8,128)}, /*index=5*/f3...) custom-call(bf16[4,4,136,256]{3,2,1,0:T(8,128)(2,1)} %copy-done, ...), custom_call_target="tpu_custom_call" | custom-call | tf_op jit(solution)/shard_map/unpack/pallas_call | solution.py:601
  159.4 0.8 copy.23
  (37 shorter events, 1.0 us)
Async XLA Ops:
  32.6 19.9 %all-to-all-start.1 = ((bf16[32,4,8,256]{3,2,1,0:T(8,128)(2,1)}), bf16[32,4,8,256]{3,2,1,0:T(8,128)(2,1)S(1)}, u32[]{:S(2)}, u32[]{:S(2)}) async-start(bf16[32,4,8,256]{3,2,1,0:T(8,128)(2,1)} %get-tuple-element.47), calls=%async_computation.1 | async-start | bytes 1048576 | tf_op jit(solution)/shard_map/all_to_all | solution.py:610
  38.2 8.1 %collective-permute-start = (bf16[264,256]{1,0:T(8,128)(2,1)}, bf16[264,256]{1,0:T(8,128)(2,1)S(1)}, u32[]{:S(2)}, u32[]{:S(2)}) collective-permute-start(bf16[264,256]{1,0:T(8,128)(2,1)} %get-tuple-element.49), channel_id=1, source_target_pairs={{0,8},{8,0},{16,24},{24,16},{1,9},{9,1},{17,25},{25,17},{2,10},{10... | collective-permute-start | bytes 405512 | tf_op jit(solution)/shard_map/ppermute | solution.py:615
  40.0 9.4 %collective-permute-start.1 = (bf16[264,256]{1,0:T(8,128)(2,1)}, bf16[264,256]{1,0:T(8,128)(2,1)S(1)}, u32[]{:S(2)}, u32[]{:S(2)}) collective-permute-start(bf16[264,256]{1,0:T(8,128)(2,1)} %get-tuple-element.50), channel_id=1, source_target_pairs={{0,16},{8,24},{16,0},{24,8},{1,17},{9,25},{17,1},{25,9},{2,18},{10... | collective-permute-start | bytes 405512 | tf_op jit(solution)/shard_map/ppermute | solution.py:615
  41.5 9.9 %collective-permute-start.2 = (bf16[264,256]{1,0:T(8,128)(2,1)}, bf16[264,256]{1,0:T(8,128)(2,1)S(1)}, u32[]{:S(2)}, u32[]{:S(2)}) collective-permute-start(bf16[264,256]{1,0:T(8,128)(2,1)} %get-tuple-element.51), channel_id=1, source_target_pairs={{0,24},{8,16},{16,8},{24,0},{1,25},{9,17},{17,9},{25,1},{2,26},{10... | collective-permute-start | bytes 405512 | tf_op jit(solution)/shard_map/ppermute | solution.py:615
  46.3 6.2 %copy-start.6 = (bf16[264,256]{1,0:T(8,128)(2,1)}, bf16[264,256]{1,0:T(8,128)(2,1)S(1)}, u32[]{:S(2)}) copy-start(bf16[264,256]{1,0:T(8,128)(2,1)S(1)} %collective-permute-done.refs_2_) | copy-start | bytes 405508
  49.4 3.1 %copy-start.7 = (bf16[264,256]{1,0:T(8,128)(2,1)}, bf16[264,256]{1,0:T(8,128)(2,1)S(1)}, u32[]{:S(2)}) copy-start(bf16[264,256]{1,0:T(8,128)(2,1)S(1)} %collective-permute-done.1.refs_3_) | copy-start | bytes 405508
  51.4 1.1 copy-start.8
  52.5 0.8 copy-start.2
  72.0 19.5 %all-to-all-start.2 = ((bf16[32,4,8,256]{3,2,1,0:T(8,128)(2,1)}), bf16[32,4,8,256]{3,2,1,0:T(8,128)(2,1)S(1)}, u32[]{:S(2)}, u32[]{:S(2)}) async-start(bf16[32,4,8,256]{3,2,1,0:T(8,128)(2,1)} %bitcast.59), calls=%async_computation.2 | async-start | bytes 1048576 | tf_op jit(solution)/shard_map/all_to_all | solution.py:610
  81.9 18.9 %collective-permute-start.3 = (bf16[768,256]{1,0:T(8,128)(2,1)}, bf16[768,256]{1,0:T(8,128)(2,1)S(1)}, u32[]{:S(2)}, u32[]{:S(2)}) collective-permute-start(bf16[768,256]{1,0:T(8,128)(2,1)} %get-tuple-element.61), channel_id=1, source_target_pairs={{0,8},{8,0},{16,24},{24,16},{1,9},{9,1},{17,25},{25,17},{2,10},{10... | collective-permute-start | bytes 1179656 | tf_op jit(solution)/shard_map/ppermute | solution.py:615
  83.5 19.4 %collective-permute-start.4 = (bf16[768,256]{1,0:T(8,128)(2,1)}, bf16[768,256]{1,0:T(8,128)(2,1)S(1)}, u32[]{:S(2)}, u32[]{:S(2)}) collective-permute-start(bf16[768,256]{1,0:T(8,128)(2,1)} %get-tuple-element.62), channel_id=1, source_target_pairs={{0,16},{8,24},{16,0},{24,8},{1,17},{9,25},{17,1},{25,9},{2,18},{10... | collective-permute-start | bytes 1179656 | tf_op jit(solution)/shard_map/ppermute | solution.py:615
  84.9 19.6 %collective-permute-start.5 = (bf16[768,256]{1,0:T(8,128)(2,1)}, bf16[768,256]{1,0:T(8,128)(2,1)S(1)}, u32[]{:S(2)}, u32[]{:S(2)}) collective-permute-start(bf16[768,256]{1,0:T(8,128)(2,1)} %get-tuple-element.63), channel_id=1, source_target_pairs={{0,24},{8,16},{16,8},{24,0},{1,25},{9,17},{17,9},{25,1},{2,26},{10... | collective-permute-start | bytes 1179656 | tf_op jit(solution)/shard_map/ppermute | solution.py:615
  91.5 0.8 copy-start.1
  92.3 12.2 %copy-start.4 = (bf16[768,256]{1,0:T(8,128)(2,1)S(1)}, bf16[768,256]{1,0:T(8,128)(2,1)}, u32[]{:S(2)}) copy-start(bf16[768,256]{1,0:T(8,128)(2,1)} %get-tuple-element.60) | copy-start | bytes 1179652
  100.7 8.0 %collective-permute-start.7 = (bf16[640,256]{1,0:T(8,128)(2,1)}, bf16[640,256]{1,0:T(8,128)(2,1)S(1)}, u32[]{:S(2)}, u32[]{:S(2)}) collective-permute-start(bf16[640,256]{1,0:T(8,128)(2,1)} %get-tuple-element.71), channel_id=1, source_target_pairs={{0,1},{1,0},{2,3},{3,2},{4,5},{5,4},{6,7},{7,6},{8,9},{9,8},{10,11... | collective-permute-start | bytes 983048 | tf_op jit(solution)/shard_map/ppermute | solution.py:615
  104.7 4.0 %copy-start.5 = (bf16[640,256]{1,0:T(8,128)(2,1)S(1)}, bf16[640,256]{1,0:T(8,128)(2,1)}, u32[]{:S(2)}) copy-start(bf16[640,256]{1,0:T(8,128)(2,1)} %get-tuple-element.70) | copy-start | bytes 983044
  104.7 7.7 %collective-permute-start.6 = (bf16[384,256]{1,0:T(8,128)(2,1)S(1)}, bf16[384,256]{1,0:T(8,128)(2,1)S(1)}, u32[]{:S(2)}, u32[]{:S(2)}) collective-permute-start(bf16[384,256]{1,0:T(8,128)(2,1)S(1)} %dynamic-slice_bitcast_fusion), channel_id=1, source_target_pairs={{0,1},{1,0},{2,3},{3,2},{4,5},{5,4},{6,7},{7,6},{8,9},{9,8},{10,11... | collective-permute-start | bytes 589832 | tf_op jit(solution)/shard_map/ppermute | solution.py:615
  104.8 33.9 %all-to-all-start.3 = ((bf16[8,128,256]{2,1,0:T(8,128)(2,1)}), bf16[8,128,256]{2,1,0:T(8,128)(2,1)S(1)}, u32[]{:S(2)}, u32[]{:S(2)}) async-start(bf16[8,128,256]{2,1,0:T(8,128)(2,1)} %get-tuple-element.72), calls=%async_computation.3 | async-start | bytes 1048576 | tf_op jit(solution)/shard_map/all_to_all | solution.py:610
  108.9 6.2 %collective-permute-start.10 = (bf16[160,256]{1,0:T(8,128)(2,1)S(1)}, bf16[160,256]{1,0:T(8,128)(2,1)S(1)}, u32[]{:S(2)}, u32[]{:S(2)}) collective-permute-start(bf16[160,256]{1,0:T(8,128)(2,1)S(1)} %get-tuple-element.85), channel_id=1, source_target_pairs={{0,24},{8,16},{16,8},{24,0},{1,25},{9,17},{17,9},{25,1},{2,26},{10... | collective-permute-start | bytes 245768 | tf_op jit(solution)/shard_map/ppermute | solution.py:615
  110.4 5.8 %collective-permute-start.8 = (bf16[160,256]{1,0:T(8,128)(2,1)S(1)}, bf16[160,256]{1,0:T(8,128)(2,1)S(1)}, u32[]{:S(2)}, u32[]{:S(2)}) collective-permute-start(bf16[160,256]{1,0:T(8,128)(2,1)S(1)} %get-tuple-element.84), channel_id=1, source_target_pairs={{0,8},{8,0},{16,24},{24,16},{1,9},{9,1},{17,25},{25,17},{2,10},{10... | collective-permute-start | bytes 245768 | tf_op jit(solution)/shard_map/ppermute | solution.py:615
  111.6 4.9 %collective-permute-start.9 = (bf16[160,256]{1,0:T(8,128)(2,1)S(1)}, bf16[160,256]{1,0:T(8,128)(2,1)S(1)}, u32[]{:S(2)}, u32[]{:S(2)}) collective-permute-start(bf16[160,256]{1,0:T(8,128)(2,1)S(1)} %get-tuple-element.86), channel_id=1, source_target_pairs={{0,16},{8,24},{16,0},{24,8},{1,17},{9,25},{17,1},{25,9},{2,18},{10... | collective-permute-start | bytes 245768 | tf_op jit(solution)/shard_map/ppermute | solution.py:615
  116.5 5.2 %collective-permute-start.11 = (bf16[136,256]{1,0:T(8,128)(2,1)S(1)}, bf16[136,256]{1,0:T(8,128)(2,1)S(1)}, u32[]{:S(2)}, u32[]{:S(2)}) collective-permute-start(bf16[136,256]{1,0:T(8,128)(2,1)S(1)} %get-tuple-element.87), channel_id=1, source_target_pairs={{0,2},{1,3},{2,0},{3,1},{4,6},{5,7},{6,4},{7,5},{8,10},{9,11},{10,... | collective-permute-start | bytes 208904 | tf_op jit(solution)/shard_map/ppermute | solution.py:615
  118.4 10.7 %collective-permute-start.12 = (bf16[136,256]{1,0:T(8,128)(2,1)S(1)}, bf16[136,256]{1,0:T(8,128)(2,1)S(1)}, u32[]{:S(2)}, u32[]{:S(2)}) collective-permute-start(bf16[136,256]{1,0:T(8,128)(2,1)S(1)} %get-tuple-element.88), channel_id=1, source_target_pairs={{0,4},{1,5},{2,6},{3,7},{4,0},{5,1},{6,2},{7,3},{8,12},{9,13},{10,... | collective-permute-start | bytes 208904 | tf_op jit(solution)/shard_map/ppermute | solution.py:615
  120.7 8.3 %collective-permute-start.13 = (bf16[136,256]{1,0:T(8,128)(2,1)S(1)}, bf16[136,256]{1,0:T(8,128)(2,1)S(1)}, u32[]{:S(2)}, u32[]{:S(2)}) collective-permute-start(bf16[136,256]{1,0:T(8,128)(2,1)S(1)} %get-tuple-element.89), channel_id=1, source_target_pairs={{0,6},{1,7},{2,4},{3,5},{4,2},{5,3},{6,0},{7,1},{8,14},{9,15},{10,... | collective-permute-start | bytes 208904 | tf_op jit(solution)/shard_map/ppermute | solution.py:615
  129.1 4.5 %collective-permute-start.14 = (bf16[136,256]{1,0:T(8,128)(2,1)S(1)}, bf16[136,256]{1,0:T(8,128)(2,1)S(1)}, u32[]{:S(2)}, u32[]{:S(2)}) collective-permute-start(bf16[136,256]{1,0:T(8,128)(2,1)S(1)} %fusion.6), channel_id=1, source_target_pairs={{0,2},{1,3},{2,0},{3,1},{4,6},{5,7},{6,4},{7,5},{8,10},{9,11},{10,... | collective-permute-start | bytes 208904 | tf_op jit(solution)/shard_map/ppermute | solution.py:615
  130.8 7.9 %collective-permute-start.15 = (bf16[136,256]{1,0:T(8,128)(2,1)S(1)}, bf16[136,256]{1,0:T(8,128)(2,1)S(1)}, u32[]{:S(2)}, u32[]{:S(2)}) collective-permute-start(bf16[136,256]{1,0:T(8,128)(2,1)S(1)} %fusion.6), channel_id=1, source_target_pairs={{0,4},{1,5},{2,6},{3,7},{4,0},{5,1},{6,2},{7,3},{8,12},{9,13},{10,... | collective-permute-start | bytes 208904 | tf_op jit(solution)/shard_map/ppermute | solution.py:615
  130.8 7.9 %collective-permute-start.16 = (bf16[136,256]{1,0:T(8,128)(2,1)S(1)}, bf16[136,256]{1,0:T(8,128)(2,1)S(1)}, u32[]{:S(2)}, u32[]{:S(2)}) collective-permute-start(bf16[136,256]{1,0:T(8,128)(2,1)S(1)} %fusion.6), channel_id=1, source_target_pairs={{0,6},{1,7},{2,4},{3,5},{4,2},{5,3},{6,0},{7,1},{8,14},{9,15},{10,... | collective-permute-start | bytes 208904 | tf_op jit(solution)/shard_map/ppermute | solution.py:615
  138.7 9.0 %collective-permute-start.17 = (bf16[4,136,256]{2,1,0:T(8,128)(2,1)S(1)}, bf16[4,136,256]{2,1,0:T(8,128)(2,1)S(1)}, u32[]{:S(2)}, u32[]{:S(2)}) collective-permute-start(bf16[4,136,256]{2,1,0:T(8,128)(2,1)S(1)} %pad_maximum_fusion.1), channel_id=1, source_target_pairs={{0,8},{8,0},{16,24},{24,16},{1,9},{9,1},{17,25},{25,17},{2,10},{10... | collective-permute-start | bytes 835592 | tf_op jit(solution)/shard_map/ppermute | solution.py:615
  139.9 11.7 %collective-permute-start.18 = (bf16[4,136,256]{2,1,0:T(8,128)(2,1)S(1)}, bf16[4,136,256]{2,1,0:T(8,128)(2,1)S(1)}, u32[]{:S(2)}, u32[]{:S(2)}) collective-permute-start(bf16[4,136,256]{2,1,0:T(8,128)(2,1)S(1)} %pad_maximum_fusion.1), channel_id=1, source_target_pairs={{0,16},{8,24},{16,0},{24,8},{1,17},{9,25},{17,1},{25,9},{2,18},{10... | collective-permute-start | bytes 835592 | tf_op jit(solution)/shard_map/ppermute | solution.py:615
  140.8 10.8 %collective-permute-start.19 = (bf16[4,136,256]{2,1,0:T(8,128)(2,1)S(1)}, bf16[4,136,256]{2,1,0:T(8,128)(2,1)S(1)}, u32[]{:S(2)}, u32[]{:S(2)}) collective-permute-start(bf16[4,136,256]{2,1,0:T(8,128)(2,1)S(1)} %pad_maximum_fusion.1), channel_id=1, source_target_pairs={{0,24},{8,16},{16,8},{24,0},{1,25},{9,17},{17,9},{25,1},{2,26},{10... | collective-permute-start | bytes 835592 | tf_op jit(solution)/shard_map/ppermute | solution.py:615
  151.7 2.8 %copy-start = (bf16[4,4,136,256]{3,2,1,0:T(8,128)(2,1)}, bf16[4,4,136,256]{3,2,1,0:T(8,128)(2,1)S(1)}, u32[]{:S(2)}) copy-start(bf16[4,4,136,256]{3,2,1,0:T(8,128)(2,1)S(1)} %pad_maximum_fusion.own_ref) | copy-start | bytes 3342340
  151.7 2.8 %collective-permute-start.20 = (bf16[4,4,136,256]{3,2,1,0:T(8,128)(2,1)S(1)}, bf16[4,4,136,256]{3,2,1,0:T(8,128)(2,1)S(1)}, u32[]{:S(2)}, u32[]{:S(2)}) collective-permute-start(bf16[4,4,136,256]{3,2,1,0:T(8,128)(2,1)S(1)} %pad_maximum_fusion.own_ref), channel_id=1, source_target_pairs={{0,1},{1,0},{2,3},{3,2},{4,5},{5,4},{6,7},{7,6},{8,9},{9,8},{10,11... | collective-permute-start | bytes 3342344 | tf_op jit(solution)/shard_map/ppermute | solution.py:615
  154.5 1.0 copy-start.3

commit v4 on v3

--- a/solution.py
+++ b/solution.py
@@ -11,6 +11,8 @@
 ALL = ("rows", "cols")
 BF = jnp.bfloat16
 F32 = jnp.float32
+ROWS_FORWARD = 4
+ROWS_BACKWARD = 2
 VMEM_LIMIT = 56 * 1024 * 1024
 
 
@@ -80,8 +82,16 @@
     return dq.astype(BF), dk.astype(BF), dv.astype(BF)
 
 
-def load_cells(ref, pieces):
-    return jnp.concatenate([ref[s].astype(F32) for s in range(pieces)], axis=0)
+def load_cells(ref, pieces, wl):
+    rows = ref.shape[1] // wl
+    return jnp.concatenate(
+        [
+            ref[s, i * wl : (i + 1) * wl].astype(F32)
+            for i in range(rows)
+            for s in range(pieces)
+        ],
+        axis=0,
+    )
 
 
 def row_bias(b_ref, row, pieces, length):
@@ -106,24 +116,28 @@
     r_size, c_size, wl, cpd, length, d = dims
     factor = float(d // HEADS) ** (-0.5)
     masks = head_masks(d)
-    x = load_cells(x_ref, c_size)
+    x = load_cells(x_ref, c_size, wl)
+    rows = x_ref.shape[1] // wl
     n, _ = norm(x)
     h = (n * gain_ref[...]).astype(BF)
     qkv = dot(h, wqkv_ref[...]).astype(BF)
-    qkv_ref[0] = qkv
-    q, k, v = qkv[:, :d], qkv[:, d : 2 * d], qkv[:, 2 * d :]
-    bias = row_bias(b_ref, pl.program_id(0), c_size, length)
-    weights = softmax_heads(q, k, bias, masks, factor)
-    low = [w.astype(BF) for w in weights]
-    for i in range(HEADS):
-        p_ref[0, i] = low[i]
-    o = mix_heads(low, v, masks).astype(BF)
-    o_ref[0] = o
-    y = (x + dot(o, wout_ref[...])).astype(BF)
-    for c in range(c_size):
-        for r in range(r_size):
-            at = c * wl + r * cpd
-            y_ref[r * c_size + c, 0] = y[at : at + cpd]
+    outs = []
+    for row in range(rows):
+        part = slice(row * length, (row + 1) * length)
+        qkv_ref[row] = qkv[part]
+        q, k, v = qkv[part, :d], qkv[part, d : 2 * d], qkv[part, 2 * d :]
+        bias = row_bias(b_ref, pl.program_id(0) * rows + row, c_size, length)
+        low = [w.astype(BF) for w in softmax_heads(q, k, bias, masks, factor)]
+        for i in range(HEADS):
+            p_ref[row, i] = low[i]
+        outs.append(mix_heads(low, v, masks).astype(BF))
+        o_ref[row] = outs[row]
+    y = (x + dot(jnp.concatenate(outs, axis=0), wout_ref[...])).astype(BF)
+    for row in range(rows):
+        for c in range(c_size):
+            for r in range(r_size):
+                at = row * length + c * wl + r * cpd
+                y_ref[r * c_size + c, row] = y[at : at + cpd]
 
 
 def store_rows(keep_ref, send_ref, parity, row, value):
@@ -160,31 +174,44 @@
         keep_ref[...] = jnp.zeros_like(keep_ref)
         send_ref[...] = jnp.zeros_like(send_ref)
 
+    rows = dy_ref.shape[1]
     dy = jnp.concatenate(
-        [dy_ref[r * c_size + c, 0].astype(F32) for c in range(c_size) for r in range(r_size)],
+        [
+            dy_ref[r * c_size + c, row].astype(F32)
+            for row in range(rows)
+            for c in range(c_size)
+            for r in range(r_size)
+        ],
         axis=0,
     )
     dy_low = dy.astype(BF)
     do = dot_nt(dy_low, wout_ref[...]).astype(BF)
-    qkv = qkv_ref[0]
-    q, k, v = qkv[:, :d], qkv[:, d : 2 * d], qkv[:, 2 * d :]
-    low = [p_ref[0, i] for i in range(HEADS)]
-    weights = [w.astype(F32) for w in low]
-    dq, dk, dv = heads_back(weights, low, do, q, k, v, masks, factor)
-    dqkv = jnp.concatenate([dq, dk, dv], axis=1)
+    grads = []
+    for row in range(rows):
+        qkv = qkv_ref[row]
+        q, k, v = qkv[:, :d], qkv[:, d : 2 * d], qkv[:, 2 * d :]
+        low = [p_ref[row, i] for i in range(HEADS)]
+        weights = [w.astype(F32) for w in low]
+        part = slice(row * length, (row + 1) * length)
+        grads.append(
+            jnp.concatenate(heads_back(weights, low, do[part], q, k, v, masks, factor), axis=1)
+        )
+    dqkv = jnp.concatenate(grads, axis=0)
     g = dot_nt(dqkv, wqkv_ref[...])
-    n, inverse = norm(load_cells(x_ref, c_size))
+    n, inverse = norm(load_cells(x_ref, c_size, wl))
     h = (n * gain_ref[...]).astype(BF)
     dt = (dy + norm_back(g, n, inverse, gain_ref[...])).astype(BF)
-    for s in range(c_size):
-        dt_ref[s] = dt[s * wl : (s + 1) * wl]
+    for row in range(rows):
+        for s in range(c_size):
+            at = row * length + s * wl
+            dt_ref[s, row * wl : (row + 1) * wl] = dt[at : at + wl]
     dg_s[...] += jnp.sum(g * n, axis=0, keepdims=True)
     dwqkv_s[...] += dot_tn(h, dqkv)
-    dwout_s[...] += dot_tn(o_ref[0], dy_low)
+    dwout_s[...] += dot_tn(jnp.concatenate([o_ref[row] for row in range(rows)], axis=0), dy_low)
 
     @pl.when(step == steps - 1)
     def _():
-        scale = float(length * steps * r_size * c_size) ** (-0.5)
+        scale = float(length * steps * rows * r_size * c_size) ** (-0.5)
         parity = lax.rem(lax.axis_index("cols"), 2)
         for i in range(3):
             grad = (dwqkv_s[:, i * d : (i + 1) * d] * scale).astype(BF)
@@ -330,82 +357,85 @@
 def column_kernel(
     dims, *refs
 ):
-    r_size, hl, cpd, length, d, chunk = dims
+    r_size, hl, cpd, length, d = dims
     y_ref, *ct_refs = refs[: 1 + r_size]
     (
         gain_ref, wqkv_ref, wout_ref, gmlp_ref, wup_ref, wdown_ref,
         dy_ref, h2_ref, dqkv_ref, o2_ref, dy2_ref, h3_ref, du_ref, act_ref, ctc_ref,
-        dg_ref, dgm_ref, wire_s, x_s, ct_s, bias_s, p_s,
+        dg_ref, dgm_ref, wire_s, x_s, ct_s, bias_s, p_s, sems, *bufs
     ) = refs[1 + r_size :]
-    step, steps = pl.program_id(0), pl.num_programs(0)
+    copies = []
     factor = float(d // HEADS) ** (-0.5)
     masks = head_masks(d)
-    tokens = chunk * length
+    tokens = cpd * length
+
+    def emit(out_ref, value):
+        at = len(copies)
+        bufs[at][...] = value
+        copies.append(pltpu.make_async_copy(bufs[at], out_ref, sems.at[at]))
+        copies[at].start()
+
 
     r_at = lax.axis_index("rows")
 
-    @pl.when(step == 0)
-    def _():
-        for lanes in range(d // LANES):
-            cut = slice(lanes * LANES, (lanes + 1) * LANES)
-            wire_s[lanes] = y_ref[:, cut].astype(F32)
-            for j in range(cpd):
-                x_s[j, :, cut] = wire_s[lanes, pl.ds(j, length, stride=cpd), :]
-        block = hl * cpd
-        for lanes in range(d // LANES):
-            cut = slice(lanes * LANES, (lanes + 1) * LANES)
-            for s in range(r_size):
-                source = jnp.bitwise_xor(r_at, s)
-                to = pl.ds(pl.multiple_of(source * block, block), block)
-                wire_s[lanes, to, :] = ct_refs[s][:block, cut].astype(F32)
-            for j in range(cpd):
-                ct_s[j, :, cut] = wire_s[lanes, pl.ds(j, length, stride=cpd), :]
-        total = ct_refs[0][block:].astype(F32)
-        for s in range(1, r_size):
-            total = total + ct_refs[s][block:].astype(F32)
+    for lanes in range(d // LANES):
+        cut = slice(lanes * LANES, (lanes + 1) * LANES)
+        wire_s[lanes] = y_ref[:, cut].astype(F32)
         for j in range(cpd):
-            bias_s[j] = total[j : j + 1, :length]
-        dg_ref[...] = jnp.zeros_like(dg_ref)
-        dgm_ref[...] = jnp.zeros_like(dgm_ref)
-
-    at = pl.ds(step * chunk, chunk)
-    x = x_s[at].reshape(tokens, d)
-    ct = ct_s[at].reshape(tokens, d)
+            x_s[j, :, cut] = wire_s[lanes, pl.ds(j, length, stride=cpd), :]
+    block = hl * cpd
+    for lanes in range(d // LANES):
+        cut = slice(lanes * LANES, (lanes + 1) * LANES)
+        for s in range(r_size):
+            source = jnp.bitwise_xor(r_at, s)
+            to = pl.ds(pl.multiple_of(source * block, block), block)
+            wire_s[lanes, to, :] = ct_refs[s][:block, cut].astype(F32)
+        for j in range(cpd):
+            ct_s[j, :, cut] = wire_s[lanes, pl.ds(j, length, stride=cpd), :]
+    total = ct_refs[0][block:].astype(F32)
+    for s in range(1, r_size):
+        total = total + ct_refs[s][block:].astype(F32)
+    for j in range(cpd):
+        bias_s[j] = total[j : j + 1, :length]
+
+    x = x_s[...].reshape(tokens, d)
+    ct = ct_s[...].reshape(tokens, d)
     n2, r2 = norm(x)
     h2 = (n2 * gain_ref[...]).astype(BF)
-    h2_ref[...] = h2
+    emit(h2_ref, h2)
     qkv = dot(h2, wqkv_ref[...]).astype(BF)
     outs = []
-    for j in range(chunk):
+    for j in range(cpd):
         part = slice(j * length, (j + 1) * length)
         q, k, v = qkv[part, :d], qkv[part, d : 2 * d], qkv[part, 2 * d :]
-        weights = softmax_heads(q, k, bias_s[step * chunk + j], masks, factor)
+        weights = softmax_heads(q, k, bias_s[j], masks, factor)
         for i in range(HEADS):
             p_s[j, i] = weights[i]
         outs.append(mix_heads([w.astype(BF) for w in weights], v, masks))
     o2 = jnp.concatenate(outs, axis=0).astype(BF)
-    o2_ref[...] = o2
+    emit(o2_ref, o2)
     y2 = (x + dot(o2, wout_ref[...])).astype(BF).astype(F32)
     n3, r3 = norm(y2)
     h3 = (n3 * gmlp_ref[...]).astype(BF)
-    h3_ref[...] = h3
+    emit(h3_ref, h3)
     ct_low = ct.astype(BF)
-    ctc_ref[...] = ct_low
+    emit(ctc_ref, ct_low)
     u = dot(h3, wup_ref[...])
     root = 0.7978845608028654
+    cube = 0.044715 * root
     square = u * u
-    t = jnp.tanh(root * (u + 0.044715 * (u * square)))
-    act_ref[...] = (0.5 * u * (1.0 + t)).astype(BF)
-    slope = 0.5 * (1.0 + t) + 0.5 * u * (1.0 - t * t) * (root * (1.0 + 3.0 * 0.044715 * square))
+    c = 0.5 + 0.5 * jnp.tanh(u * (root + cube * square))
+    emit(act_ref, (u * c).astype(BF))
+    slope = c * (1.0 + (1.0 - c) * (u * (2.0 * root + 6.0 * cube * square)))
     du = (dot_nt(ct_low, wdown_ref[...]) * slope).astype(BF)
-    du_ref[...] = du
+    emit(du_ref, du)
     g3 = dot_nt(du, wup_ref[...])
-    dgm_ref[...] += jnp.sum(g3 * n3, axis=0, keepdims=True)
+    dgm_ref[...] = jnp.sum(g3 * n3, axis=0, keepdims=True)
     dy2 = (ct + norm_back(g3, n3, r3, gmlp_ref[...])).astype(BF)
-    dy2_ref[...] = dy2
+    emit(dy2_ref, dy2)
     do = dot_nt(dy2, wout_ref[...]).astype(BF)
     grads = []
-    for j in range(chunk):
+    for j in range(cpd):
         part = slice(j * length, (j + 1) * length)
         q, k, v = qkv[part, :d], qkv[part, d : 2 * d], qkv[part, 2 * d :]
         weights = [p_s[j, i] for i in range(HEADS)]
@@ -414,19 +444,18 @@
             jnp.concatenate(heads_back(weights, low, do[part], q, k, v, masks, factor), axis=1)
         )
     dqkv = jnp.concatenate(grads, axis=0)
-    dqkv_ref[...] = dqkv
+    emit(dqkv_ref, dqkv)
     g2 = dot_nt(dqkv, wqkv_ref[...])
-    dg_ref[...] += jnp.sum(g2 * n2, axis=0, keepdims=True)
+    dg_ref[...] = jnp.sum(g2 * n2, axis=0, keepdims=True)
     dy1 = dy2.astype(F32) + norm_back(g2, n2, r2, gain_ref[...])
-    x_s[at] = dy1.reshape(chunk, length, d)
-
-    @pl.when(step == steps - 1)
-    def _():
-        for lanes in range(d // LANES):
-            cut = slice(lanes * LANES, (lanes + 1) * LANES)
-            for j in range(cpd):
-                wire_s[lanes, pl.ds(j, length, stride=cpd), :] = x_s[j, :, cut]
-            dy_ref[:, cut] = wire_s[lanes].astype(BF)
+    x_s[...] = dy1.reshape(cpd, length, d)
+    for lanes in range(d // LANES):
+        cut = slice(lanes * LANES, (lanes + 1) * LANES)
+        for j in range(cpd):
+            wire_s[lanes, pl.ds(j, length, stride=cpd), :] = x_s[j, :, cut]
+        dy_ref[:, cut] = wire_s[lanes].astype(BF)
+    for copy in copies:
+        copy.wait()
 
 
 def whole(shape):
@@ -450,24 +479,25 @@
 
 
 def row_forward(dims, rpd, recv, gain, w_qkv, w_out):
+    rows = min(rpd, ROWS_FORWARD)
     r_size, c_size, wl, cpd, length, d = dims
     n_dev = r_size * c_size
     extra = recv.shape[1] - rpd * wl
     return pl.pallas_call(
         functools.partial(row_forward_kernel, dims),
-        grid=(rpd,),
+        grid=(rpd // rows,),
         in_specs=[
-            pl.BlockSpec((c_size, wl, d), lambda i: (0, i, 0)),
+            pl.BlockSpec((c_size, rows * wl, d), lambda i: (0, i, 0)),
             pl.BlockSpec((c_size, extra, d), lambda i: (0, rpd * wl // extra, 0)),
             whole((1, d)),
             whole((d, 3 * d)),
             whole((d, d)),
         ],
         out_specs=[
-            pl.BlockSpec((n_dev, 1, cpd, d), lambda i: (0, i, 0, 0)),
-            pl.BlockSpec((1, length, 3 * d), lambda i: (i, 0, 0)),
-            pl.BlockSpec((1, length, d), lambda i: (i, 0, 0)),
-            pl.BlockSpec((1, HEADS, length, length), lambda i: (i, 0, 0, 0)),
+            pl.BlockSpec((n_dev, rows, cpd, d), lambda i: (0, i, 0, 0)),
+            pl.BlockSpec((rows, length, 3 * d), lambda i: (i, 0, 0)),
+            pl.BlockSpec((rows, length, d), lambda i: (i, 0, 0)),
+            pl.BlockSpec((rows, HEADS, length, length), lambda i: (i, 0, 0, 0)),
         ],
         out_shape=[
             jax.ShapeDtypeStruct((n_dev, rpd, cpd, d), BF),
@@ -481,17 +511,18 @@
 
 
 def row_backward(dims, rpd, half, recv, dy, qkv, o, p, gain, w_qkv, w_out, dg_col, dg_mlp):
+    rows = min(rpd, ROWS_BACKWARD)
     r_size, c_size, wl, cpd, length, d = dims
     n_dev = r_size * c_size
     return pl.pallas_call(
         functools.partial(row_backward_kernel, dims),
-        grid=(rpd,),
+        grid=(rpd // rows,),
         in_specs=[
-            pl.BlockSpec((c_size, wl, d), lambda i: (0, i, 0)),
-            pl.BlockSpec((n_dev, 1, cpd, d), lambda i: (0, i, 0, 0)),
-            pl.BlockSpec((1, length, 3 * d), lambda i: (i, 0, 0)),
-            pl.BlockSpec((1, length, d), lambda i: (i, 0, 0)),
-            pl.BlockSpec((1, HEADS, length, length), lambda i: (i, 0, 0, 0)),
+            pl.BlockSpec((c_size, rows * wl, d), lambda i: (0, i, 0)),
+            pl.BlockSpec((n_dev, rows, cpd, d), lambda i: (0, i, 0, 0)),
+            pl.BlockSpec((rows, length, 3 * d), lambda i: (i, 0, 0)),
+            pl.BlockSpec((rows, length, d), lambda i: (i, 0, 0)),
+            pl.BlockSpec((rows, HEADS, length, length), lambda i: (i, 0, 0, 0)),
             whole((1, d)),
             whole((d, 3 * d)),
             whole((d, d)),
@@ -499,7 +530,7 @@
             whole((1, d)),
         ],
         out_specs=[
-            pl.BlockSpec((c_size, wl, d), lambda i: (0, i, 0)),
+            pl.BlockSpec((c_size, rows * wl, d), lambda i: (0, i, 0)),
             whole((half, d)),
             whole((half, d)),
         ],
@@ -519,43 +550,28 @@
 
 
 def column_stage(dims, y_wire, ct_blocks, gain, w_qkv, w_out, gain_mlp, w_up, w_down):
-    r_size, hl, cpd, length, d, chunk = dims
+    r_size, hl, cpd, length, d = dims
     tokens = cpd * length
     ff = w_up.shape[1]
-    part = chunk * length
-
-    def rows_of(width):
-        return pl.BlockSpec((part, width), lambda i: (i, 0))
-
-    def shape_of(width):
-        return jax.ShapeDtypeStruct((tokens, width), BF)
-
     widths = (d, 3 * d, d, d, d, ff, ff, d)
+    order = (d, d, d, d, ff, ff, d, 3 * d)
     return pl.pallas_call(
         functools.partial(column_kernel, dims),
-        grid=(cpd // chunk,),
-        in_specs=[
-            whole((tokens, d)),
-            *[whole(block.shape) for block in ct_blocks],
-            whole((1, d)),
-            whole((d, 3 * d)),
-            whole((d, d)),
-            whole((1, d)),
-            whole((d, ff)),
-            whole((ff, d)),
-        ],
-        out_specs=[whole((tokens, d))] + [rows_of(w) for w in widths] + [whole((1, d))] * 2,
-        out_shape=[shape_of(d)]
-        + [shape_of(w) for w in widths]
+        out_specs=[pl.BlockSpec(memory_space=pltpu.VMEM)]
+        + [pl.BlockSpec(memory_space=pl.ANY)] * len(widths)
+        + [pl.BlockSpec(memory_space=pltpu.VMEM)] * 2,
+        out_shape=[jax.ShapeDtypeStruct((tokens, w), BF) for w in (d,) + widths]
         + [jax.ShapeDtypeStruct((1, d), F32)] * 2,
         scratch_shapes=[
             pltpu.VMEM((d // LANES, tokens, LANES), F32),
             pltpu.VMEM((cpd, length, d), F32),
             pltpu.VMEM((cpd, length, d), F32),
             pltpu.VMEM((cpd, 1, length), F32),
-            pltpu.VMEM((chunk, HEADS, length, length), F32),
-        ],
-        compiler_params=params(),
+            pltpu.VMEM((cpd, HEADS, length, length), F32),
+            pltpu.SemaphoreType.DMA((len(order),)),
+        ]
+        + [pltpu.VMEM((tokens, w), BF) for w in order],
+        compiler_params=pltpu.CompilerParams(vmem_limit_bytes=VMEM_LIMIT),
         name="column_stage",
     )(y_wire, *ct_blocks, gain, w_qkv, w_out, gain_mlp, w_up, w_down)
 
@@ -652,8 +668,7 @@
     r_at, c_at = lax.axis_index("rows"), lax.axis_index("cols")
     z_size, z_at = c_size // 2, lax.axis_index("cols") // 2
     row_dims = (r_size, c_size, wl, cpd, row_len, d)
-    chunk = min(cpd, max(1, 512 // col_len))
-    col_dims = (r_size, hl, cpd, col_len, d, chunk)
+    col_dims = (r_size, hl, cpd, col_len, d)
     unit = 8 * 2 * r_size * z_size
     col_half = padded(3 * d + d + 2 * ff, unit) // 2
     row_half = padded(4 * d + 8, unit) // 2
@@ -662,7 +677,7 @@
     recv = exchange(
         pack_tokens(row_dims, extra, tokens.reshape(c_size, rpd * wl, d), key_bias), "cols"
     )
-    ct_blocks = pack_cotangent(col_dims[:5], cotangent, key_bias)
+    ct_blocks = pack_cotangent(col_dims, cotangent, key_bias)
     ct_blocks = [ct_blocks[0]] + [swap(ct_blocks[s], "rows", s) for s in range(1, r_size)]
 
     y_send, qkv1, o1, p1 = row_forward(row_dims, rpd, recv, gain_row[None], w_qkv_row, w_out_row)
@@ -674,7 +689,7 @@
     dy_wire = exchange(dy_send.reshape(y_send.shape), ALL)
 
     col_blocks = weight_grads(
-        scale, r_size, 2 * col_half, 4, ((h2, dqkv2), (o2, dy2), (h3, du), (act, ct_cols))
+        scale, r_size, 2 * col_half, 2, ((h2, dqkv2), (o2, dy2), (h3, du), (act, ct_cols))
     )
     col_sum = add(
         [col_blocks[0]] + [swap(col_blocks[s], "rows", s) for s in range(1, r_size)]

time: 161 us -> 156 us (0.969)
  Pallas kernels: 49.3 us -> 44.6 us
    pallas_call x3, Pallas kernels: 34.7 us -> 30.5 us  [the longest x1 16.3 us: column_stage(): pl.pallas_call(functools.partial(column_kernel, dims), out_specs=[pl.Bloc...]
  transfers between devices with their start and end apart: 24 -> 24, of which waited for: 16 -> 15; matrix products, arithmetic and copies ran while one was open for 0% -> 0% of each run, Pallas kernels for 11% -> 11%
where the time goes in v4:
time: 156 us
  waiting for transfers between devices  50 us (32%)
  Pallas kernels  44.6 us (29%)
  starting transfers between devices  33.7 us (22%)
  blocking collectives  22.5 us (14%)
  local copies, waits for them, and re-layouts  3.45 us (2%)
    ppermute x21, waiting for transfers between devices, swap(): return lax.ppermute(x, axis, [(i, i ^ step) for i in range(size)])  42.1 us
    ppermute x21, starting transfers between devices, swap(): return lax.ppermute(x, axis, [(i, i ^ step) for i in range(size)])  23.2 us
    all_to_all x1, blocking collectives, exchange(): return lax.all_to_all(x, axes, split_axis=0, concat_axis=0, tiled=True)  22.5 us
    pallas_call x1, Pallas kernels, column_stage(): pl.pallas_call(functools.partial(column_kernel, dims), out_specs=[pl.Bloc...  16.3 us
    all_to_all x3, starting transfers between devices, exchange(): return lax.all_to_all(x, axes, split_axis=0, concat_axis=0, tiled=True)  10.5 us
    pallas_call x1, Pallas kernels, row_backward(): pl.pallas_call(functools.partial(row_backward_kernel, dims), grid=(rpd //...  8.36 us
    all_to_all x3, waiting for transfers between devices, exchange(): return lax.all_to_all(x, axes, split_axis=0, concat_axis=0, tiled=True)  7.97 us
    pallas_call x1, Pallas kernels, weight_grads(): pl.pallas_call(functools.partial(weight_grad_kernel, scale, n_out), grid=...  6 us
  transfers between devices with their start and end apart: 24, of which 15 were waited for; matrix products, arithmetic and copies ran while one was open for 0% of the time, Pallas kernels for 11%

profile of v4, /device:TPU:0, one launch (start us, length us, event | category | flops | bytes accessed | tf_op | source)
XLA Modules:
  0.0 155.8 jit_solution(10554918069874109516)
XLA Ops:
  0.6 2.0 %pack_tokens.1 = bf16[8,136,256]{2,1,0:T(8,128)(2,1)} custom-call(bf16[8,128,256]{2,1,0:T(8,128)(2,1)} %bitcast.58, bf16[32,32]{1,0:T(8,128)(2,1)} %b_ref.3), custom_call_target="tpu_custom_call" | custom-call | tf_op jit(solution)/shard_map/pack_tokens/pallas_call | solution.py:581
  2.6 22.5 %all_to_all.20.x_ref.b_ref = bf16[8,136,256]{2,1,0:T(8,128)(2,1)} all-to-all(bf16[8,136,256]{2,1,0:T(8,128)(2,1)} %pack_tokens.1), channel_id=1, replica_groups=mesh['rows'=4,'cols'=8] {'cols'}, dimensions={0} | all-to-all | bytes 1114112 | tf_op jit(solution)/shard_map/all_to_all | solution.py:626
  25.1 5.8 %row_forward.1 = (bf16[32,4,8,256]{3,2,1,0:T(8,128)(2,1)}, bf16[4,256,768]{2,1,0:T(8,128)(2,1)}, bf16[4,256,256]{2,1,0:T(8,128)(2,1)}, bf16[4,4,256,256]{3,2,1,0:T(8,128)(2,1)}) custom-call(bf16[8,136,256]{2,1,0:T(8,128)(2,1)} %all_to_all.20.x_ref.b_ref, bf16[8,136,256]{2,1,0:T(8,128)(2,1)} %all_to_all.20.x_ref.b_ref, f32[1,256]{1,0:T(1,128)} %bitcast.67, ...), custom_call_target="tpu_custom_call" | custom-call | tf_op jit(solution)/shard_map/row_forward/pallas_call | solution.py:486
  30.9 3.5 %all-to-all-start.1 = ((bf16[32,4,8,256]{3,2,1,0:T(8,128)(2,1)}), bf16[32,4,8,256]{3,2,1,0:T(8,128)(2,1)S(1)}, u32[]{:S(2)}, u32[]{:S(2)}) async-start(bf16[32,4,8,256]{3,2,1,0:T(8,128)(2,1)} %get-tuple-element.47), calls=%async_computation.1 | async-start | bytes 1048576 | tf_op jit(solution)/shard_map/all_to_all | solution.py:626
  34.4 2.3 %pack_cotangent.1 = (bf16[264,256]{1,0:T(8,128)(2,1)}, bf16[264,256]{1,0:T(8,128)(2,1)}, bf16[264,256]{1,0:T(8,128)(2,1)}, bf16[264,256]{1,0:T(8,128)(2,1)}) custom-call(bf16[32,32,256]{2,1,0:T(8,128)(2,1)} %ct_ref.1, bf16[32,32]{1,0:T(8,128)(2,1)} %b_ref.3), custom_call_target="tpu_custom_call" | custom-call | tf_op jit(solution)/shard_map/pack_cotangent/pallas_call | solution.py:592
  36.7 1.8 %collective-permute-start = (bf16[264,256]{1,0:T(8,128)(2,1)}, bf16[264,256]{1,0:T(8,128)(2,1)S(1)}, u32[]{:S(2)}, u32[]{:S(2)}) collective-permute-start(bf16[264,256]{1,0:T(8,128)(2,1)} %get-tuple-element.49), channel_id=1, source_target_pairs={{0,8},{8,0},{16,24},{24,16},{1,9},{9,1},{17,25},{25,17},{2,10},{10... | collective-permute-start | bytes 405512 | tf_op jit(solution)/shard_map/ppermute | solution.py:631
  38.5 1.5 collective-permute-start.1
  40.0 0.2 collective-permute-start.2
  40.2 4.6 %collective-permute-done.refs_2_ = bf16[264,256]{1,0:T(8,128)(2,1)S(1)} collective-permute-done((bf16[264,256]{1,0:T(8,128)(2,1)}, bf16[264,256]{1,0:T(8,128)(2,1)S(1)}, u32[]{:S(2)}, u32[]{:S(2)}) %collective-permute-start) | collective-permute-done | bytes 135200 | tf_op jit(solution)/shard_map/ppermute | solution.py:631
  44.8 2.8 %collective-permute-done.1.refs_3_ = bf16[264,256]{1,0:T(8,128)(2,1)S(1)} collective-permute-done((bf16[264,256]{1,0:T(8,128)(2,1)}, bf16[264,256]{1,0:T(8,128)(2,1)S(1)}, u32[]{:S(2)}, u32[]{:S(2)}) %collective-permute-start.1) | collective-permute-done | bytes 135200 | tf_op jit(solution)/shard_map/ppermute | solution.py:631
  47.6 2.1 %collective-permute-done.2.refs_4_ = bf16[264,256]{1,0:T(8,128)(2,1)S(1)} collective-permute-done((bf16[264,256]{1,0:T(8,128)(2,1)}, bf16[264,256]{1,0:T(8,128)(2,1)S(1)}, u32[]{:S(2)}, u32[]{:S(2)}) %collective-permute-start.2) | collective-permute-done | bytes 135200 | tf_op jit(solution)/shard_map/ppermute | solution.py:631
  49.8 1.0 all-to-all-done.1
  50.8 0.8 copy-done.2
  51.6 16.3 %column_stage.1 = (bf16[1024,256]{1,0:T(8,128)(2,1)}, bf16[1024,256]{1,0:T(8,128)(2,1)}, bf16[1024,768]{1,0:T(8,128)(2,1)}, bf16[1024,256]{1,0:T(8,128)(2,1)}, b...) custom-call(bf16[1024,256]{1,0:T(8,128)(2,1)} %bitcast.48, ...), custom_call_target="tpu_custom_call" | custom-call | tf_op jit(solution)/shard_map/column_stage/pallas_call | solution.py:558
  67.9 3.2 %all-to-all-start.2 = ((bf16[32,4,8,256]{3,2,1,0:T(8,128)(2,1)}), bf16[32,4,8,256]{3,2,1,0:T(8,128)(2,1)S(1)}, u32[]{:S(2)}, u32[]{:S(2)}) async-start(bf16[32,4,8,256]{3,2,1,0:T(8,128)(2,1)} %bitcast.59), calls=%async_computation.2 | async-start | bytes 1048576 | tf_op jit(solution)/shard_map/all_to_all | solution.py:626
  71.1 6.0 %weight_grads.1 = (bf16[768,256]{1,0:T(8,128)(2,1)}, bf16[768,256]{1,0:T(8,128)(2,1)}, bf16[768,256]{1,0:T(8,128)(2,1)}, bf16[768,256]{1,0:T(8,128)(2,1)}) custom-call(bf16[1024,256]{1,0:T(8,128)(2,1)} %get-tuple-element.52.refs_0_, bf16[1024,768]{1,0:T(8,128)(2,1)} %get-tuple-element.53.refs_1_, bf16[1024,256]{1,0:T(8,128)(2,1)} %get-tuple-element.54.refs_2_, ...), custom_call_target="tpu_custom_call" | custom-call | tf_op jit(solution)/shard_map/weight_grads/pallas_call | solution.py:604
  77.1 1.8 %collective-permute-start.3 = (bf16[768,256]{1,0:T(8,128)(2,1)}, bf16[768,256]{1,0:T(8,128)(2,1)S(1)}, u32[]{:S(2)}, u32[]{:S(2)}) collective-permute-start(bf16[768,256]{1,0:T(8,128)(2,1)} %get-tuple-element.61), channel_id=1, source_target_pairs={{0,8},{8,0},{16,24},{24,16},{1,9},{9,1},{17,25},{25,17},{2,10},{10... | collective-permute-start | bytes 1179656 | tf_op jit(solution)/shard_map/ppermute | solution.py:631
  78.8 1.5 collective-permute-start.4
  80.3 0.3 collective-permute-start.5
  80.6 6.9 %all-to-all-done.2.dy_ref = bf16[32,4,8,256]{3,2,1,0:T(8,128)(2,1)S(1)} async-done(((bf16[32,4,8,256]{3,2,1,0:T(8,128)(2,1)}), bf16[32,4,8,256]{3,2,1,0:T(8,128)(2,1)S(1)}, u32[]{:S(2)}, u32[]{:S(2)}) %all-to-all-start.2) | async-done | bytes 524320 | tf_op jit(solution)/shard_map/all_to_all | solution.py:626
  87.5 0.8 copy-done.1
  88.3 8.4 %row_backward.1 = (bf16[8,128,256]{2,1,0:T(8,128)(2,1)}, bf16[640,256]{1,0:T(8,128)(2,1)}, bf16[640,256]{1,0:T(8,128)(2,1)}) custom-call(bf16[8,136,256]{2,1,0:T(8,128)(2,1)} %all_to_all.20.x_ref.b_ref, bf16[32,4,8,256]{3,2,1,0:T(8,128)(2,1)} %copy-done.1, bf16[4,256,768]{2,1,0:T(8,128)(2,1)} %get-tuple-element.65.qkv_ref, ...), custom_call_target="tpu_custom_call" | custom-call | tf_op jit(solution)/shard_map/row_backward/pallas_call | solution.py:517
  96.7 3.3 %collective-permute-done.4 = bf16[768,256]{1,0:T(8,128)(2,1)S(1)} collective-permute-done((bf16[768,256]{1,0:T(8,128)(2,1)}, bf16[768,256]{1,0:T(8,128)(2,1)S(1)}, u32[]{:S(2)}, u32[]{:S(2)}) %collective-permute-start.4) | collective-permute-done | bytes 393248 | tf_op jit(solution)/shard_map/ppermute | solution.py:631
  100.0 0.2 add_convert_fusion
  100.4 3.9 %all-to-all-start.3 = ((bf16[8,128,256]{2,1,0:T(8,128)(2,1)}), bf16[8,128,256]{2,1,0:T(8,128)(2,1)S(1)}, u32[]{:S(2)}, u32[]{:S(2)}) async-start(bf16[8,128,256]{2,1,0:T(8,128)(2,1)} %get-tuple-element.72), calls=%async_computation.3 | async-start | bytes 1048576 | tf_op jit(solution)/shard_map/all_to_all | solution.py:626
  104.4 1.4 collective-permute-start.10
  105.8 1.4 collective-permute-start.8
  107.2 0.7 collective-permute-start.9
  108.0 2.6 %collective-permute-done.10 = bf16[160,256]{1,0:T(8,128)(2,1)S(1)} collective-permute-done((bf16[160,256]{1,0:T(8,128)(2,1)S(1)}, bf16[160,256]{1,0:T(8,128)(2,1)S(1)}, u32[]{:S(2)}, u32[]{:S(2)}) %collective-permute-start.10) | collective-permute-done | bytes 81952 | tf_op jit(solution)/shard_map/ppermute | solution.py:631
  110.6 1.2 collective-permute-done.8
  112.0 1.9 %collective-permute-start.11 = (bf16[136,256]{1,0:T(8,128)(2,1)S(1)}, bf16[136,256]{1,0:T(8,128)(2,1)S(1)}, u32[]{:S(2)}, u32[]{:S(2)}) collective-permute-start(bf16[136,256]{1,0:T(8,128)(2,1)S(1)} %get-tuple-element.87), channel_id=1, source_target_pairs={{0,2},{1,3},{2,0},{3,1},{4,6},{5,7},{6,4},{7,5},{8,10},{9,11},{10,... | collective-permute-start | bytes 208904 | tf_op jit(solution)/shard_map/ppermute | solution.py:631
  113.9 2.4 %collective-permute-start.12 = (bf16[136,256]{1,0:T(8,128)(2,1)S(1)}, bf16[136,256]{1,0:T(8,128)(2,1)S(1)}, u32[]{:S(2)}, u32[]{:S(2)}) collective-permute-start(bf16[136,256]{1,0:T(8,128)(2,1)S(1)} %get-tuple-element.88), channel_id=1, source_target_pairs={{0,4},{1,5},{2,6},{3,7},{4,0},{5,1},{6,2},{7,3},{8,12},{9,13},{10,... | collective-permute-start | bytes 208904 | tf_op jit(solution)/shard_map/ppermute | solution.py:631
  116.3 0.2 collective-permute-start.13
  116.5 0.7 collective-permute-done.11
  117.2 7.4 %collective-permute-done.12 = bf16[136,256]{1,0:T(8,128)(2,1)S(1)} collective-permute-done((bf16[136,256]{1,0:T(8,128)(2,1)S(1)}, bf16[136,256]{1,0:T(8,128)(2,1)S(1)}, u32[]{:S(2)}, u32[]{:S(2)}) %collective-permute-start.12) | collective-permute-done | bytes 69664 | tf_op jit(solution)/shard_map/ppermute | solution.py:631
  124.6 1.6 %collective-permute-start.14 = (bf16[136,256]{1,0:T(8,128)(2,1)S(1)}, bf16[136,256]{1,0:T(8,128)(2,1)S(1)}, u32[]{:S(2)}, u32[]{:S(2)}) collective-permute-start(bf16[136,256]{1,0:T(8,128)(2,1)S(1)} %fusion.6), channel_id=1, source_target_pairs={{0,2},{1,3},{2,0},{3,1},{4,6},{5,7},{6,4},{7,5},{8,10},{9,11},{10,... | collective-permute-start | bytes 208904 | tf_op jit(solution)/shard_map/ppermute | solution.py:631
  126.2 2.8 %collective-permute-start.16 = (bf16[136,256]{1,0:T(8,128)(2,1)S(1)}, bf16[136,256]{1,0:T(8,128)(2,1)S(1)}, u32[]{:S(2)}, u32[]{:S(2)}) collective-permute-start(bf16[136,256]{1,0:T(8,128)(2,1)S(1)} %fusion.6), channel_id=1, source_target_pairs={{0,6},{1,7},{2,4},{3,5},{4,2},{5,3},{6,0},{7,1},{8,14},{9,15},{10,... | collective-permute-start | bytes 208904 | tf_op jit(solution)/shard_map/ppermute | solution.py:631
  129.0 5.1 %collective-permute-done.15 = bf16[136,256]{1,0:T(8,128)(2,1)S(1)} collective-permute-done((bf16[136,256]{1,0:T(8,128)(2,1)S(1)}, bf16[136,256]{1,0:T(8,128)(2,1)S(1)}, u32[]{:S(2)}, u32[]{:S(2)}) %collective-permute-start.15) | collective-permute-done | bytes 69664 | tf_op jit(solution)/shard_map/ppermute | solution.py:631
  134.2 1.2 collective-permute-start.17
  135.4 0.9 collective-permute-start.18
  136.2 1.5 collective-permute-start.19
  137.7 5.5 %collective-permute-done.17 = bf16[4,136,256]{2,1,0:T(8,128)(2,1)S(1)} collective-permute-done((bf16[4,136,256]{2,1,0:T(8,128)(2,1)S(1)}, bf16[4,136,256]{2,1,0:T(8,128)(2,1)S(1)}, u32[]{:S(2)}, u32[]{:S(2)}) %collective-permute-start.17) | collective-permute-done | bytes 278560 | tf_op jit(solution)/shard_map/ppermute | solution.py:631
  143.2 3.9 %collective-permute-done.18 = bf16[4,136,256]{2,1,0:T(8,128)(2,1)S(1)} collective-permute-done((bf16[4,136,256]{2,1,0:T(8,128)(2,1)S(1)}, bf16[4,136,256]{2,1,0:T(8,128)(2,1)S(1)}, u32[]{:S(2)}, u32[]{:S(2)}) %collective-permute-start.18) | collective-permute-done | bytes 278560 | tf_op jit(solution)/shard_map/ppermute | solution.py:631
  147.1 0.1 pad_maximum_fusion.own_ref
  147.4 2.7 %collective-permute-done.20.got_ref = bf16[4,4,136,256]{3,2,1,0:T(8,128)(2,1)S(1)} collective-permute-done((bf16[4,4,136,256]{3,2,1,0:T(8,128)(2,1)S(1)}, bf16[4,4,136,256]{3,2,1,0:T(8,128)(2,1)S(1)}, u32[]{:S(2)}, u32[]{:S(2)}) %collective-permute-start.20) | collective-permute-done | bytes 1114144 | tf_op jit(solution)/shard_map/ppermute | solution.py:631
  150.1 1.0 copy-done.3
  151.1 3.9 %unpack.1 = (f32[1,256]{1,0:T(1,128)}, f32[1,256]{1,0:T(1,128)}, f32[1,256]{1,0:T(1,128)}, f32[256,768]{1,0:T(8,128)}, f32[256,256]{1,0:T(8,128)}, /*index=5*/f3...) custom-call(bf16[4,4,136,256]{3,2,1,0:T(8,128)(2,1)} %copy-done, ...), custom_call_target="tpu_custom_call" | custom-call | tf_op jit(solution)/shard_map/unpack/pallas_call | solution.py:617
  155.0 0.8 copy.23
  (37 shorter events, 0.8 us)
Async XLA Ops:
  30.9 19.9 %all-to-all-start.1 = ((bf16[32,4,8,256]{3,2,1,0:T(8,128)(2,1)}), bf16[32,4,8,256]{3,2,1,0:T(8,128)(2,1)S(1)}, u32[]{:S(2)}, u32[]{:S(2)}) async-start(bf16[32,4,8,256]{3,2,1,0:T(8,128)(2,1)} %get-tuple-element.47), calls=%async_computation.1 | async-start | bytes 1048576 | tf_op jit(solution)/shard_map/all_to_all | solution.py:626
  36.7 8.1 %collective-permute-start = (bf16[264,256]{1,0:T(8,128)(2,1)}, bf16[264,256]{1,0:T(8,128)(2,1)S(1)}, u32[]{:S(2)}, u32[]{:S(2)}) collective-permute-start(bf16[264,256]{1,0:T(8,128)(2,1)} %get-tuple-element.49), channel_id=1, source_target_pairs={{0,8},{8,0},{16,24},{24,16},{1,9},{9,1},{17,25},{25,17},{2,10},{10... | collective-permute-start | bytes 405512 | tf_op jit(solution)/shard_map/ppermute | solution.py:631
  38.5 9.1 %collective-permute-start.1 = (bf16[264,256]{1,0:T(8,128)(2,1)}, bf16[264,256]{1,0:T(8,128)(2,1)S(1)}, u32[]{:S(2)}, u32[]{:S(2)}) collective-permute-start(bf16[264,256]{1,0:T(8,128)(2,1)} %get-tuple-element.50), channel_id=1, source_target_pairs={{0,16},{8,24},{16,0},{24,8},{1,17},{9,25},{17,1},{25,9},{2,18},{10... | collective-permute-start | bytes 405512 | tf_op jit(solution)/shard_map/ppermute | solution.py:631
  40.0 9.8 %collective-permute-start.2 = (bf16[264,256]{1,0:T(8,128)(2,1)}, bf16[264,256]{1,0:T(8,128)(2,1)S(1)}, u32[]{:S(2)}, u32[]{:S(2)}) collective-permute-start(bf16[264,256]{1,0:T(8,128)(2,1)} %get-tuple-element.51), channel_id=1, source_target_pairs={{0,24},{8,16},{16,8},{24,0},{1,25},{9,17},{17,9},{25,1},{2,26},{10... | collective-permute-start | bytes 405512 | tf_op jit(solution)/shard_map/ppermute | solution.py:631
  44.8 6.0 %copy-start.6 = (bf16[264,256]{1,0:T(8,128)(2,1)}, bf16[264,256]{1,0:T(8,128)(2,1)S(1)}, u32[]{:S(2)}) copy-start(bf16[264,256]{1,0:T(8,128)(2,1)S(1)} %collective-permute-done.refs_2_) | copy-start | bytes 405508
  47.6 3.2 %copy-start.7 = (bf16[264,256]{1,0:T(8,128)(2,1)}, bf16[264,256]{1,0:T(8,128)(2,1)S(1)}, u32[]{:S(2)}) copy-start(bf16[264,256]{1,0:T(8,128)(2,1)S(1)} %collective-permute-done.1.refs_3_) | copy-start | bytes 405508
  49.8 1.0 copy-start.8
  50.8 0.8 copy-start.2
  67.9 19.6 %all-to-all-start.2 = ((bf16[32,4,8,256]{3,2,1,0:T(8,128)(2,1)}), bf16[32,4,8,256]{3,2,1,0:T(8,128)(2,1)S(1)}, u32[]{:S(2)}, u32[]{:S(2)}) async-start(bf16[32,4,8,256]{3,2,1,0:T(8,128)(2,1)} %bitcast.59), calls=%async_computation.2 | async-start | bytes 1048576 | tf_op jit(solution)/shard_map/all_to_all | solution.py:626
  77.1 19.7 %collective-permute-start.3 = (bf16[768,256]{1,0:T(8,128)(2,1)}, bf16[768,256]{1,0:T(8,128)(2,1)S(1)}, u32[]{:S(2)}, u32[]{:S(2)}) collective-permute-start(bf16[768,256]{1,0:T(8,128)(2,1)} %get-tuple-element.61), channel_id=1, source_target_pairs={{0,8},{8,0},{16,24},{24,16},{1,9},{9,1},{17,25},{25,17},{2,10},{10... | collective-permute-start | bytes 1179656 | tf_op jit(solution)/shard_map/ppermute | solution.py:631
  78.8 21.2 %collective-permute-start.4 = (bf16[768,256]{1,0:T(8,128)(2,1)}, bf16[768,256]{1,0:T(8,128)(2,1)S(1)}, u32[]{:S(2)}, u32[]{:S(2)}) collective-permute-start(bf16[768,256]{1,0:T(8,128)(2,1)} %get-tuple-element.62), channel_id=1, source_target_pairs={{0,16},{8,24},{16,0},{24,8},{1,17},{9,25},{17,1},{25,9},{2,18},{10... | collective-permute-start | bytes 1179656 | tf_op jit(solution)/shard_map/ppermute | solution.py:631
  80.3 19.7 %collective-permute-start.5 = (bf16[768,256]{1,0:T(8,128)(2,1)}, bf16[768,256]{1,0:T(8,128)(2,1)S(1)}, u32[]{:S(2)}, u32[]{:S(2)}) collective-permute-start(bf16[768,256]{1,0:T(8,128)(2,1)} %get-tuple-element.63), channel_id=1, source_target_pairs={{0,24},{8,16},{16,8},{24,0},{1,25},{9,17},{17,9},{25,1},{2,26},{10... | collective-permute-start | bytes 1179656 | tf_op jit(solution)/shard_map/ppermute | solution.py:631
  87.5 0.8 copy-start.1
  88.3 11.7 %copy-start.4 = (bf16[768,256]{1,0:T(8,128)(2,1)S(1)}, bf16[768,256]{1,0:T(8,128)(2,1)}, u32[]{:S(2)}) copy-start(bf16[768,256]{1,0:T(8,128)(2,1)} %get-tuple-element.60) | copy-start | bytes 1179652
  96.7 7.6 %collective-permute-start.7 = (bf16[640,256]{1,0:T(8,128)(2,1)}, bf16[640,256]{1,0:T(8,128)(2,1)S(1)}, u32[]{:S(2)}, u32[]{:S(2)}) collective-permute-start(bf16[640,256]{1,0:T(8,128)(2,1)} %get-tuple-element.71), channel_id=1, source_target_pairs={{0,1},{1,0},{2,3},{3,2},{4,5},{5,4},{6,7},{7,6},{8,9},{9,8},{10,11... | collective-permute-start | bytes 983048 | tf_op jit(solution)/shard_map/ppermute | solution.py:631
  100.2 4.0 %copy-start.5 = (bf16[640,256]{1,0:T(8,128)(2,1)S(1)}, bf16[640,256]{1,0:T(8,128)(2,1)}, u32[]{:S(2)}) copy-start(bf16[640,256]{1,0:T(8,128)(2,1)} %get-tuple-element.70) | copy-start | bytes 983044
  100.3 7.6 %collective-permute-start.6 = (bf16[384,256]{1,0:T(8,128)(2,1)S(1)}, bf16[384,256]{1,0:T(8,128)(2,1)S(1)}, u32[]{:S(2)}, u32[]{:S(2)}) collective-permute-start(bf16[384,256]{1,0:T(8,128)(2,1)S(1)} %dynamic-slice_bitcast_fusion), channel_id=1, source_target_pairs={{0,1},{1,0},{2,3},{3,2},{4,5},{5,4},{6,7},{7,6},{8,9},{9,8},{10,11... | collective-permute-start | bytes 589832 | tf_op jit(solution)/shard_map/ppermute | solution.py:631
  100.4 33.8 %all-to-all-start.3 = ((bf16[8,128,256]{2,1,0:T(8,128)(2,1)}), bf16[8,128,256]{2,1,0:T(8,128)(2,1)S(1)}, u32[]{:S(2)}, u32[]{:S(2)}) async-start(bf16[8,128,256]{2,1,0:T(8,128)(2,1)} %get-tuple-element.72), calls=%async_computation.3 | async-start | bytes 1048576 | tf_op jit(solution)/shard_map/all_to_all | solution.py:626
  104.4 6.2 %collective-permute-start.10 = (bf16[160,256]{1,0:T(8,128)(2,1)S(1)}, bf16[160,256]{1,0:T(8,128)(2,1)S(1)}, u32[]{:S(2)}, u32[]{:S(2)}) collective-permute-start(bf16[160,256]{1,0:T(8,128)(2,1)S(1)} %get-tuple-element.85), channel_id=1, source_target_pairs={{0,24},{8,16},{16,8},{24,0},{1,25},{9,17},{17,9},{25,1},{2,26},{10... | collective-permute-start | bytes 245768 | tf_op jit(solution)/shard_map/ppermute | solution.py:631
  105.8 6.0 %collective-permute-start.8 = (bf16[160,256]{1,0:T(8,128)(2,1)S(1)}, bf16[160,256]{1,0:T(8,128)(2,1)S(1)}, u32[]{:S(2)}, u32[]{:S(2)}) collective-permute-start(bf16[160,256]{1,0:T(8,128)(2,1)S(1)} %get-tuple-element.84), channel_id=1, source_target_pairs={{0,8},{8,0},{16,24},{24,16},{1,9},{9,1},{17,25},{25,17},{2,10},{10... | collective-permute-start | bytes 245768 | tf_op jit(solution)/shard_map/ppermute | solution.py:631
  107.2 4.7 %collective-permute-start.9 = (bf16[160,256]{1,0:T(8,128)(2,1)S(1)}, bf16[160,256]{1,0:T(8,128)(2,1)S(1)}, u32[]{:S(2)}, u32[]{:S(2)}) collective-permute-start(bf16[160,256]{1,0:T(8,128)(2,1)S(1)} %get-tuple-element.86), channel_id=1, source_target_pairs={{0,16},{8,24},{16,0},{24,8},{1,17},{9,25},{17,1},{25,9},{2,18},{10... | collective-permute-start | bytes 245768 | tf_op jit(solution)/shard_map/ppermute | solution.py:631
  112.0 5.1 %collective-permute-start.11 = (bf16[136,256]{1,0:T(8,128)(2,1)S(1)}, bf16[136,256]{1,0:T(8,128)(2,1)S(1)}, u32[]{:S(2)}, u32[]{:S(2)}) collective-permute-start(bf16[136,256]{1,0:T(8,128)(2,1)S(1)} %get-tuple-element.87), channel_id=1, source_target_pairs={{0,2},{1,3},{2,0},{3,1},{4,6},{5,7},{6,4},{7,5},{8,10},{9,11},{10,... | collective-permute-start | bytes 208904 | tf_op jit(solution)/shard_map/ppermute | solution.py:631
  113.9 10.6 %collective-permute-start.12 = (bf16[136,256]{1,0:T(8,128)(2,1)S(1)}, bf16[136,256]{1,0:T(8,128)(2,1)S(1)}, u32[]{:S(2)}, u32[]{:S(2)}) collective-permute-start(bf16[136,256]{1,0:T(8,128)(2,1)S(1)} %get-tuple-element.88), channel_id=1, source_target_pairs={{0,4},{1,5},{2,6},{3,7},{4,0},{5,1},{6,2},{7,3},{8,12},{9,13},{10,... | collective-permute-start | bytes 208904 | tf_op jit(solution)/shard_map/ppermute | solution.py:631
  116.3 8.2 %collective-permute-start.13 = (bf16[136,256]{1,0:T(8,128)(2,1)S(1)}, bf16[136,256]{1,0:T(8,128)(2,1)S(1)}, u32[]{:S(2)}, u32[]{:S(2)}) collective-permute-start(bf16[136,256]{1,0:T(8,128)(2,1)S(1)} %get-tuple-element.89), channel_id=1, source_target_pairs={{0,6},{1,7},{2,4},{3,5},{4,2},{5,3},{6,0},{7,1},{8,14},{9,15},{10,... | collective-permute-start | bytes 208904 | tf_op jit(solution)/shard_map/ppermute | solution.py:631
  124.6 4.5 %collective-permute-start.14 = (bf16[136,256]{1,0:T(8,128)(2,1)S(1)}, bf16[136,256]{1,0:T(8,128)(2,1)S(1)}, u32[]{:S(2)}, u32[]{:S(2)}) collective-permute-start(bf16[136,256]{1,0:T(8,128)(2,1)S(1)} %fusion.6), channel_id=1, source_target_pairs={{0,2},{1,3},{2,0},{3,1},{4,6},{5,7},{6,4},{7,5},{8,10},{9,11},{10,... | collective-permute-start | bytes 208904 | tf_op jit(solution)/shard_map/ppermute | solution.py:631
  126.2 7.9 %collective-permute-start.15 = (bf16[136,256]{1,0:T(8,128)(2,1)S(1)}, bf16[136,256]{1,0:T(8,128)(2,1)S(1)}, u32[]{:S(2)}, u32[]{:S(2)}) collective-permute-start(bf16[136,256]{1,0:T(8,128)(2,1)S(1)} %fusion.6), channel_id=1, source_target_pairs={{0,4},{1,5},{2,6},{3,7},{4,0},{5,1},{6,2},{7,3},{8,12},{9,13},{10,... | collective-permute-start | bytes 208904 | tf_op jit(solution)/shard_map/ppermute | solution.py:631
  126.2 7.9 %collective-permute-start.16 = (bf16[136,256]{1,0:T(8,128)(2,1)S(1)}, bf16[136,256]{1,0:T(8,128)(2,1)S(1)}, u32[]{:S(2)}, u32[]{:S(2)}) collective-permute-start(bf16[136,256]{1,0:T(8,128)(2,1)S(1)} %fusion.6), channel_id=1, source_target_pairs={{0,6},{1,7},{2,4},{3,5},{4,2},{5,3},{6,0},{7,1},{8,14},{9,15},{10,... | collective-permute-start | bytes 208904 | tf_op jit(solution)/shard_map/ppermute | solution.py:631
  134.2 9.1 %collective-permute-start.17 = (bf16[4,136,256]{2,1,0:T(8,128)(2,1)S(1)}, bf16[4,136,256]{2,1,0:T(8,128)(2,1)S(1)}, u32[]{:S(2)}, u32[]{:S(2)}) collective-permute-start(bf16[4,136,256]{2,1,0:T(8,128)(2,1)S(1)} %pad_maximum_fusion.1), channel_id=1, source_target_pairs={{0,8},{8,0},{16,24},{24,16},{1,9},{9,1},{17,25},{25,17},{2,10},{10... | collective-permute-start | bytes 835592 | tf_op jit(solution)/shard_map/ppermute | solution.py:631
  135.4 11.8 %collective-permute-start.18 = (bf16[4,136,256]{2,1,0:T(8,128)(2,1)S(1)}, bf16[4,136,256]{2,1,0:T(8,128)(2,1)S(1)}, u32[]{:S(2)}, u32[]{:S(2)}) collective-permute-start(bf16[4,136,256]{2,1,0:T(8,128)(2,1)S(1)} %pad_maximum_fusion.1), channel_id=1, source_target_pairs={{0,16},{8,24},{16,0},{24,8},{1,17},{9,25},{17,1},{25,9},{2,18},{10... | collective-permute-start | bytes 835592 | tf_op jit(solution)/shard_map/ppermute | solution.py:631
  136.2 10.9 %collective-permute-start.19 = (bf16[4,136,256]{2,1,0:T(8,128)(2,1)S(1)}, bf16[4,136,256]{2,1,0:T(8,128)(2,1)S(1)}, u32[]{:S(2)}, u32[]{:S(2)}) collective-permute-start(bf16[4,136,256]{2,1,0:T(8,128)(2,1)S(1)} %pad_maximum_fusion.1), channel_id=1, source_target_pairs={{0,24},{8,16},{16,8},{24,0},{1,25},{9,17},{17,9},{25,1},{2,26},{10... | collective-permute-start | bytes 835592 | tf_op jit(solution)/shard_map/ppermute | solution.py:631
  147.3 2.8 %copy-start = (bf16[4,4,136,256]{3,2,1,0:T(8,128)(2,1)}, bf16[4,4,136,256]{3,2,1,0:T(8,128)(2,1)S(1)}, u32[]{:S(2)}) copy-start(bf16[4,4,136,256]{3,2,1,0:T(8,128)(2,1)S(1)} %pad_maximum_fusion.own_ref) | copy-start | bytes 3342340
  147.3 2.8 %collective-permute-start.20 = (bf16[4,4,136,256]{3,2,1,0:T(8,128)(2,1)S(1)}, bf16[4,4,136,256]{3,2,1,0:T(8,128)(2,1)S(1)}, u32[]{:S(2)}, u32[]{:S(2)}) collective-permute-start(bf16[4,4,136,256]{3,2,1,0:T(8,128)(2,1)S(1)} %pad_maximum_fusion.own_ref), channel_id=1, source_target_pairs={{0,1},{1,0},{2,3},{3,2},{4,5},{5,4},{6,7},{7,6},{8,9},{9,8},{10,11... | collective-permute-start | bytes 3342344 | tf_op jit(solution)/shard_map/ppermute | solution.py:631
  150.1 1.0 copy-start.3

commit v5 on v4

--- a/solution.py
+++ b/solution.py
@@ -315,10 +315,14 @@
                             row, size = row + part, size - part
 
 
-def unpack_kernel(dims, own_ref, got_ref, *out_refs):
+def unpack_kernel(dims, own_ref, got_ref, *refs):
     r_size, z_size, col_rows, row_rows, d, layout = dims
+    *out_refs, got_s, sem = refs
+    got_copy = pltpu.make_async_copy(got_ref, got_s, sem)
+    got_copy.start()
     r_at, c_at = lax.axis_index("rows"), lax.axis_index("cols")
     z_at, parity = lax.div(c_at, 2), lax.rem(c_at, 2)
+    halves = []
     for core in range(2):
         copies = []
         for r in range(r_size):
@@ -334,24 +338,30 @@
                             cut = slice(base + low - first, base + high - first)
                             to = slice(row0 + low - start, row0 + high - start)
                             copies.append((r, z, cut, which, to, slice(lane0, lane0 + d)))
-
-        def place(source):
-            for r, z, cut, which, to, lanes in copies:
-                s, t = jnp.bitwise_xor(r_at, r), jnp.bitwise_xor(z_at, z)
-                piece = source[s, t, cut, :].astype(F32)
-                if which < 0:
-                    for i in range(3):
-                        out_refs[i][...] = piece[i : i + 1]
-                else:
-                    out_refs[which][to, lanes] = piece
+        halves.append(copies)
+
+    def place(copies, source):
+        for r, z, cut, which, to, lanes in copies:
+            s, t = jnp.bitwise_xor(r_at, r), jnp.bitwise_xor(z_at, z)
+            piece = source[s, t, cut, :].astype(F32)
+            if which < 0:
+                for i in range(3):
+                    out_refs[i][...] = piece[i : i + 1]
+            else:
+                out_refs[which][to, lanes] = piece
+
+    for core in range(2):
 
         @pl.when(parity == core)
         def _():
-            place(own_ref)
+            place(halves[core], own_ref)
+
+    got_copy.wait()
+    for core in range(2):
 
         @pl.when(parity != core)
         def _():
-            place(got_ref)
+            place(halves[core], got_s)
 
 
 def column_kernel(
@@ -614,10 +624,14 @@
 
 
 def unpack(dims, own, got, shapes):
+    inside = pl.BlockSpec(memory_space=pltpu.VMEM)
     return pl.pallas_call(
         functools.partial(unpack_kernel, dims),
+        in_specs=[inside, pl.BlockSpec(memory_space=pltpu.HBM)],
+        out_specs=[inside] * len(shapes),
         out_shape=[jax.ShapeDtypeStruct(shape, F32) for shape in shapes],
-        compiler_params=pltpu.CompilerParams(vmem_limit_bytes=VMEM_LIMIT),
+        scratch_shapes=[pltpu.VMEM(got.shape, BF), pltpu.SemaphoreType.DMA],
+        compiler_params=pltpu.CompilerParams(vmem_limit_bytes=12 * 1024 * 1024),
         name="unpack",
     )(own, got)
 

time: 156 us -> 154 us (0.987)
    unnamed x19 -> x15, local copies, waits for them, and re-layouts: 3.4 us -> 2.39 us
where the time goes in v5:
time: 154 us; the launch traced here: 153 us
  waiting for transfers between devices  50 us (32%)
  Pallas kernels  43.2 us (28%)
  starting transfers between devices  33.8 us (22%)
  blocking collectives  22.5 us (15%)
  local copies, waits for them, and re-layouts  2.44 us (2%)
    ppermute x21, waiting for transfers between devices, swap(): return lax.ppermute(x, axis, [(i, i ^ step) for i in range(size)])  42 us
    ppermute x21, starting transfers between devices, swap(): return lax.ppermute(x, axis, [(i, i ^ step) for i in range(size)])  23.2 us
    all_to_all x1, blocking collectives, exchange(): return lax.all_to_all(x, axes, split_axis=0, concat_axis=0, tiled=True)  22.5 us
    pallas_call x1, Pallas kernels, column_stage(): pl.pallas_call(functools.partial(column_kernel, dims), out_specs=[pl.Bloc...  16.3 us
    all_to_all x3, starting transfers between devices, exchange(): return lax.all_to_all(x, axes, split_axis=0, concat_axis=0, tiled=True)  10.6 us
    pallas_call x1, Pallas kernels, row_backward(): pl.pallas_call(functools.partial(row_backward_kernel, dims), grid=(rpd //...  8.35 us
    all_to_all x3, waiting for transfers between devices, exchange(): return lax.all_to_all(x, axes, split_axis=0, concat_axis=0, tiled=True)  8 us
    pallas_call x1, Pallas kernels, weight_grads(): pl.pallas_call(functools.partial(weight_grad_kernel, scale, n_out), grid=...  5.98 us
  transfers between devices with their start and end apart: 24, of which 15 were waited for; matrix products, arithmetic and copies ran while one was open for 0% of the time, Pallas kernels for 11%

profile of v5, /device:TPU:0, one launch (start us, length us, event | category | flops | bytes accessed | tf_op | source)
XLA Modules:
  0.0 153.4 jit_solution(9127381384331497611)
XLA Ops:
  0.6 2.0 %pack_tokens.1 = bf16[8,136,256]{2,1,0:T(8,128)(2,1)} custom-call(bf16[8,128,256]{2,1,0:T(8,128)(2,1)} %bitcast.58, bf16[32,32]{1,0:T(8,128)(2,1)} %b_ref.3), custom_call_target="tpu_custom_call" | custom-call | tf_op jit(solution)/shard_map/pack_tokens/pallas_call | solution.py:591
  2.6 22.5 %all_to_all.20.x_ref.b_ref = bf16[8,136,256]{2,1,0:T(8,128)(2,1)} all-to-all(bf16[8,136,256]{2,1,0:T(8,128)(2,1)} %pack_tokens.1), channel_id=1, replica_groups=mesh['rows'=4,'cols'=8] {'cols'}, dimensions={0} | all-to-all | bytes 1114112 | tf_op jit(solution)/shard_map/all_to_all | solution.py:640
  25.1 5.8 %row_forward.1 = (bf16[32,4,8,256]{3,2,1,0:T(8,128)(2,1)}, bf16[4,256,768]{2,1,0:T(8,128)(2,1)}, bf16[4,256,256]{2,1,0:T(8,128)(2,1)}, bf16[4,4,256,256]{3,2,1,0:T(8,128)(2,1)}) custom-call(bf16[8,136,256]{2,1,0:T(8,128)(2,1)} %all_to_all.20.x_ref.b_ref, bf16[8,136,256]{2,1,0:T(8,128)(2,1)} %all_to_all.20.x_ref.b_ref, f32[1,256]{1,0:T(1,128)} %bitcast.67, ...), custom_call_target="tpu_custom_call" | custom-call | tf_op jit(solution)/shard_map/row_forward/pallas_call | solution.py:496
  30.9 3.5 %all-to-all-start.1 = ((bf16[32,4,8,256]{3,2,1,0:T(8,128)(2,1)}), bf16[32,4,8,256]{3,2,1,0:T(8,128)(2,1)S(1)}, u32[]{:S(2)}, u32[]{:S(2)}) async-start(bf16[32,4,8,256]{3,2,1,0:T(8,128)(2,1)} %get-tuple-element.47), calls=%async_computation.1 | async-start | bytes 1048576 | tf_op jit(solution)/shard_map/all_to_all | solution.py:640
  34.4 2.3 %pack_cotangent.1 = (bf16[264,256]{1,0:T(8,128)(2,1)}, bf16[264,256]{1,0:T(8,128)(2,1)}, bf16[264,256]{1,0:T(8,128)(2,1)}, bf16[264,256]{1,0:T(8,128)(2,1)}) custom-call(bf16[32,32,256]{2,1,0:T(8,128)(2,1)} %ct_ref.1, bf16[32,32]{1,0:T(8,128)(2,1)} %b_ref.3), custom_call_target="tpu_custom_call" | custom-call | tf_op jit(solution)/shard_map/pack_cotangent/pallas_call | solution.py:602
  36.7 1.8 %collective-permute-start = (bf16[264,256]{1,0:T(8,128)(2,1)}, bf16[264,256]{1,0:T(8,128)(2,1)S(1)}, u32[]{:S(2)}, u32[]{:S(2)}) collective-permute-start(bf16[264,256]{1,0:T(8,128)(2,1)} %get-tuple-element.49), channel_id=1, source_target_pairs={{0,8},{8,0},{16,24},{24,16},{1,9},{9,1},{17,25},{25,17},{2,10},{10... | collective-permute-start | bytes 405512 | tf_op jit(solution)/shard_map/ppermute | solution.py:645
  38.5 1.5 collective-permute-start.1
  40.0 0.2 collective-permute-start.2
  40.2 4.6 %collective-permute-done.refs_2_ = bf16[264,256]{1,0:T(8,128)(2,1)S(1)} collective-permute-done((bf16[264,256]{1,0:T(8,128)(2,1)}, bf16[264,256]{1,0:T(8,128)(2,1)S(1)}, u32[]{:S(2)}, u32[]{:S(2)}) %collective-permute-start) | collective-permute-done | bytes 135200 | tf_op jit(solution)/shard_map/ppermute | solution.py:645
  44.8 2.8 %collective-permute-done.1.refs_3_ = bf16[264,256]{1,0:T(8,128)(2,1)S(1)} collective-permute-done((bf16[264,256]{1,0:T(8,128)(2,1)}, bf16[264,256]{1,0:T(8,128)(2,1)S(1)}, u32[]{:S(2)}, u32[]{:S(2)}) %collective-permute-start.1) | collective-permute-done | bytes 135200 | tf_op jit(solution)/shard_map/ppermute | solution.py:645
  47.6 2.1 %collective-permute-done.2.refs_4_ = bf16[264,256]{1,0:T(8,128)(2,1)S(1)} collective-permute-done((bf16[264,256]{1,0:T(8,128)(2,1)}, bf16[264,256]{1,0:T(8,128)(2,1)S(1)}, u32[]{:S(2)}, u32[]{:S(2)}) %collective-permute-start.2) | collective-permute-done | bytes 135200 | tf_op jit(solution)/shard_map/ppermute | solution.py:645
  49.8 1.0 all-to-all-done.1
  50.8 0.8 copy-done.1
  51.6 16.3 %column_stage.1 = (bf16[1024,256]{1,0:T(8,128)(2,1)}, bf16[1024,256]{1,0:T(8,128)(2,1)}, bf16[1024,768]{1,0:T(8,128)(2,1)}, bf16[1024,256]{1,0:T(8,128)(2,1)}, b...) custom-call(bf16[1024,256]{1,0:T(8,128)(2,1)} %bitcast.48, ...), custom_call_target="tpu_custom_call" | custom-call | tf_op jit(solution)/shard_map/column_stage/pallas_call | solution.py:568
  67.9 3.2 %all-to-all-start.2 = ((bf16[32,4,8,256]{3,2,1,0:T(8,128)(2,1)}), bf16[32,4,8,256]{3,2,1,0:T(8,128)(2,1)S(1)}, u32[]{:S(2)}, u32[]{:S(2)}) async-start(bf16[32,4,8,256]{3,2,1,0:T(8,128)(2,1)} %bitcast.59), calls=%async_computation.2 | async-start | bytes 1048576 | tf_op jit(solution)/shard_map/all_to_all | solution.py:640
  71.1 6.0 %weight_grads.1 = (bf16[768,256]{1,0:T(8,128)(2,1)}, bf16[768,256]{1,0:T(8,128)(2,1)}, bf16[768,256]{1,0:T(8,128)(2,1)}, bf16[768,256]{1,0:T(8,128)(2,1)}) custom-call(bf16[1024,256]{1,0:T(8,128)(2,1)} %get-tuple-element.52.refs_0_, bf16[1024,768]{1,0:T(8,128)(2,1)} %get-tuple-element.53.refs_1_, bf16[1024,256]{1,0:T(8,128)(2,1)} %get-tuple-element.54.refs_2_, ...), custom_call_target="tpu_custom_call" | custom-call | tf_op jit(solution)/shard_map/weight_grads/pallas_call | solution.py:614
  77.1 1.8 %collective-permute-start.3 = (bf16[768,256]{1,0:T(8,128)(2,1)}, bf16[768,256]{1,0:T(8,128)(2,1)S(1)}, u32[]{:S(2)}, u32[]{:S(2)}) collective-permute-start(bf16[768,256]{1,0:T(8,128)(2,1)} %get-tuple-element.61), channel_id=1, source_target_pairs={{0,8},{8,0},{16,24},{24,16},{1,9},{9,1},{17,25},{25,17},{2,10},{10... | collective-permute-start | bytes 1179656 | tf_op jit(solution)/shard_map/ppermute | solution.py:645
  78.8 1.5 collective-permute-start.4
  80.3 0.3 collective-permute-start.5
  80.5 7.0 %all-to-all-done.2.dy_ref = bf16[32,4,8,256]{3,2,1,0:T(8,128)(2,1)S(1)} async-done(((bf16[32,4,8,256]{3,2,1,0:T(8,128)(2,1)}), bf16[32,4,8,256]{3,2,1,0:T(8,128)(2,1)S(1)}, u32[]{:S(2)}, u32[]{:S(2)}) %all-to-all-start.2) | async-done | bytes 524320 | tf_op jit(solution)/shard_map/all_to_all | solution.py:640
  87.5 0.8 copy-done
  88.3 8.4 %row_backward.1 = (bf16[8,128,256]{2,1,0:T(8,128)(2,1)}, bf16[640,256]{1,0:T(8,128)(2,1)}, bf16[640,256]{1,0:T(8,128)(2,1)}) custom-call(bf16[8,136,256]{2,1,0:T(8,128)(2,1)} %all_to_all.20.x_ref.b_ref, bf16[32,4,8,256]{3,2,1,0:T(8,128)(2,1)} %copy-done, bf16[4,256,768]{2,1,0:T(8,128)(2,1)} %get-tuple-element.65.qkv_ref, ...), custom_call_target="tpu_custom_call" | custom-call | tf_op jit(solution)/shard_map/row_backward/pallas_call | solution.py:527
  96.8 3.3 %collective-permute-done.4 = bf16[768,256]{1,0:T(8,128)(2,1)S(1)} collective-permute-done((bf16[768,256]{1,0:T(8,128)(2,1)}, bf16[768,256]{1,0:T(8,128)(2,1)S(1)}, u32[]{:S(2)}, u32[]{:S(2)}) %collective-permute-start.4) | collective-permute-done | bytes 393248 | tf_op jit(solution)/shard_map/ppermute | solution.py:645
  100.0 0.2 add_convert_fusion
  100.3 3.9 %all-to-all-start.3 = ((bf16[8,128,256]{2,1,0:T(8,128)(2,1)}), bf16[8,128,256]{2,1,0:T(8,128)(2,1)S(1)}, u32[]{:S(2)}, u32[]{:S(2)}) async-start(bf16[8,128,256]{2,1,0:T(8,128)(2,1)} %get-tuple-element.72), calls=%async_computation.3 | async-start | bytes 1048576 | tf_op jit(solution)/shard_map/all_to_all | solution.py:640
  104.4 1.4 collective-permute-start.10
  105.8 1.4 collective-permute-start.8
  107.2 0.7 collective-permute-start.9
  108.0 2.6 %collective-permute-done.10 = bf16[160,256]{1,0:T(8,128)(2,1)S(1)} collective-permute-done((bf16[160,256]{1,0:T(8,128)(2,1)S(1)}, bf16[160,256]{1,0:T(8,128)(2,1)S(1)}, u32[]{:S(2)}, u32[]{:S(2)}) %collective-permute-start.10) | collective-permute-done | bytes 81952 | tf_op jit(solution)/shard_map/ppermute | solution.py:645
  110.6 1.2 collective-permute-done.8
  111.8 0.1 collective-permute-done.9
  112.0 1.9 %collective-permute-start.11 = (bf16[136,256]{1,0:T(8,128)(2,1)S(1)}, bf16[136,256]{1,0:T(8,128)(2,1)S(1)}, u32[]{:S(2)}, u32[]{:S(2)}) collective-permute-start(bf16[136,256]{1,0:T(8,128)(2,1)S(1)} %get-tuple-element.87), channel_id=1, source_target_pairs={{0,2},{1,3},{2,0},{3,1},{4,6},{5,7},{6,4},{7,5},{8,10},{9,11},{10,... | collective-permute-start | bytes 208904 | tf_op jit(solution)/shard_map/ppermute | solution.py:645
  113.9 2.4 %collective-permute-start.12 = (bf16[136,256]{1,0:T(8,128)(2,1)S(1)}, bf16[136,256]{1,0:T(8,128)(2,1)S(1)}, u32[]{:S(2)}, u32[]{:S(2)}) collective-permute-start(bf16[136,256]{1,0:T(8,128)(2,1)S(1)} %get-tuple-element.88), channel_id=1, source_target_pairs={{0,4},{1,5},{2,6},{3,7},{4,0},{5,1},{6,2},{7,3},{8,12},{9,13},{10,... | collective-permute-start | bytes 208904 | tf_op jit(solution)/shard_map/ppermute | solution.py:645
  116.3 0.2 collective-permute-start.13
  116.5 0.7 collective-permute-done.11
  117.1 7.4 %collective-permute-done.12 = bf16[136,256]{1,0:T(8,128)(2,1)S(1)} collective-permute-done((bf16[136,256]{1,0:T(8,128)(2,1)S(1)}, bf16[136,256]{1,0:T(8,128)(2,1)S(1)}, u32[]{:S(2)}, u32[]{:S(2)}) %collective-permute-start.12) | collective-permute-done | bytes 69664 | tf_op jit(solution)/shard_map/ppermute | solution.py:645
  124.6 1.6 %collective-permute-start.14 = (bf16[136,256]{1,0:T(8,128)(2,1)S(1)}, bf16[136,256]{1,0:T(8,128)(2,1)S(1)}, u32[]{:S(2)}, u32[]{:S(2)}) collective-permute-start(bf16[136,256]{1,0:T(8,128)(2,1)S(1)} %fusion.6), channel_id=1, source_target_pairs={{0,2},{1,3},{2,0},{3,1},{4,6},{5,7},{6,4},{7,5},{8,10},{9,11},{10,... | collective-permute-start | bytes 208904 | tf_op jit(solution)/shard_map/ppermute | solution.py:645
  126.2 2.8 %collective-permute-start.16 = (bf16[136,256]{1,0:T(8,128)(2,1)S(1)}, bf16[136,256]{1,0:T(8,128)(2,1)S(1)}, u32[]{:S(2)}, u32[]{:S(2)}) collective-permute-start(bf16[136,256]{1,0:T(8,128)(2,1)S(1)} %fusion.6), channel_id=1, source_target_pairs={{0,6},{1,7},{2,4},{3,5},{4,2},{5,3},{6,0},{7,1},{8,14},{9,15},{10,... | collective-permute-start | bytes 208904 | tf_op jit(solution)/shard_map/ppermute | solution.py:645
  129.0 5.1 %collective-permute-done.15 = bf16[136,256]{1,0:T(8,128)(2,1)S(1)} collective-permute-done((bf16[136,256]{1,0:T(8,128)(2,1)S(1)}, bf16[136,256]{1,0:T(8,128)(2,1)S(1)}, u32[]{:S(2)}, u32[]{:S(2)}) %collective-permute-start.15) | collective-permute-done | bytes 69664 | tf_op jit(solution)/shard_map/ppermute | solution.py:645
  134.2 1.2 collective-permute-start.17
  135.4 0.8 collective-permute-start.18
  136.2 1.5 %collective-permute-start.19 = (bf16[4,136,256]{2,1,0:T(8,128)(2,1)S(1)}, bf16[4,136,256]{2,1,0:T(8,128)(2,1)S(1)}, u32[]{:S(2)}, u32[]{:S(2)}) collective-permute-start(bf16[4,136,256]{2,1,0:T(8,128)(2,1)S(1)} %pad_maximum_fusion.1), channel_id=1, source_target_pairs={{0,24},{8,16},{16,8},{24,0},{1,25},{9,17},{17,9},{25,1},{2,26},{10... | collective-permute-start | bytes 835592 | tf_op jit(solution)/shard_map/ppermute | solution.py:645
  137.7 5.5 %collective-permute-done.17 = bf16[4,136,256]{2,1,0:T(8,128)(2,1)S(1)} collective-permute-done((bf16[4,136,256]{2,1,0:T(8,128)(2,1)S(1)}, bf16[4,136,256]{2,1,0:T(8,128)(2,1)S(1)}, u32[]{:S(2)}, u32[]{:S(2)}) %collective-permute-start.17) | collective-permute-done | bytes 278560 | tf_op jit(solution)/shard_map/ppermute | solution.py:645
  143.2 3.9 %collective-permute-done.18 = bf16[4,136,256]{2,1,0:T(8,128)(2,1)S(1)} collective-permute-done((bf16[4,136,256]{2,1,0:T(8,128)(2,1)S(1)}, bf16[4,136,256]{2,1,0:T(8,128)(2,1)S(1)}, u32[]{:S(2)}, u32[]{:S(2)}) %collective-permute-start.18) | collective-permute-done | bytes 278560 | tf_op jit(solution)/shard_map/ppermute | solution.py:645
  147.1 0.1 pad_maximum_fusion.own_ref
  147.3 2.7 %collective-permute-done.20.got_ref = bf16[4,4,136,256]{3,2,1,0:T(8,128)(2,1)S(1)} collective-permute-done((bf16[4,4,136,256]{3,2,1,0:T(8,128)(2,1)S(1)}, bf16[4,4,136,256]{3,2,1,0:T(8,128)(2,1)S(1)}, u32[]{:S(2)}, u32[]{:S(2)}) %collective-permute-start.20) | collective-permute-done | bytes 1114144 | tf_op jit(solution)/shard_map/ppermute | solution.py:645
  150.1 2.5 %unpack.1 = (f32[1,256]{1,0:T(1,128)}, f32[1,256]{1,0:T(1,128)}, f32[1,256]{1,0:T(1,128)}, f32[256,768]{1,0:T(8,128)}, f32[256,256]{1,0:T(8,128)}, /*index=5*/f3...) custom-call(bf16[4,4,136,256]{3,2,1,0:T(8,128)(2,1)S(1)} %pad_maximum_fusion.own_ref, ...), custom_call_target="tpu_custom_call" | custom-call | tf_op jit(solution)/shard_map/unpack/pallas_call | solution.py:628
  152.6 0.8 copy.23
  (33 shorter events, 0.6 us)
Async XLA Ops:
  30.9 19.9 %all-to-all-start.1 = ((bf16[32,4,8,256]{3,2,1,0:T(8,128)(2,1)}), bf16[32,4,8,256]{3,2,1,0:T(8,128)(2,1)S(1)}, u32[]{:S(2)}, u32[]{:S(2)}) async-start(bf16[32,4,8,256]{3,2,1,0:T(8,128)(2,1)} %get-tuple-element.47), calls=%async_computation.1 | async-start | bytes 1048576 | tf_op jit(solution)/shard_map/all_to_all | solution.py:640
  36.7 8.1 %collective-permute-start = (bf16[264,256]{1,0:T(8,128)(2,1)}, bf16[264,256]{1,0:T(8,128)(2,1)S(1)}, u32[]{:S(2)}, u32[]{:S(2)}) collective-permute-start(bf16[264,256]{1,0:T(8,128)(2,1)} %get-tuple-element.49), channel_id=1, source_target_pairs={{0,8},{8,0},{16,24},{24,16},{1,9},{9,1},{17,25},{25,17},{2,10},{10... | collective-permute-start | bytes 405512 | tf_op jit(solution)/shard_map/ppermute | solution.py:645
  38.5 9.1 %collective-permute-start.1 = (bf16[264,256]{1,0:T(8,128)(2,1)}, bf16[264,256]{1,0:T(8,128)(2,1)S(1)}, u32[]{:S(2)}, u32[]{:S(2)}) collective-permute-start(bf16[264,256]{1,0:T(8,128)(2,1)} %get-tuple-element.50), channel_id=1, source_target_pairs={{0,16},{8,24},{16,0},{24,8},{1,17},{9,25},{17,1},{25,9},{2,18},{10... | collective-permute-start | bytes 405512 | tf_op jit(solution)/shard_map/ppermute | solution.py:645
  40.0 9.8 %collective-permute-start.2 = (bf16[264,256]{1,0:T(8,128)(2,1)}, bf16[264,256]{1,0:T(8,128)(2,1)S(1)}, u32[]{:S(2)}, u32[]{:S(2)}) collective-permute-start(bf16[264,256]{1,0:T(8,128)(2,1)} %get-tuple-element.51), channel_id=1, source_target_pairs={{0,24},{8,16},{16,8},{24,0},{1,25},{9,17},{17,9},{25,1},{2,26},{10... | collective-permute-start | bytes 405512 | tf_op jit(solution)/shard_map/ppermute | solution.py:645
  44.8 6.0 %copy-start.4 = (bf16[264,256]{1,0:T(8,128)(2,1)}, bf16[264,256]{1,0:T(8,128)(2,1)S(1)}, u32[]{:S(2)}) copy-start(bf16[264,256]{1,0:T(8,128)(2,1)S(1)} %collective-permute-done.refs_2_) | copy-start | bytes 405508
  47.6 3.2 %copy-start.5 = (bf16[264,256]{1,0:T(8,128)(2,1)}, bf16[264,256]{1,0:T(8,128)(2,1)S(1)}, u32[]{:S(2)}) copy-start(bf16[264,256]{1,0:T(8,128)(2,1)S(1)} %collective-permute-done.1.refs_3_) | copy-start | bytes 405508
  49.8 1.0 copy-start.6
  50.8 0.8 copy-start.1
  67.9 19.6 %all-to-all-start.2 = ((bf16[32,4,8,256]{3,2,1,0:T(8,128)(2,1)}), bf16[32,4,8,256]{3,2,1,0:T(8,128)(2,1)S(1)}, u32[]{:S(2)}, u32[]{:S(2)}) async-start(bf16[32,4,8,256]{3,2,1,0:T(8,128)(2,1)} %bitcast.59), calls=%async_computation.2 | async-start | bytes 1048576 | tf_op jit(solution)/shard_map/all_to_all | solution.py:640
  77.1 19.7 %collective-permute-start.3 = (bf16[768,256]{1,0:T(8,128)(2,1)}, bf16[768,256]{1,0:T(8,128)(2,1)S(1)}, u32[]{:S(2)}, u32[]{:S(2)}) collective-permute-start(bf16[768,256]{1,0:T(8,128)(2,1)} %get-tuple-element.61), channel_id=1, source_target_pairs={{0,8},{8,0},{16,24},{24,16},{1,9},{9,1},{17,25},{25,17},{2,10},{10... | collective-permute-start | bytes 1179656 | tf_op jit(solution)/shard_map/ppermute | solution.py:645
  78.8 21.2 %collective-permute-start.4 = (bf16[768,256]{1,0:T(8,128)(2,1)}, bf16[768,256]{1,0:T(8,128)(2,1)S(1)}, u32[]{:S(2)}, u32[]{:S(2)}) collective-permute-start(bf16[768,256]{1,0:T(8,128)(2,1)} %get-tuple-element.62), channel_id=1, source_target_pairs={{0,16},{8,24},{16,0},{24,8},{1,17},{9,25},{17,1},{25,9},{2,18},{10... | collective-permute-start | bytes 1179656 | tf_op jit(solution)/shard_map/ppermute | solution.py:645
  80.3 19.7 %collective-permute-start.5 = (bf16[768,256]{1,0:T(8,128)(2,1)}, bf16[768,256]{1,0:T(8,128)(2,1)S(1)}, u32[]{:S(2)}, u32[]{:S(2)}) collective-permute-start(bf16[768,256]{1,0:T(8,128)(2,1)} %get-tuple-element.63), channel_id=1, source_target_pairs={{0,24},{8,16},{16,8},{24,0},{1,25},{9,17},{17,9},{25,1},{2,26},{10... | collective-permute-start | bytes 1179656 | tf_op jit(solution)/shard_map/ppermute | solution.py:645
  87.5 0.8 copy-start
  88.3 11.7 %copy-start.2 = (bf16[768,256]{1,0:T(8,128)(2,1)S(1)}, bf16[768,256]{1,0:T(8,128)(2,1)}, u32[]{:S(2)}) copy-start(bf16[768,256]{1,0:T(8,128)(2,1)} %get-tuple-element.60) | copy-start | bytes 1179652
  96.7 7.6 %collective-permute-start.7 = (bf16[640,256]{1,0:T(8,128)(2,1)}, bf16[640,256]{1,0:T(8,128)(2,1)S(1)}, u32[]{:S(2)}, u32[]{:S(2)}) collective-permute-start(bf16[640,256]{1,0:T(8,128)(2,1)} %get-tuple-element.71), channel_id=1, source_target_pairs={{0,1},{1,0},{2,3},{3,2},{4,5},{5,4},{6,7},{7,6},{8,9},{9,8},{10,11... | collective-permute-start | bytes 983048 | tf_op jit(solution)/shard_map/ppermute | solution.py:645
  100.2 4.0 %copy-start.3 = (bf16[640,256]{1,0:T(8,128)(2,1)S(1)}, bf16[640,256]{1,0:T(8,128)(2,1)}, u32[]{:S(2)}) copy-start(bf16[640,256]{1,0:T(8,128)(2,1)} %get-tuple-element.70) | copy-start | bytes 983044
  100.3 7.7 %collective-permute-start.6 = (bf16[384,256]{1,0:T(8,128)(2,1)S(1)}, bf16[384,256]{1,0:T(8,128)(2,1)S(1)}, u32[]{:S(2)}, u32[]{:S(2)}) collective-permute-start(bf16[384,256]{1,0:T(8,128)(2,1)S(1)} %dynamic-slice_bitcast_fusion), channel_id=1, source_target_pairs={{0,1},{1,0},{2,3},{3,2},{4,5},{5,4},{6,7},{7,6},{8,9},{9,8},{10,11... | collective-permute-start | bytes 589832 | tf_op jit(solution)/shard_map/ppermute | solution.py:645
  100.3 33.8 %all-to-all-start.3 = ((bf16[8,128,256]{2,1,0:T(8,128)(2,1)}), bf16[8,128,256]{2,1,0:T(8,128)(2,1)S(1)}, u32[]{:S(2)}, u32[]{:S(2)}) async-start(bf16[8,128,256]{2,1,0:T(8,128)(2,1)} %get-tuple-element.72), calls=%async_computation.3 | async-start | bytes 1048576 | tf_op jit(solution)/shard_map/all_to_all | solution.py:640
  104.4 6.2 %collective-permute-start.10 = (bf16[160,256]{1,0:T(8,128)(2,1)S(1)}, bf16[160,256]{1,0:T(8,128)(2,1)S(1)}, u32[]{:S(2)}, u32[]{:S(2)}) collective-permute-start(bf16[160,256]{1,0:T(8,128)(2,1)S(1)} %get-tuple-element.85), channel_id=1, source_target_pairs={{0,24},{8,16},{16,8},{24,0},{1,25},{9,17},{17,9},{25,1},{2,26},{10... | collective-permute-start | bytes 245768 | tf_op jit(solution)/shard_map/ppermute | solution.py:645
  105.8 6.0 %collective-permute-start.8 = (bf16[160,256]{1,0:T(8,128)(2,1)S(1)}, bf16[160,256]{1,0:T(8,128)(2,1)S(1)}, u32[]{:S(2)}, u32[]{:S(2)}) collective-permute-start(bf16[160,256]{1,0:T(8,128)(2,1)S(1)} %get-tuple-element.84), channel_id=1, source_target_pairs={{0,8},{8,0},{16,24},{24,16},{1,9},{9,1},{17,25},{25,17},{2,10},{10... | collective-permute-start | bytes 245768 | tf_op jit(solution)/shard_map/ppermute | solution.py:645
  107.2 4.7 %collective-permute-start.9 = (bf16[160,256]{1,0:T(8,128)(2,1)S(1)}, bf16[160,256]{1,0:T(8,128)(2,1)S(1)}, u32[]{:S(2)}, u32[]{:S(2)}) collective-permute-start(bf16[160,256]{1,0:T(8,128)(2,1)S(1)} %get-tuple-element.86), channel_id=1, source_target_pairs={{0,16},{8,24},{16,0},{24,8},{1,17},{9,25},{17,1},{25,9},{2,18},{10... | collective-permute-start | bytes 245768 | tf_op jit(solution)/shard_map/ppermute | solution.py:645
  112.0 5.1 %collective-permute-start.11 = (bf16[136,256]{1,0:T(8,128)(2,1)S(1)}, bf16[136,256]{1,0:T(8,128)(2,1)S(1)}, u32[]{:S(2)}, u32[]{:S(2)}) collective-permute-start(bf16[136,256]{1,0:T(8,128)(2,1)S(1)} %get-tuple-element.87), channel_id=1, source_target_pairs={{0,2},{1,3},{2,0},{3,1},{4,6},{5,7},{6,4},{7,5},{8,10},{9,11},{10,... | collective-permute-start | bytes 208904 | tf_op jit(solution)/shard_map/ppermute | solution.py:645
  113.9 10.6 %collective-permute-start.12 = (bf16[136,256]{1,0:T(8,128)(2,1)S(1)}, bf16[136,256]{1,0:T(8,128)(2,1)S(1)}, u32[]{:S(2)}, u32[]{:S(2)}) collective-permute-start(bf16[136,256]{1,0:T(8,128)(2,1)S(1)} %get-tuple-element.88), channel_id=1, source_target_pairs={{0,4},{1,5},{2,6},{3,7},{4,0},{5,1},{6,2},{7,3},{8,12},{9,13},{10,... | collective-permute-start | bytes 208904 | tf_op jit(solution)/shard_map/ppermute | solution.py:645
  116.3 8.2 %collective-permute-start.13 = (bf16[136,256]{1,0:T(8,128)(2,1)S(1)}, bf16[136,256]{1,0:T(8,128)(2,1)S(1)}, u32[]{:S(2)}, u32[]{:S(2)}) collective-permute-start(bf16[136,256]{1,0:T(8,128)(2,1)S(1)} %get-tuple-element.89), channel_id=1, source_target_pairs={{0,6},{1,7},{2,4},{3,5},{4,2},{5,3},{6,0},{7,1},{8,14},{9,15},{10,... | collective-permute-start | bytes 208904 | tf_op jit(solution)/shard_map/ppermute | solution.py:645
  124.6 4.5 %collective-permute-start.14 = (bf16[136,256]{1,0:T(8,128)(2,1)S(1)}, bf16[136,256]{1,0:T(8,128)(2,1)S(1)}, u32[]{:S(2)}, u32[]{:S(2)}) collective-permute-start(bf16[136,256]{1,0:T(8,128)(2,1)S(1)} %fusion.6), channel_id=1, source_target_pairs={{0,2},{1,3},{2,0},{3,1},{4,6},{5,7},{6,4},{7,5},{8,10},{9,11},{10,... | collective-permute-start | bytes 208904 | tf_op jit(solution)/shard_map/ppermute | solution.py:645
  126.2 7.9 %collective-permute-start.15 = (bf16[136,256]{1,0:T(8,128)(2,1)S(1)}, bf16[136,256]{1,0:T(8,128)(2,1)S(1)}, u32[]{:S(2)}, u32[]{:S(2)}) collective-permute-start(bf16[136,256]{1,0:T(8,128)(2,1)S(1)} %fusion.6), channel_id=1, source_target_pairs={{0,4},{1,5},{2,6},{3,7},{4,0},{5,1},{6,2},{7,3},{8,12},{9,13},{10,... | collective-permute-start | bytes 208904 | tf_op jit(solution)/shard_map/ppermute | solution.py:645
  126.2 7.9 %collective-permute-start.16 = (bf16[136,256]{1,0:T(8,128)(2,1)S(1)}, bf16[136,256]{1,0:T(8,128)(2,1)S(1)}, u32[]{:S(2)}, u32[]{:S(2)}) collective-permute-start(bf16[136,256]{1,0:T(8,128)(2,1)S(1)} %fusion.6), channel_id=1, source_target_pairs={{0,6},{1,7},{2,4},{3,5},{4,2},{5,3},{6,0},{7,1},{8,14},{9,15},{10,... | collective-permute-start | bytes 208904 | tf_op jit(solution)/shard_map/ppermute | solution.py:645
  134.2 9.0 %collective-permute-start.17 = (bf16[4,136,256]{2,1,0:T(8,128)(2,1)S(1)}, bf16[4,136,256]{2,1,0:T(8,128)(2,1)S(1)}, u32[]{:S(2)}, u32[]{:S(2)}) collective-permute-start(bf16[4,136,256]{2,1,0:T(8,128)(2,1)S(1)} %pad_maximum_fusion.1), channel_id=1, source_target_pairs={{0,8},{8,0},{16,24},{24,16},{1,9},{9,1},{17,25},{25,17},{2,10},{10... | collective-permute-start | bytes 835592 | tf_op jit(solution)/shard_map/ppermute | solution.py:645
  135.4 11.8 %collective-permute-start.18 = (bf16[4,136,256]{2,1,0:T(8,128)(2,1)S(1)}, bf16[4,136,256]{2,1,0:T(8,128)(2,1)S(1)}, u32[]{:S(2)}, u32[]{:S(2)}) collective-permute-start(bf16[4,136,256]{2,1,0:T(8,128)(2,1)S(1)} %pad_maximum_fusion.1), channel_id=1, source_target_pairs={{0,16},{8,24},{16,0},{24,8},{1,17},{9,25},{17,1},{25,9},{2,18},{10... | collective-permute-start | bytes 835592 | tf_op jit(solution)/shard_map/ppermute | solution.py:645
  136.2 10.9 %collective-permute-start.19 = (bf16[4,136,256]{2,1,0:T(8,128)(2,1)S(1)}, bf16[4,136,256]{2,1,0:T(8,128)(2,1)S(1)}, u32[]{:S(2)}, u32[]{:S(2)}) collective-permute-start(bf16[4,136,256]{2,1,0:T(8,128)(2,1)S(1)} %pad_maximum_fusion.1), channel_id=1, source_target_pairs={{0,24},{8,16},{16,8},{24,0},{1,25},{9,17},{17,9},{25,1},{2,26},{10... | collective-permute-start | bytes 835592 | tf_op jit(solution)/shard_map/ppermute | solution.py:645
  147.3 2.8 %collective-permute-start.20 = (bf16[4,4,136,256]{3,2,1,0:T(8,128)(2,1)S(1)}, bf16[4,4,136,256]{3,2,1,0:T(8,128)(2,1)S(1)}, u32[]{:S(2)}, u32[]{:S(2)}) collective-permute-start(bf16[4,4,136,256]{3,2,1,0:T(8,128)(2,1)S(1)} %pad_maximum_fusion.own_ref), channel_id=1, source_target_pairs={{0,1},{1,0},{2,3},{3,2},{4,5},{5,4},{6,7},{7,6},{8,9},{9,8},{10,11... | collective-permute-start | bytes 3342344 | tf_op jit(solution)/shard_map/ppermute | solution.py:645
